TPU v7x, 128 devices: a whole 4x4x4 slice. The times are simulated.
128 devices in a mesh: blk: 32 (over x, z, core), sim: 4 (over y).
Axes of the slice: x: 4, y: 4, z: 4, core: 2. Of those that a mesh axis runs over, the one named last changes fastest.
Arguments:
- sky_maps: float32 [2, 32, 64, 4096], P(None, 'sim', 'blk'), may hold values from -30 to 30
- noise_weight: float32 [64, 4096], P('blk'), may hold values from 0.5 to 2
- signal_inverse: float32 [2048], replicated, may hold values from 0.1 to 3
- legendre: bfloat16 [1088, 16, 64, 128], P('blk'), may hold values from -4 to 4, as said below
- m_groups: int32 [32, 4], replicated, may hold values from 0 to 127, as said below
- block_list: int32 [1088, 2], P('blk'), may hold values from 0 to 15, as said below
- band_of_ell: int32 [2048], replicated, may hold values from 0 to 31, never falling along the last dimension, each value on 1 to 128 neighbouring positions
Outputs:
- filtered: bfloat16 [1088, 16, 2, 32, 2, 128], P('blk', None, None, 'sim')
- band_proj: float32 [32, 32], P('sim')
- fisher: float32 [32, 32], replicated
Inputs may be any that keep to these rules, and one draw needn't show every extreme that they name: `m_groups`: each index of blk owns 4 distinct groups of 16 orders, in pairs k and 127 - k; every group of 0 to 127 is owned once. `block_list`: rows d * 34 to (d + 1) * 34 - 1 list, in some order and each once, the pairs (slot s, degree block e) of index d of blk with e at least 16 * m_groups[d, s] // 128. `legendre`: entries with degree below order are zero.
All inputs are finite; a program needn't handle non-finite values.
Results may differ from a plain program's by a relative error of at most 0.014.
Values may be sent and summed in bfloat16 or wider, within the bound.
No kernel may reach another device: no remote copies, remote signals or barrier semaphores. Data moves between devices by JAX's collectives and lax.ppermute only.
A program may use at most 192 MiB of HBM per device.

v0:
```python
import math

import jax
import jax.numpy as jnp
from jax import lax
from jax.sharding import PartitionSpec as P

BANDS = 32
ITERS = 4


PRECISE = lax.Precision.HIGHEST


def angle_tables(cycle_pixels, degree_total):
    outer_count = cycle_pixels // 128
    upper_count = degree_total // outer_count
    outer_index = jnp.arange(outer_count, dtype=jnp.int32)
    inner_index = jnp.arange(128, dtype=jnp.int32)
    upper_index = jnp.arange(upper_count, dtype=jnp.int32)
    two_pi = 2.0 * math.pi
    outer_angle = (
        two_pi
        * (outer_index[:, None] * outer_index[None, :] % outer_count).astype(jnp.float32)
        / outer_count
    )
    twist_angle = (
        two_pi
        * (outer_index[:, None] * inner_index[None, :] % cycle_pixels).astype(jnp.float32)
        / cycle_pixels
    )
    inner_angle = (
        two_pi * (upper_index[:, None] * inner_index[None, :] % 128).astype(jnp.float32) / 128
    )
    orders = outer_index[None, :] + outer_count * upper_index[:, None]
    cycle_scale = jnp.where(
        orders == 0, math.sqrt(1.0 / cycle_pixels), math.sqrt(2.0 / cycle_pixels)
    ).astype(jnp.float32)
    return (
        jnp.cos(outer_angle),
        jnp.sin(outer_angle),
        jnp.cos(twist_angle),
        jnp.sin(twist_angle),
        jnp.cos(inner_angle),
        jnp.sin(inner_angle),
        cycle_scale,
    )


def forward_rows(field_rows, tables):
    cos_outer, sin_outer, cos_twist, sin_twist, cos_inner, sin_inner, cycle_scale = tables
    row_count = field_rows.shape[0]
    outer_count = cos_outer.shape[0]
    shaped = field_rows.reshape(row_count, outer_count, 128)
    first_cos = jnp.einsum("rab,ka->rkb", shaped, cos_outer, precision=PRECISE)
    first_sin = jnp.einsum("rab,ka->rkb", shaped, sin_outer, precision=PRECISE)
    twist_real = first_cos * cos_twist - first_sin * sin_twist
    twist_imag = -(first_cos * sin_twist + first_sin * cos_twist)
    part_real = jnp.einsum("rkb,ub->ruk", twist_real, cos_inner, precision=PRECISE) + jnp.einsum(
        "rkb,ub->ruk", twist_imag, sin_inner, precision=PRECISE
    )
    part_imag = jnp.einsum("rkb,ub->ruk", twist_imag, cos_inner, precision=PRECISE) - jnp.einsum(
        "rkb,ub->ruk", twist_real, sin_inner, precision=PRECISE
    )
    return jnp.stack([part_real * cycle_scale, part_imag * cycle_scale], axis=1)


def inverse_rows(coeffs, tables):
    cos_outer, sin_outer, cos_twist, sin_twist, cos_inner, sin_inner, cycle_scale = tables
    row_count = coeffs.shape[0]
    real_part = coeffs[:, 0] * cycle_scale
    imag_part = coeffs[:, 1] * cycle_scale
    half_real = jnp.einsum("ruk,ub->rkb", real_part, cos_inner, precision=PRECISE) - jnp.einsum(
        "ruk,ub->rkb", imag_part, sin_inner, precision=PRECISE
    )
    half_imag = jnp.einsum("ruk,ub->rkb", real_part, sin_inner, precision=PRECISE) + jnp.einsum(
        "ruk,ub->rkb", imag_part, cos_inner, precision=PRECISE
    )
    turned_real = half_real * cos_twist - half_imag * sin_twist
    turned_imag = half_real * sin_twist + half_imag * cos_twist
    pixels = jnp.einsum("rkb,ka->rab", turned_real, cos_outer, precision=PRECISE) - jnp.einsum(
        "rkb,ka->rab", turned_imag, sin_outer, precision=PRECISE
    )
    return pixels.reshape(row_count, -1)


def shards(sky_maps, noise_weight, signal_inverse, legendre, m_groups, block_list, band_of_ell):
    blk_count = lax.axis_size("blk")
    blk_index = lax.axis_index("blk")
    set_count, sim_local, cycle_local, cycle_pixels = sky_maps.shape
    block_count, group_size, cycle_total, degree_block = legendre.shape
    group_slots = m_groups.shape[1]
    degree_total = signal_inverse.shape[0]
    group_total = degree_total // group_size
    tables = angle_tables(cycle_pixels, degree_total)
    outer_count = cycle_pixels // 128
    upper_count = degree_total // outer_count
    column_count = group_slots * 2 * group_size
    slot_ids = block_list[:, 0]
    degree_ids = block_list[:, 1]
    own_groups = lax.dynamic_index_in_dim(m_groups, blk_index, 0, keepdims=False)
    block_group = jnp.take(own_groups, slot_ids)
    degrees = (
        degree_block * degree_ids[:, None] + jnp.arange(degree_block, dtype=jnp.int32)[None, :]
    )
    signal_blk = jnp.take(signal_inverse, degrees)
    precond = 1.0 / (2.0 + signal_blk)
    signal_b = signal_blk[:, None, None, None, None, :]
    precond_b = precond[:, None, None, None, None, :]
    slot_onehot = (slot_ids[:, None] == jnp.arange(group_slots, dtype=jnp.int32)[None, :]).astype(
        jnp.float32
    )
    slot_table = slot_onehot.astype(jnp.bfloat16)
    owner_table = (
        m_groups[None, :, :] == jnp.arange(group_total, dtype=jnp.int32)[:, None, None]
    ).astype(jnp.bfloat16)

    def project(received):
        set_number = received.shape[0]
        shaped = received.reshape(set_number, sim_local, cycle_total, group_slots, 2, group_size)
        chosen = jnp.einsum(
            "bg,sdrgpi->bsdrpi", slot_table, shaped, preferred_element_type=jnp.bfloat16
        )
        return jnp.einsum(
            "bsdrpi,birl->bisdpl", chosen, legendre, preferred_element_type=jnp.float32
        )

    def analysis(residual):
        coeffs = forward_rows(residual.reshape(-1, cycle_pixels), tables).astype(jnp.bfloat16)
        grouped = coeffs.reshape(-1, 2, group_total, group_size)
        outgoing = jnp.einsum(
            "rpgi,gdo->rdopi", grouped, owner_table, preferred_element_type=jnp.bfloat16
        )
        outgoing = outgoing.reshape(set_count, sim_local, cycle_local, blk_count, column_count)
        received = lax.all_to_all(outgoing, "blk", split_axis=3, concat_axis=2, tiled=True)
        return project(received)

    harmonic_state = precond_b * analysis(noise_weight[None, None] * sky_maps)
    for sweep_index in range(ITERS - 1):
        slot_set_number = harmonic_state.shape[2]
        rounded = harmonic_state.astype(jnp.bfloat16)
        block_terms = jnp.einsum(
            "bisdpl,birl->bsdrpi", rounded, legendre, preferred_element_type=jnp.float32
        )
        per_slot = jnp.einsum("bg,bsdrpi->sdrgpi", slot_onehot, block_terms, precision=PRECISE)
        synthesis_received = lax.all_to_all(
            per_slot.astype(jnp.bfloat16).reshape(
                slot_set_number, sim_local, blk_count, cycle_local, column_count
            ),
            "blk",
            split_axis=2,
            concat_axis=2,
            tiled=True,
        )
        to_set_number = synthesis_received.shape[0]
        to_shaped = synthesis_received.reshape(
            to_set_number, sim_local, blk_count, cycle_local, group_slots, 2, group_size
        )
        ordered = jnp.einsum(
            "sdxrgpi,hxg->sdrphi", to_shaped, owner_table, preferred_element_type=jnp.bfloat16
        )
        to_coeffs = ordered.astype(jnp.float32).reshape(
            to_set_number * sim_local * cycle_local, 2, upper_count, outer_count
        )
        residual = noise_weight[None, None] * (
            sky_maps
            - inverse_rows(to_coeffs, tables).reshape(
                to_set_number, sim_local, cycle_local, cycle_pixels
            )
        )
        harmonic = analysis(residual)
        harmonic_state = harmonic_state + precond_b * (harmonic - signal_b * harmonic_state)
    products = (
        harmonic_state[:, :, 0, :, 0, :] * harmonic_state[:, :, 1, :, 0, :]
        + harmonic_state[:, :, 0, :, 1, :] * harmonic_state[:, :, 1, :, 1, :]
    )
    orders = group_size * block_group[:, None] + jnp.arange(group_size, dtype=jnp.int32)[None, :]
    mode_weight = jnp.where(orders == 0, 1.0, 2.0).astype(jnp.float32)
    band_ids = jnp.take(band_of_ell, degrees)
    band_onehot = (band_ids[..., None] == jnp.arange(BANDS, dtype=jnp.int32)).astype(jnp.float32)
    partial_value = jnp.einsum(
        "bisl,bi,blk->sk", products, mode_weight, band_onehot, precision=PRECISE
    )
    all_onehot = (band_of_ell[:, None] == jnp.arange(BANDS, dtype=jnp.int32)[None, :]).astype(
        jnp.float32
    )
    ell_weight = (2 * jnp.arange(degree_total, dtype=jnp.int32) + 1).astype(jnp.float32)
    mode_count = jnp.dot(ell_weight, all_onehot, precision=PRECISE)
    norm_scale = 1.0 / jnp.sqrt(mode_count)
    band_proj = lax.psum(partial_value, "blk") * norm_scale[None, :]
    all_proj = lax.all_gather(band_proj, "sim", axis=0, tiled=True)
    sim_mean = jnp.mean(all_proj, axis=0)
    center = all_proj - sim_mean[None, :]
    fisher = jnp.dot(center.T, center, precision=PRECISE) / all_proj.shape[0]
    return (harmonic_state.astype(jnp.bfloat16), band_proj, fisher)


def solution(mesh):
    return jax.shard_map(
        shards,
        mesh=mesh,
        in_specs=(
            P(None, "sim", "blk", None),
            P("blk", None),
            P(),
            P("blk", None, None, None),
            P(),
            P("blk", None),
            P(),
        ),
        out_specs=(P("blk", None, None, "sim", None, None), P("sim", None), P()),
        check_vma=False,
    )
```

profile of v0, /device:TPU:0, one launch (start us, length us, event | category | flops | bytes accessed | tf_op | source)
XLA Modules:
  0.0 506.9 jit_solution(14966533592947972003)
XLA Ops:
  10.6 1.8 copy.82
  13.7 8.2 %all-to-all-start = ((bf16[2,8,2,32,128]{4,1,2,0,3:T(8,128)(2,1)}), bf16[2,8,2,32,128]{4,1,2,0,3:T(8,128)(2,1)S(1)}, u32[]{:S(2)}, u32[]{:S(2)}) async-start(bf16[2,8,2,32,128]{4,1,2,0,3:T(8,128)(2,1)} %copy.83), calls=%async_computation | async-start | bytes 524288 | tf_op jit(solution)/shard_map/all_to_all | solution.py:135
  22.6 2.6 fusion.358
  25.2 22.8 %gather_fusion = f32[4352]{0:T(1024)S(1)} fusion(f32[2048]{0:T(1024)S(1)} %copy-done, s32[5120]{0:T(1024)S(1)} %pad_clamp_fusion), kind=kCustom, calls=%fused_computation | custom fusion | bytes 52224 | tf_op jit(solution)/shard_map/jit(_take)/gather | solution.py:106
  49.5 2.6 copy.85
  53.7 12.6 %fusion.18 = f32[34,16,2,8,2,128]{5,3,4,2,1,0:T(8,128)} fusion(bf16[34,16,64,128]{3,2,1,0:T(8,128)(2,1)} %param.10, bf16[34,2,8,64,2,16]{3,0,5,4,2,1:T(8,128)(2,1)S(1)} %fusion.351), kind=kOutput, calls=%fused_computation.20 | convolution fusion | flops 285212672 | bytes 20054016 | tf_op jit(solution)/shard_map/bsdrpi,birl->bisdpl/dot_general | solution.py:124
  66.3 14.2 %fusion.27 = f32[34,2,8,64,2,16]{3,2,4,1,5,0:T(8,128)} fusion(bf16[34,16,64,128]{3,2,1,0:T(8,128)(2,1)} %param.10, f32[34,16,2,8,2,128]{5,3,4,2,1,0:T(8,128)} %fusion.18, f32[34,128]{1,0:T(8,128)S(1)} %get-tuple-element.12), kind=kOutput, calls=%fused_computation.33 | convolution fusion | flops 289669120 | bytes 22299648 | tf_op jit(solution)/shard_map/bisdpl,birl->bsdrpi/dot_general | solution.py:142
  80.5 15.3 %fusion.63 = bf16[2,8,64,4,2,16]{2,3,5,4,1,0:T(4,128)(2,1)S(1)} fusion(f32[34,2,8,64,2,16]{3,2,4,1,5,0:T(8,128)} %fusion.27, s32[34]{0:T(128)S(1)} %get-tuple-element.19), kind=kOutput, calls=%fused_computation.51 | convolution fusion | flops 53608584 | bytes 4718728 | tf_op jit(solution)/shard_map/bg,bsdrpi->sdrgpi/dot_general | solution.py:145
  95.8 2.1 copy.88
  100.1 7.4 %all-to-all-start.1 = ((bf16[2,8,32,2,128]{4,1,3,0,2:T(8,128)(2,1)}), bf16[2,8,32,2,128]{4,1,3,0,2:T(8,128)(2,1)S(1)}, u32[]{:S(2)}, u32[]{:S(2)}) async-start(bf16[2,8,32,2,128]{4,1,3,0,2:T(8,128)(2,1)} %copy.89), calls=%async_computation.1 | async-start | bytes 524288 | tf_op jit(solution)/shard_map/all_to_all | solution.py:146
  107.6 8.9 %all-to-all-done.1 = bf16[2,8,32,2,128]{4,1,3,0,2:T(8,128)(2,1)S(1)} async-done(((bf16[2,8,32,2,128]{4,1,3,0,2:T(8,128)(2,1)}), bf16[2,8,32,2,128]{4,1,3,0,2:T(8,128)(2,1)S(1)}, u32[]{:S(2)}, u32[]{:S(2)}) %all-to-all-start.1) | async-done | bytes 262176 | tf_op jit(solution)/shard_map/all_to_all | solution.py:146
  117.4 2.7 copy.92
  120.1 3.5 reshape.320
  129.0 1.8 convolution_add_fusion.2
  141.0 1.8 copy.105
  143.4 12.5 %all_to_all.75 = bf16[2,8,2,32,128]{4,1,2,0,3:T(8,128)(2,1)S(1)} all-to-all(bf16[2,8,2,32,128]{4,1,2,0,3:T(8,128)(2,1)S(1)} %copy.106), channel_id=1, replica_groups=mesh['blk'=32,'sim'=4] {'blk'}, dimensions={3} | all-to-all | bytes 524288 | tf_op jit(solution)/shard_map/all_to_all | solution.py:135
  157.3 2.4 copy.108
  161.3 12.6 %fusion.14 = f32[34,16,2,8,2,128]{5,3,4,2,1,0:T(8,128)} fusion(bf16[34,16,64,128]{3,2,1,0:T(8,128)(2,1)} %param.10, bf16[34,2,8,64,2,16]{3,0,5,4,2,1:T(8,128)(2,1)S(1)} %fusion.349), kind=kOutput, calls=%fused_computation.16 | convolution fusion | flops 285212672 | bytes 20054016 | tf_op jit(solution)/shard_map/bsdrpi,birl->bisdpl/dot_general | solution.py:124
  173.9 14.2 %fusion.30 = f32[34,2,8,64,2,16]{3,2,4,1,5,0:T(8,128)} fusion(bf16[34,16,64,128]{3,2,1,0:T(8,128)(2,1)} %param.10, f32[34,16,2,8,2,128]{5,3,4,2,1,0:T(8,128)} %fusion.14, f32[34,16,2,8,2,128]{5,3,4,2,1,0:T(8,128)} %fusion.18, f32[34,128]{1,0:T(8,128)S(1)} %get-tuple-element.13, f32[34,128]{1,0:T(8,128)S(1)} %get-tuple-element.12), kind=kOutput, calls=%fused_computation.34 | convolution fusion | flops 298582016 | bytes 31229952 | tf_op jit(solution)/shard_map/bisdpl,birl->bsdrpi/dot_general | solution.py:142
  188.1 14.8 %fusion.60 = bf16[2,8,64,4,2,16]{2,3,5,4,1,0:T(4,128)(2,1)S(1)} fusion(f32[34,2,8,64,2,16]{3,2,4,1,5,0:T(8,128)} %fusion.30, s32[34]{0:T(128)S(1)} %get-tuple-element.19), kind=kOutput, calls=%fused_computation.50 | convolution fusion | flops 53608584 | bytes 4718728 | tf_op jit(solution)/shard_map/bg,bsdrpi->sdrgpi/dot_general | solution.py:145
  203.0 2.1 copy.111
  206.5 12.5 %all_to_all.76 = bf16[2,8,32,2,128]{4,1,3,0,2:T(8,128)(2,1)S(1)} all-to-all(bf16[2,8,32,2,128]{4,1,3,0,2:T(8,128)(2,1)S(1)} %copy.112), channel_id=1, replica_groups=mesh['blk'=32,'sim'=4] {'blk'}, dimensions={2} | all-to-all | bytes 524288 | tf_op jit(solution)/shard_map/all_to_all | solution.py:146
  220.0 2.7 copy.192
  222.6 3.7 reshape.410
  231.8 1.8 convolution_add_fusion.1
  243.5 1.8 copy.128
  245.9 12.5 %all_to_all.77 = bf16[2,8,2,32,128]{4,1,2,0,3:T(8,128)(2,1)S(1)} all-to-all(bf16[2,8,2,32,128]{4,1,2,0,3:T(8,128)(2,1)S(1)} %copy.129), channel_id=1, replica_groups=mesh['blk'=32,'sim'=4] {'blk'}, dimensions={3} | all-to-all | bytes 524288 | tf_op jit(solution)/shard_map/all_to_all | solution.py:135
  259.8 2.4 copy.131
  263.7 12.6 %fusion.10 = f32[34,16,2,8,2,128]{5,3,4,2,1,0:T(8,128)} fusion(bf16[34,16,64,128]{3,2,1,0:T(8,128)(2,1)} %param.10, bf16[34,2,8,64,2,16]{3,0,5,4,2,1:T(8,128)(2,1)S(1)} %fusion.347), kind=kOutput, calls=%fused_computation.12 | convolution fusion | flops 285212672 | bytes 20054016 | tf_op jit(solution)/shard_map/bsdrpi,birl->bisdpl/dot_general | solution.py:124
  276.4 17.7 %fusion.35 = f32[34,2,8,64,2,16]{3,2,4,1,5,0:T(8,128)} fusion(bf16[34,16,64,128]{3,2,1,0:T(8,128)(2,1)} %param.10, f32[34,16,2,8,2,128]{5,3,4,2,1,0:T(8,128)} %fusion.10, f32[34,128]{1,0:T(8,128)S(1)} %get-tuple-element.13, f32[34,128]{1,0:T(8,128)S(1)} %get-tuple-element.12, f32[34,16,2,8,2,128]{5,3,4,2,1,0:T(8,128)} %fusion.14, ...), kind=kOutput, calls=%fused_computation.35 | convolution fusion | flops 307494912 | bytes 40142848 | tf_op jit(solution)/shard_map/bisdpl,birl->bsdrpi/dot_general | solution.py:142
  294.0 14.8 %fusion.57 = bf16[2,8,64,4,2,16]{2,3,5,4,1,0:T(4,128)(2,1)S(1)} fusion(f32[34,2,8,64,2,16]{3,2,4,1,5,0:T(8,128)} %fusion.35, s32[34]{0:T(128)S(1)} %get-tuple-element.19), kind=kOutput, calls=%fused_computation.49 | convolution fusion | flops 53608584 | bytes 4718728 | tf_op jit(solution)/shard_map/bg,bsdrpi->sdrgpi/dot_general | solution.py:145
  308.9 2.1 copy.134
  313.1 3.9 all-to-all-start.5
  317.1 8.9 %all-to-all-done.5 = bf16[2,8,32,2,128]{4,1,3,0,2:T(8,128)(2,1)S(1)} async-done(((bf16[2,8,32,2,128]{4,1,3,0,2:T(8,128)(2,1)}), bf16[2,8,32,2,128]{4,1,3,0,2:T(8,128)(2,1)S(1)}, u32[]{:S(2)}, u32[]{:S(2)}) %all-to-all-start.5) | async-done | bytes 262176 | tf_op jit(solution)/shard_map/all_to_all | solution.py:146
  326.9 2.7 copy.194
  329.6 3.4 reshape.411
  336.7 1.8 convolution_subtract_fusion
  338.5 1.8 convolution_add_fusion
  350.3 1.8 copy.151
  353.4 3.9 all-to-all-start.6
  357.9 22.8 %gather_fusion.1 = s32[4352]{0:T(1024)S(1)} fusion(s32[2048]{0:T(1024)S(1)} %copy-done.2, s32[5120]{0:T(1024)S(1)} %pad_clamp_fusion), kind=kCustom, calls=%fused_computation.1 | custom fusion | bytes 52224 | tf_op jit(solution)/shard_map/jit(_take)/gather | solution.py:179
  382.1 2.4 copy.154
  384.5 3.9 fusion.345
  388.5 20.9 %fusion.535 = (bf16[34,16,2,8,2,128]{5,3,4,2,1,0:T(8,128)(2,1)}, f32[34,16,2,8,2,128]{5,3,4,2,1,0:T(8,128)}) fusion(bf16[34,16,64,128]{3,2,1,0:T(8,128)(2,1)} %param.10, bf16[34,2,8,64,2,16]{3,0,5,4,2,1:T(8,128)(2,1)} %fusion.345, f32[34,16,2,8,2,128]{5,3,4,2,1,0:T(8,128)} %fusion.10, f32[34,16,2,8,2,128]{5,3,4,2,1,0:T(8,128)} %fusion.14, ...), kind=kOutput, calls=%fused_computation.533 | convolution fusion | flops 316407808 | bytes 51283968 | tf_op jit(solution)/shard_map/bsdrpi,birl->bisdpl/dot_general | solution.py:124
  409.4 4.5 fusion.45
  415.8 67.6 %psum.7 = f32[8,32]{1,0:T(8,128)S(1)} all-reduce(f32[8,32]{1,0:T(8,128)S(1)} %convolution_bitcast_fusion.7), channel_id=1, replica_groups=mesh['blk'=32,'sim'=4] {'blk'}, use_global_device_ids=true, to_apply=%region_0.1 | all-reduce | flops 256 | bytes 2048 | tf_op jit(solution)/shard_map/psum | solution.py:190
  483.4 12.7 %all_gather.3 = f32[32,32]{1,0:T(8,128)S(1)} all-gather(f32[8,32]{1,0:T(8,128)S(1)} %broadcast_multiply_fusion.1), channel_id=1, replica_groups=mesh['blk'=32,'sim'=4] {'sim'}, dimensions={0}, use_global_device_ids=true | all-gather | bytes 5120 | tf_op jit(solution)/shard_map/all_gather | solution.py:191
  497.0 9.5 %copy.156 = bf16[34,16,2,8,2,128]{5,4,3,2,1,0:T(2,128)(2,1)} copy(bf16[34,16,2,8,2,128]{5,3,4,2,1,0:T(8,128)(2,1)} %get-tuple-element.21) | data formatting | bytes 8912896
  (137 shorter events, 80.8 us)
Async XLA Ops:
  0.6 24.6 %copy-start = (f32[2048]{0:T(1024)S(1)}, f32[2048]{0:T(1024)}, u32[]{:S(2)}) copy-start(f32[2048]{0:T(1024)} %param.9) | copy-start | bytes 24580
  0.6 9.3 %copy-start.5 = (s32[32,4]{0,1:T(4,128)S(1)}, s32[32,4]{0,1:T(4,128)}, u32[]{:S(2)}) copy-start(s32[32,4]{0,1:T(4,128)} %param.11) | copy-start | bytes 1540
  2.6 20.0 %copy-start.7 = (s32[34,2]{0,1:T(2,128)S(1)}, s32[34,2]{0,1:T(2,128)}, u32[]{:S(2)}) copy-start(s32[34,2]{0,1:T(2,128)} %param.12) | copy-start | bytes 820
  13.7 34.5 %all-to-all-start = ((bf16[2,8,2,32,128]{4,1,2,0,3:T(8,128)(2,1)}), bf16[2,8,2,32,128]{4,1,2,0,3:T(8,128)(2,1)S(1)}, u32[]{:S(2)}, u32[]{:S(2)}) async-start(bf16[2,8,2,32,128]{4,1,2,0,3:T(8,128)(2,1)} %copy.83), calls=%async_computation | async-start | bytes 524288 | tf_op jit(solution)/shard_map/all_to_all | solution.py:135
  100.1 16.3 %all-to-all-start.1 = ((bf16[2,8,32,2,128]{4,1,3,0,2:T(8,128)(2,1)}), bf16[2,8,32,2,128]{4,1,3,0,2:T(8,128)(2,1)S(1)}, u32[]{:S(2)}, u32[]{:S(2)}) async-start(bf16[2,8,32,2,128]{4,1,3,0,2:T(8,128)(2,1)} %copy.89), calls=%async_computation.1 | async-start | bytes 524288 | tf_op jit(solution)/shard_map/all_to_all | solution.py:146
  120.1 12.5 %copy-start.4 = (f32[2,4096]{1,0:T(2,128)S(1)}, f32[2,4096]{1,0:T(2,128)}, u32[]{:S(2)}) copy-start(f32[2,4096]{1,0:T(2,128)} %param.8) | copy-start | bytes 98308
  120.1 12.6 %copy-start.3 = (f32[2,8,2,4096]{3,2,1,0:T(2,128)S(1)}, f32[2,8,2,4096]{3,2,1,0:T(2,128)}, u32[]{:S(2)}) copy-start(f32[2,8,2,4096]{3,2,1,0:T(2,128)} %param.7) | copy-start | bytes 1572868
  313.1 12.8 %all-to-all-start.5 = ((bf16[2,8,32,2,128]{4,1,3,0,2:T(8,128)(2,1)}), bf16[2,8,32,2,128]{4,1,3,0,2:T(8,128)(2,1)S(1)}, u32[]{:S(2)}, u32[]{:S(2)}) async-start(bf16[2,8,32,2,128]{4,1,3,0,2:T(8,128)(2,1)} %copy.135), calls=%async_computation.5 | async-start | bytes 524288 | tf_op jit(solution)/shard_map/all_to_all | solution.py:146
  342.2 15.1 %copy-start.2 = (s32[2048]{0:T(1024)S(1)}, s32[2048]{0:T(1024)}, u32[]{:S(2)}) copy-start(s32[2048]{0:T(1024)} %param.13) | copy-start | bytes 24580
  353.4 27.3 %all-to-all-start.6 = ((bf16[2,8,2,32,128]{4,1,2,0,3:T(8,128)(2,1)}), bf16[2,8,2,32,128]{4,1,2,0,3:T(8,128)(2,1)S(1)}, u32[]{:S(2)}, u32[]{:S(2)}) async-start(bf16[2,8,2,32,128]{4,1,2,0,3:T(8,128)(2,1)} %copy.152), calls=%async_computation.6 | async-start | bytes 524288 | tf_op jit(solution)/shard_map/all_to_all | solution.py:135
  409.4 97.1 %copy-start.1 = (f32[2048]{0:T(1024)S(1)}, f32[2048]{0:T(1024)}, u32[]{:S(2)}) copy-start(f32[2048]{0:T(1024)} %param.9) | copy-start | bytes 24580
  483.4 23.0 %copy-start.6 = (f32[8,32]{1,0:T(8,128)}, f32[8,32]{1,0:T(8,128)S(1)}, u32[]{:S(2)}) copy-start(f32[8,32]{1,0:T(8,128)S(1)} %broadcast_multiply_fusion.1) | copy-start | bytes 3076
where the time goes:
time: 516 us; the launch traced here: 507 us
  matrix products  209 us (41%)
  local copies, waits for them, and re-layouts  128 us (25%)
  blocking collectives  118 us (23%)
  starting transfers between devices  23.4 us (5%)
  waiting for transfers between devices  17.7 us (3%)
  other arithmetic  8.83 us (2%)
    psum x1, blocking collectives, shards(): band_proj = lax.psum(partial_value, 'blk') * norm_scale[None, :]  67.6 us
    dot_general x4, matrix products, project(): jnp.einsum('bsdrpi,birl->bisdpl', chosen, legendre, preferred_element_typ...  58.8 us
    dot_general x3, matrix products, shards(): jnp.einsum('bisdpl,birl->bsdrpi', rounded, legendre, preferred_element_ty...  46.2 us
    dot_general x3, matrix products, shards(): jnp.einsum('bg,bsdrpi->sdrgpi', slot_onehot, block_terms, precision=PRECISE)  45 us
    all_to_all x2, blocking collectives, analysis(): lax.all_to_all(outgoing, 'blk', split_axis=3, concat_axis=2, tiled=True)  24.9 us
    gather x1, local copies, waits for them, and re-layouts, shards(): band_ids = jnp.take(band_of_ell, degrees)  22.8 us
    gather x1, local copies, waits for them, and re-layouts, shards(): signal_blk = jnp.take(signal_inverse, degrees)  22.8 us
    reshape x6, local copies, waits for them, and re-layouts, shards(): ordered.astype(jnp.float32)  18.6 us
  transfers between devices with their start and end apart: 4, of which 2 were waited for; matrix products, arithmetic and copies ran while one was open for 10% of the time, Pallas kernels for 0%

commit v1 on v0

v1 whole, which is shorter than its diff:
```python
import math

import jax
import jax.numpy as jnp
import numpy as np
from jax import lax
from jax.experimental import pallas as pl
from jax.experimental.pallas import tpu as pltpu
from jax.sharding import PartitionSpec as P

NPHI = 4096
BANDS = 32
ITERS = 4
BLK = 32
CYC = 2
VEC = 16
OUTER = 32
INNER = 128
MG = 16
SLOTS = 4
NQ = 4
F32 = jnp.float32
BF16 = jnp.bfloat16
PRECISE = lax.Precision.HIGHEST
STEP_BLOCKS = 2
NT = (((1,), (1,)), ((), ()))
TN = (((0,), (0,)), ((), ()))
NN = (((1,), (0,)), ((), ()))


def split(value):
    high = value.astype(BF16)
    return high, (value - high.astype(F32)).astype(BF16)


def dot(left, right, dims=NN):
    return lax.dot_general(left, right, dims, preferred_element_type=F32)


def dot3(left, right, dims=NN):
    return (
        dot(left[0], right[0], dims) + dot(left[0], right[1], dims) + dot(left[1], right[0], dims)
    )


def np_split(value):
    high = value.astype(np.float32).astype(jnp.bfloat16)
    low = (value - high.astype(np.float64)).astype(np.float32).astype(jnp.bfloat16)
    return np.stack([high, low])


def constant_tables():
    k = np.arange(OUTER).reshape(2, 1, MG)
    k_rows = np.broadcast_to(k, (2, CYC, MG)).reshape(-1)
    cycle_rows = np.broadcast_to(np.arange(CYC).reshape(1, CYC, 1), (2, CYC, MG)).reshape(-1)
    a_cols = np.repeat(np.arange(OUTER), CYC)
    cycle_cols = np.tile(np.arange(CYC), OUTER)
    angle = 2.0 * np.pi * (k_rows[:, None] * a_cols[None, :] % OUTER) / OUTER
    same = cycle_rows[:, None] == cycle_cols[None, :]
    outer = np.concatenate([np.cos(angle) * same, -np.sin(angle) * same], axis=0)
    twist = 2.0 * np.pi * (k_rows[:, None] * np.arange(INNER)[None, :]) / NPHI
    twist_table = np.stack([np.cos(twist), np.sin(twist)]).astype(np.float32)
    q = np.arange(BLK * CYC)
    cycle_of = 2 * (q % BLK) + q // BLK
    place = np.zeros((NQ, BLK * CYC, NQ * BLK * CYC), np.float32)
    for i in range(NQ):
        place[i, q, i * BLK * CYC + cycle_of] = 1.0
    spread = np.zeros((BLK * CYC, 2 * BLK * CYC), np.float32)
    spread[q, cycle_of] = 1.0
    spread[q, BLK * CYC + cycle_of] = 1.0
    return (
        np_split(outer),
        np_split(outer.T),
        twist_table,
        place.astype(jnp.bfloat16),
        spread.astype(jnp.bfloat16),
    )


def column(half, j, p, h):
    return ((half * 2 + j) * 2 + p) * 2 + h


def forward_part(field_of, outer_ref, twist_ref, inner_ref, zero_ref, out_ref, turned, staged):
    outer = (outer_ref[0], outer_ref[1])
    cos_twist, sin_twist = twist_ref[0], twist_ref[1]
    for v in range(VEC):
        first = dot3(outer, split(field_of(v)))
        real, imag = first[:64], first[64:]
        turned_real = split(real * cos_twist + imag * sin_twist)
        turned_imag = split(imag * cos_twist - real * sin_twist)
        for half in range(2):
            for cycle in range(CYC):
                rows = slice((half * 2 + cycle) * MG, (half * 2 + cycle + 1) * MG)
                at = cycle * 256 + v * MG
                for part in range(2):
                    turned[part, half, at : at + MG, 0:128] = turned_real[part][rows]
                    turned[part, half, at : at + MG, 128:256] = turned_imag[part][rows]
    for half in range(2):
        inner = (inner_ref[0, half], inner_ref[1, half])
        coeffs = dot3(inner, (turned[0, half], turned[1, half]), NT)
        if half == 0:
            coeffs = coeffs * zero_scale(zero_ref)
        for j in range(2):
            for p in range(2):
                for h in range(2):
                    for cycle in range(CYC):
                        row = column(half, j, p, h) * 2 + cycle
                        lanes = cycle * 256 + h * 128
                        staged[:, row, :] = coeffs[
                            (j * 2 + p) * 32 : (j * 2 + p + 1) * 32, lanes : lanes + 128
                        ]
    out_ref[...] = staged[...].astype(BF16)


def zero_scale(zero_ref):
    lane = lax.broadcasted_iota(jnp.int32, (128, 512), 1)
    own = jnp.broadcast_to(zero_ref[...], (128, 512))
    return jnp.where(jnp.logical_and(lane % MG == 0, own > 0.0), math.sqrt(0.5), 1.0)


def first_rows_kernel(
    sky_ref, noise_ref, outer_ref, twist_ref, inner_ref, zero_ref, out_ref, turned, staged
):
    noise = noise_ref[...]
    forward_part(
        lambda v: noise * sky_ref[v],
        outer_ref, twist_ref, inner_ref, zero_ref, out_ref, turned, staged,
    )


def rows_kernel(
    sky_ref, noise_ref, outer_ref, outer_t_ref, twist_ref, inner_ref, zero_ref, coeff_ref,
    out_ref, turned, staged, spectrum,
):
    staged[...] = coeff_ref[...].astype(F32)
    for half in range(2):
        rows = []
        for j in range(2):
            for p in range(2):
                rows.append(
                    jnp.concatenate(
                        [
                            staged[:, column(half, j, p, h) * 2 + cycle, :]
                            for cycle in range(CYC)
                            for h in range(2)
                        ],
                        axis=1,
                    )
                )
        coeffs = jnp.concatenate(rows, axis=0)
        if half == 0:
            coeffs = coeffs * zero_scale(zero_ref)
        coeffs = coeffs.astype(BF16)
        inner = dot(coeffs, inner_ref[0, half], TN) + dot(coeffs, inner_ref[1, half], TN)
        shaped = inner.reshape(CYC * VEC, MG, 256)
        real, imag = shaped[:, :, :128], shaped[:, :, 128:]
        base = half * CYC * MG
        cos_twist = twist_ref[0, base : base + MG][None]
        sin_twist = twist_ref[1, base : base + MG][None]
        turned_real = split(real * cos_twist - imag * sin_twist)
        turned_imag = split(real * sin_twist + imag * cos_twist)
        for part in range(2):
            for cycle in range(CYC):
                at = (half * CYC + cycle) * MG
                spectrum[part, :, at : at + MG] = turned_real[part][cycle * VEC : (cycle + 1) * VEC]
                spectrum[part, :, 64 + at : 64 + at + MG] = turned_imag[part][
                    cycle * VEC : (cycle + 1) * VEC
                ]
    noise = noise_ref[...]
    outer_t = (outer_t_ref[0], outer_t_ref[1])

    def field_of(v):
        pixels = dot3(outer_t, (spectrum[0, v], spectrum[1, v]))
        return noise * (sky_ref[v] - pixels)

    forward_part(field_of, outer_ref, twist_ref, inner_ref, zero_ref, out_ref, turned, staged)


def modes_kernel(first, last, *refs):
    slot_ref, degree_ref, zero_ref = refs[:3]
    refs = refs[3:]
    coeff_ref, legendre_ref, signal_ref, place_ref, spread_ref = refs[:5]
    refs = refs[5:]
    if not first:
        state_ref, refs = refs[0], refs[1:]
    if last:
        band_ref, state_out, band_out, staged, ordered, packed, products = refs
    else:
        state_out, out_ref, staged, ordered, packed, sums = refs
    step = pl.program_id(0)

    @pl.when(step == 0)
    def _():
        staged[...] = coeff_ref[...].astype(F32)
        for c in range(16):
            slot, p, h = c // 4, (c // 2) % 2, c % 2
            pair = jnp.concatenate([staged[:, 2 * c, :], staged[:, 2 * c + 1, :]], axis=0)
            turned = pair.T
            for v in range(8):
                at = ((slot * VEC + h * 8 + v) * 2 + p) * MG
                ordered[at : at + MG, 0:64] = turned[v * MG : (v + 1) * MG]
        for i4 in range(NQ):
            rows = jnp.concatenate(
                [
                    ordered[pl.ds(slot * 512 + iq * 4 + i4, 32, stride=MG), 0:64]
                    for slot in range(SLOTS)
                    for iq in range(NQ)
                ],
                axis=0,
            )
            spreaded = dot(rows.astype(BF16), place_ref[i4]).astype(BF16)
            packed[:, i4 * 32 : (i4 + 1) * 32, :] = spreaded.reshape(16, 32, 256)
        if last:
            products[...] = jnp.zeros_like(products)
        else:
            sums[...] = jnp.zeros_like(sums)

    blanks = jnp.zeros((32, 128), BF16)
    for k in range(STEP_BLOCKS):
        block = step * STEP_BLOCKS + k
        slot = slot_ref[block]
        degree = degree_ref[block]
        precond = 1.0 / (2.0 + signal_ref[pl.ds(degree, 1), :])
        total = jnp.zeros((32, 128), F32)
        for iq in range(NQ):
            table = [legendre_ref[k, iq * 4 + i4] for i4 in range(NQ)]
            harmonic = dot(packed[slot * NQ + iq], jnp.concatenate(table, axis=0))
            if first:
                state = precond * harmonic
            else:
                before = state_ref[k, iq * 128 : (iq + 1) * 128].astype(F32)
                state = precond * (2.0 * before + harmonic)
            rounded = state.astype(BF16)
            state_out[k, iq * 128 : (iq + 1) * 128] = rounded
            if last:
                for i4 in range(NQ):
                    row = i4 * 32
                    one = state[row : row + 16] * state[row + 16 : row + 32]
                    if iq == 0 and i4 == 0:
                        weight = jnp.where(zero_ref[block] > 0, 0.5, 1.0)
                        one = one * weight
                    total = total + jnp.concatenate([one, jnp.zeros_like(one)], axis=0)
            else:
                left = jnp.concatenate(
                    [
                        jnp.concatenate(
                            [rounded[i4 * 32 : (i4 + 1) * 32], blanks]
                            if i4 % 2 == 0
                            else [blanks, rounded[i4 * 32 : (i4 + 1) * 32]],
                            axis=1,
                        )
                        for i4 in range(NQ)
                    ],
                    axis=0,
                )
                right = jnp.concatenate(
                    [
                        jnp.concatenate([table[0], table[1]], axis=1),
                        jnp.concatenate([table[2], table[3]], axis=1),
                    ],
                    axis=0,
                )
                sums[slot * NQ + iq] += dot(left, right, NT)
        if last:
            products[degree] += 2.0 * total[:16]

    @pl.when(step == pl.num_programs(0) - 1)
    def _():
        if last:
            raw = jnp.zeros((VEC, BANDS), F32)
            counts = jnp.zeros((VEC, BANDS), F32)
            bins = lax.broadcasted_iota(jnp.int32, (BANDS, 128), 0)
            lane = lax.broadcasted_iota(jnp.int32, (VEC, 128), 1)
            for e in range(16):
                member = (jnp.broadcast_to(band_ref[e : e + 1, :], (BANDS, 128)) == bins).astype(F32)
                raw = raw + lax.dot_general(
                    products[e], member, NT, precision=PRECISE, preferred_element_type=F32
                )
                weight = (2 * (e * 128 + lane) + 1).astype(F32)
                counts = counts + lax.dot_general(
                    weight, member, NT, precision=PRECISE, preferred_element_type=F32
                )
            band_out[...] = raw * (1.0 / jnp.sqrt(counts))
        else:
            lane = lax.broadcasted_iota(jnp.int32, (128, 128), 1)
            order = lax.broadcasted_iota(jnp.int32, (128, 128), 0) % MG
            keep = (order % 4) // 2 == lane // 64
            for slot in range(SLOTS):
                for i in range(MG):
                    ordered[pl.ds(slot * 512 + i, 32, stride=MG), :] = sums[
                        slot * NQ + i // 4, (i % 4) * 32 : (i % 4 + 1) * 32, :
                    ]
            for c in range(16):
                slot, p, h = c // 4, (c // 2) % 2, c % 2
                rows = []
                for v in range(8):
                    at = ((slot * VEC + h * 8 + v) * 2 + p) * MG
                    rows.append(ordered[at : at + MG, :])
                whole = jnp.where(keep, jnp.concatenate(rows, axis=0), 0.0).astype(BF16)
                turned = dot(spread_ref[...], whole, NT)
                staged[:, 2 * c, :] = turned[:32]
                staged[:, 2 * c + 1, :] = turned[32:]
            out_ref[...] = staged[...].astype(BF16)


def params(megabytes, **more):
    return pltpu.CompilerParams(vmem_limit_bytes=megabytes << 20, **more)


def row_transforms(sky, noise, outer, outer_t, twist, inner, zero_rows, coeffs):
    result = jax.ShapeDtypeStruct((BLK, 32, 128), BF16)
    scratch = [
        pltpu.VMEM((2, 2, 512, 256), BF16),
        pltpu.VMEM((BLK, 32, 128), F32),
    ]
    if coeffs is None:
        return pl.pallas_call(
            first_rows_kernel,
            out_shape=result,
            scratch_shapes=scratch,
            compiler_params=params(32),
            name="first_rows",
        )(sky, noise, outer, twist, inner, zero_rows)
    return pl.pallas_call(
        rows_kernel,
        out_shape=result,
        scratch_shapes=scratch + [pltpu.VMEM((2, VEC, 128, 128), BF16)],
        compiler_params=params(32),
        name="rows",
    )(sky, noise, outer, outer_t, twist, inner, zero_rows, coeffs)


def mode_step(first, last, scalars, coeffs, legendre, signal, place, spread, state, bands):
    block_count = legendre.shape[0]
    assert block_count % STEP_BLOCKS == 0
    grid = (block_count // STEP_BLOCKS,)
    state_spec = pl.BlockSpec((STEP_BLOCKS, 512, 128), lambda g, *_: (g, 0, 0))

    def whole(shape):
        return pl.BlockSpec(shape, lambda g, *_: (0,) * len(shape))

    operands = [coeffs, legendre, signal, place, spread]
    specs = [
        whole((BLK, 32, 128)),
        pl.BlockSpec((STEP_BLOCKS, MG, 64, 128), lambda g, *_: (g, 0, 0, 0)),
        whole((16, 128)),
        whole((NQ, 64, 256)),
        whole((64, 128)),
    ]
    if not first:
        operands.append(state)
        specs.append(state_spec)
    out_shapes = [jax.ShapeDtypeStruct((block_count, 512, 128), BF16)]
    out_specs = [state_spec]
    scratch = [
        pltpu.VMEM((BLK, 32, 128), F32),
        pltpu.VMEM((SLOTS * 512, 128), F32),
        pltpu.VMEM((SLOTS * NQ, 128, 256), BF16),
    ]
    if last:
        operands.append(bands)
        specs.append(whole((16, 128)))
        out_shapes.append(jax.ShapeDtypeStruct((VEC, BANDS), F32))
        out_specs.append(whole((VEC, BANDS)))
        scratch.append(pltpu.VMEM((16, VEC, 128), F32))
    else:
        out_shapes.append(jax.ShapeDtypeStruct((BLK, 32, 128), BF16))
        out_specs.append(whole((BLK, 32, 128)))
        scratch.append(pltpu.VMEM((SLOTS * NQ, 128, 128), F32))

    def body(*refs):
        modes_kernel(first, last, *refs)

    return pl.pallas_call(
        body,
        out_shape=out_shapes,
        grid_spec=pltpu.PrefetchScalarGridSpec(
            num_scalar_prefetch=3,
            grid=grid,
            in_specs=specs,
            out_specs=out_specs,
            scratch_shapes=scratch,
        ),
        compiler_params=params(32, dimension_semantics=("arbitrary",)),
        name="modes_last" if last else "modes_first" if first else "modes",
    )(*scalars, *operands)


def exchange(rows):
    return lax.all_to_all(rows, "blk", 0, 0, tiled=True)


def shards(sky_maps, noise_weight, signal_inverse, legendre, m_groups, block_list, band_of_ell):
    blk_index = lax.axis_index("blk")
    set_count, sim_local, cycle_local, cycle_pixels = sky_maps.shape
    block_count = legendre.shape[0]
    outer, outer_t, twist, place, spread = [jnp.asarray(t) for t in constant_tables()]
    sky = sky_maps.reshape(set_count, sim_local, cycle_local, OUTER, INNER)
    sky = sky.transpose(0, 1, 3, 2, 4).reshape(VEC, OUTER * CYC, INNER)
    noise = noise_weight.reshape(CYC, OUTER, INNER).transpose(1, 0, 2).reshape(OUTER * CYC, INNER)
    half_of = m_groups % 2
    upper_of = m_groups // 2
    earlier = jnp.tril(jnp.ones((SLOTS, SLOTS), jnp.int32), -1)
    rank = jnp.sum(
        (half_of[:, :, None] == half_of[:, None, :]).astype(jnp.int32) * earlier[None], axis=2
    )
    new_slot = 2 * half_of + rank
    chosen = new_slot[:, :, None] == jnp.arange(SLOTS, dtype=jnp.int32)[None, None, :]
    upper = jnp.sum(jnp.where(chosen, upper_of[:, :, None], 0), axis=1)
    upper_rows = upper.T.reshape(2, 2, 1, BLK, 1)
    angle = (2.0 * math.pi / 128.0) * (
        upper_rows * jnp.arange(128, dtype=jnp.int32) % 128
    ).astype(F32)
    cos_inner = math.sqrt(2.0 / NPHI) * jnp.cos(angle)
    sin_inner = math.sqrt(2.0 / NPHI) * jnp.sin(angle)
    inner = jnp.concatenate(
        [
            jnp.concatenate([cos_inner, sin_inner], axis=-1),
            jnp.concatenate([-sin_inner, cos_inner], axis=-1),
        ],
        axis=2,
    ).reshape(2, 128, 256)
    inner = jnp.stack(split(inner))
    zero_rows = jnp.broadcast_to(
        (upper[:, :2].T == 0).astype(F32)[:, None, :], (2, 2, BLK)
    ).reshape(128, 1)
    slot_ids = block_list[:, 0]
    degree_ids = block_list[:, 1]
    slot_hot = slot_ids[:, None] == jnp.arange(SLOTS, dtype=jnp.int32)[None, :]
    own_slot = lax.dynamic_index_in_dim(new_slot, blk_index, 0, keepdims=False)
    own_groups = lax.dynamic_index_in_dim(m_groups, blk_index, 0, keepdims=False)
    block_slot = jnp.sum(jnp.where(slot_hot, own_slot[None, :], 0), axis=1)
    block_zero = jnp.sum(
        jnp.where(slot_hot, (own_groups == 0).astype(jnp.int32)[None, :], 0), axis=1
    )
    scalars = (block_slot, degree_ids, block_zero)
    signal = signal_inverse.reshape(16, 128)
    bands = band_of_ell.reshape(16, 128)

    state = None
    rows = row_transforms(sky, noise, outer, outer_t, twist, inner, zero_rows, None)
    for sweep in range(ITERS):
        received = exchange(rows)
        last = sweep == ITERS - 1
        state, result = mode_step(
            sweep == 0, last, scalars, received, legendre, signal, place, spread, state, bands
        )
        if not last:
            rows = row_transforms(
                sky, noise, outer, outer_t, twist, inner, zero_rows, exchange(result)
            )
    partial = result.reshape(sim_local, 2, BANDS).sum(axis=1)
    copies = jnp.broadcast_to(partial[None], (BLK, sim_local, BANDS))
    band_proj = jnp.sum(lax.all_to_all(copies, "blk", 0, 0, tiled=True), axis=0)
    all_proj = lax.all_gather(band_proj, "sim", axis=0, tiled=True)
    sim_mean = jnp.mean(all_proj, axis=0)
    center = all_proj - sim_mean[None, :]
    fisher = jnp.dot(center.T, center, precision=PRECISE) / all_proj.shape[0]
    filtered = state.reshape(block_count, MG, set_count, sim_local, 2, 128)
    return (filtered, band_proj, fisher)


def solution(mesh):
    return jax.shard_map(
        shards,
        mesh=mesh,
        in_specs=(
            P(None, "sim", "blk", None),
            P("blk", None),
            P(),
            P("blk", None, None, None),
            P(),
            P("blk", None),
            P(),
        ),
        out_specs=(P("blk", None, None, "sim", None, None), P("sim", None), P()),
        check_vma=False,
    )
```

time: 516 us -> 190 us (0.37); the launches traced: 507 us -> 190 us
  matrix products: 209 us -> 0.82 us
  local copies, waits for them, and re-layouts: 128 us -> 15.3 us
  Pallas kernels: 0 us -> 55.1 us
  blocking collectives: 118 us -> 98.1 us
  starting transfers between devices: 23.4 us -> 8.24 us
  waiting for transfers between devices: 17.7 us -> 7.18 us
    dot_general x66 -> x0, matrix products: 208 us -> none  [the longest x4 58.8 us: project(): jnp.einsum('bsdrpi,birl->bisdpl', chosen, legendre, preferred_element_typ...]
    psum x1 -> x0, blocking collectives: 67.6 us -> none  [shards(): band_proj = lax.psum(partial_value, 'blk') * norm_scale[None, :]]
    pallas_call x0 -> x8, Pallas kernels: none -> 55.1 us  [the longest x4 45.3 us: mode_step(): pl.pallas_call(body, out_shape=out_shapes, grid_spec=pltpu.PrefetchScalar...]
    all_to_all x3 -> x7, blocking collectives: 37.4 us -> 85.7 us  [the longest x6 74.7 us: exchange(): return lax.all_to_all(rows, 'blk', 0, 0, tiled=True)]
    gather x3 -> x0, local copies, waits for them, and re-layouts: 46.1 us -> none  [the longest x1 22.8 us: shards(): band_ids = jnp.take(band_of_ell, degrees)]
    reshape x24 -> x1, local copies, waits for them, and re-layouts: 43.1 us -> 0.1 us  [shards(): zero_rows = jnp.broadcast_to((upper[:, :2].T == 0).astype(F32)[:, None, :...]
    all_to_all x4 -> x1, starting transfers between devices: 23.4 us -> 8.24 us  [exchange(): return lax.all_to_all(rows, 'blk', 0, 0, tiled=True)]
    all_to_all x4 -> x1, waiting for transfers between devices: 17.7 us -> 7.18 us  [exchange(): return lax.all_to_all(rows, 'blk', 0, 0, tiled=True)]
  transfers between devices with their start and end apart: 4 -> 1, of which waited for: 2 -> 1; matrix products, arithmetic and copies ran while one was open for 10% -> 1% of each run, Pallas kernels for 0% -> 0%
where the time goes in v1:
time: 190 us
  blocking collectives  98.1 us (52%)
  Pallas kernels  55.1 us (29%)
  local copies, waits for them, and re-layouts  15.3 us (8%)
  starting transfers between devices  8.24 us (4%)
  waiting for transfers between devices  7.18 us (4%)
  other arithmetic  3.77 us (2%)
    all_to_all x6, blocking collectives, exchange(): return lax.all_to_all(rows, 'blk', 0, 0, tiled=True)  74.7 us
    pallas_call x4, Pallas kernels, mode_step(): pl.pallas_call(body, out_shape=out_shapes, grid_spec=pltpu.PrefetchScalar...  45.3 us
    unnamed x44, local copies, waits for them, and re-layouts  13.9 us
    all_gather x1, blocking collectives, shards(): all_proj = lax.all_gather(band_proj, 'sim', axis=0, tiled=True)  12.5 us
    all_to_all x1, blocking collectives, shards(): band_proj = jnp.sum(lax.all_to_all(copies, 'blk', 0, 0, tiled=True), axis=0)  11 us
    all_to_all x1, starting transfers between devices, exchange(): return lax.all_to_all(rows, 'blk', 0, 0, tiled=True)  8.24 us
    pallas_call x3, Pallas kernels, row_transforms(): pl.pallas_call(rows_kernel, out_shape=result, scratch_shapes=scratch + [p...  7.77 us
    all_to_all x1, waiting for transfers between devices, exchange(): return lax.all_to_all(rows, 'blk', 0, 0, tiled=True)  7.18 us
  transfers between devices with their start and end apart: 1, of which 1 were waited for; matrix products, arithmetic and copies ran while one was open for 1% of the time, Pallas kernels for 0%

profile of v1, /device:TPU:0, one launch (start us, length us, event | category | flops | bytes accessed | tf_op | source)
XLA Modules:
  0.0 189.5 jit_solution(14803574876432242520)
XLA Ops:
  0.6 0.1 fusion.9
  0.7 0.7 add_select_fusion.2
  1.4 0.1 select_reduce_fusion.1
  1.5 0.7 add_select_fusion.1
  2.2 0.3 sine_multiply_fusion
  2.6 0.1 reshape.178.zero_ref
  2.8 0.0 copy-start.2
  2.8 1.0 copy-done.2
  3.8 0.8 copy-done.8
  4.7 0.8 copy-done.10
  5.5 0.8 copy-done.12
  6.3 2.0 %first_rows.1 = bf16[32,32,128]{2,1,0:T(8,128)(2,1)} custom-call(f32[16,64,128]{2,1,0:T(8,128)S(1)} %bitcast.24, f32[64,128]{1,0:T(8,128)S(1)} %bitcast.28, bf16[2,128,64]{2,1,0:T(8,128)(2,1)S(1)} %copy-done.8, f32[2,64,128]{2,1,0:T(8,128)S(1)} %copy-done.10, bf16[2,2,128,256]{3,2,1,0:T(8,128)(2,1)S(1)} %pad_maximum_fusion.inner_ref, ...), custom_call_target="tpu_custom_call" | custom-call | tf_op jit(solution)/shard_map/first_rows/pallas_call | solution.py:318
  8.3 8.2 %all-to-all-start = ((bf16[32,32,128]{2,1,0:T(8,128)(2,1)}), bf16[32,32,128]{2,1,0:T(8,128)(2,1)S(1)}, u32[]{:S(2)}, u32[]{:S(2)}) async-start(bf16[32,32,128]{2,1,0:T(8,128)(2,1)} %first_rows.1), calls=%async_computation | async-start | bytes 524288 | tf_op jit(solution)/shard_map/all_to_all | solution.py:391
  16.5 0.9 convert_reduce_fusion
  17.4 0.8 slice_bitcast_fusion
  18.2 0.1 select_reduce_fusion.2
  18.3 7.2 %all-to-all-done.refs_3_ = bf16[32,32,128]{2,1,0:T(8,128)(2,1)S(1)} async-done(((bf16[32,32,128]{2,1,0:T(8,128)(2,1)}), bf16[32,32,128]{2,1,0:T(8,128)(2,1)S(1)}, u32[]{:S(2)}, u32[]{:S(2)}) %all-to-all-start) | async-done | bytes 262176 | tf_op jit(solution)/shard_map/all_to_all | solution.py:391
  25.5 3.5 %copy-done = bf16[34,16,64,128]{3,2,1,0:T(8,128)(2,1)S(1)} copy-done((bf16[34,16,64,128]{3,2,1,0:T(8,128)(2,1)S(1)}, bf16[34,16,64,128]{3,2,1,0:T(8,128)(2,1)}, u32[]{:S(2)}) %copy-start) | copy-done | bytes 8912920
  29.0 0.9 copy-done.6
  29.9 0.7 copy-done.15
  30.6 0.7 copy-done.17
  31.3 0.0 copy-start.14
  31.4 0.0 copy-start.7
  31.4 0.0 copy-start.16
  31.4 11.2 %modes_first.1 = (bf16[34,512,128]{2,1,0:T(8,128)(2,1)S(1)}, bf16[32,32,128]{2,1,0:T(8,128)(2,1)S(1)}) custom-call(s32[34]{0:T(128)S(1)} %get-tuple-element.20.refs_0_, s32[34]{0:T(128)S(1)} %get-tuple-element.28.refs_1_, s32[34]{0:T(128)S(1)} %get-tuple-element.19.refs_2_, bf16[32,32,128]{2,1,0:T(8,128)(2,1)S(1)} %all-to-all-done.refs_3_, ...), custom_call_target="tpu_custom_call" | custom-call | tf_op jit(solution)/shard_map/modes_first/pallas_call | solution.py:375
  42.6 0.0 copy-start.4
  42.6 2.1 %copy-done.4 = bf16[34,512,128]{2,1,0:T(8,128)(2,1)} copy-done((bf16[34,512,128]{2,1,0:T(8,128)(2,1)}, bf16[34,512,128]{2,1,0:T(8,128)(2,1)S(1)}, u32[]{:S(2)}) %copy-start.4) | copy-done | bytes 4456472
  44.7 12.4 %all_to_all.40.coeff_ref = bf16[32,32,128]{2,1,0:T(8,128)(2,1)S(1)} all-to-all(bf16[32,32,128]{2,1,0:T(8,128)(2,1)S(1)} %get-tuple-element.11), channel_id=1, replica_groups=mesh['blk'=32,'sim'=4] {'blk'}, dimensions={0} | all-to-all | bytes 524288 | tf_op jit(solution)/shard_map/all_to_all | solution.py:391
  57.2 2.6 %rows.3 = bf16[32,32,128]{2,1,0:T(8,128)(2,1)S(1)} custom-call(f32[16,64,128]{2,1,0:T(8,128)S(1)} %bitcast.25, f32[64,128]{1,0:T(8,128)S(1)} %bitcast.29, bf16[2,128,64]{2,1,0:T(8,128)(2,1)S(1)} %copy-done.9, bf16[2,64,128]{2,1,0:T(8,128)(2,1)S(1)} %copy-done.14, f32[2,64,128]{2,1,0:T(8,128)S(1)} %copy-done.11, ...), custom_call_target="tpu_custom_call" | custom-call | tf_op jit(solution)/shard_map/rows/pallas_call | solution.py:325
  59.8 12.5 %all_to_all.41.refs_3_ = bf16[32,32,128]{2,1,0:T(8,128)(2,1)S(1)} all-to-all(bf16[32,32,128]{2,1,0:T(8,128)(2,1)S(1)} %rows.3), channel_id=1, replica_groups=mesh['blk'=32,'sim'=4] {'blk'}, dimensions={0} | all-to-all | bytes 524288 | tf_op jit(solution)/shard_map/all_to_all | solution.py:391
  72.3 0.0 copy-start.5
  72.3 2.3 %copy-done.5 = bf16[34,512,128]{2,1,0:T(8,128)(2,1)S(1)} copy-done((bf16[34,512,128]{2,1,0:T(8,128)(2,1)S(1)}, bf16[34,512,128]{2,1,0:T(8,128)(2,1)}, u32[]{:S(2)}) %copy-start.5) | copy-done | bytes 4456472
  74.6 11.4 %modes.2 = (bf16[34,512,128]{2,1,0:T(8,128)(2,1)S(1)}, bf16[32,32,128]{2,1,0:T(8,128)(2,1)S(1)}) custom-call(s32[34]{0:T(128)S(1)} %get-tuple-element.20.refs_0_, s32[34]{0:T(128)S(1)} %get-tuple-element.28.refs_1_, s32[34]{0:T(128)S(1)} %get-tuple-element.19.refs_2_, bf16[32,32,128]{2,1,0:T(8,128)(2,1)S(1)} %all_to_all.41.refs_3_, ...), custom_call_target="tpu_custom_call" | custom-call | tf_op jit(solution)/shard_map/modes/pallas_call | solution.py:375
  85.9 12.5 %all_to_all.42.coeff_ref = bf16[32,32,128]{2,1,0:T(8,128)(2,1)S(1)} all-to-all(bf16[32,32,128]{2,1,0:T(8,128)(2,1)S(1)} %get-tuple-element.13), channel_id=1, replica_groups=mesh['blk'=32,'sim'=4] {'blk'}, dimensions={0} | all-to-all | bytes 524288 | tf_op jit(solution)/shard_map/all_to_all | solution.py:391
  98.4 2.6 %rows.4 = bf16[32,32,128]{2,1,0:T(8,128)(2,1)S(1)} custom-call(f32[16,64,128]{2,1,0:T(8,128)S(1)} %bitcast.26, f32[64,128]{1,0:T(8,128)S(1)} %bitcast.30, bf16[2,128,64]{2,1,0:T(8,128)(2,1)S(1)} %copy-done.9, bf16[2,64,128]{2,1,0:T(8,128)(2,1)S(1)} %copy-done.14, f32[2,64,128]{2,1,0:T(8,128)S(1)} %copy-done.11, ...), custom_call_target="tpu_custom_call" | custom-call | tf_op jit(solution)/shard_map/rows/pallas_call | solution.py:325
  101.0 12.5 %all_to_all.43.refs_3_ = bf16[32,32,128]{2,1,0:T(8,128)(2,1)S(1)} all-to-all(bf16[32,32,128]{2,1,0:T(8,128)(2,1)S(1)} %rows.4), channel_id=1, replica_groups=mesh['blk'=32,'sim'=4] {'blk'}, dimensions={0} | all-to-all | bytes 524288 | tf_op jit(solution)/shard_map/all_to_all | solution.py:391
  113.5 11.4 %modes.3 = (bf16[34,512,128]{2,1,0:T(8,128)(2,1)S(1)}, bf16[32,32,128]{2,1,0:T(8,128)(2,1)S(1)}) custom-call(s32[34]{0:T(128)S(1)} %get-tuple-element.20.refs_0_, s32[34]{0:T(128)S(1)} %get-tuple-element.28.refs_1_, s32[34]{0:T(128)S(1)} %get-tuple-element.19.refs_2_, bf16[32,32,128]{2,1,0:T(8,128)(2,1)S(1)} %all_to_all.43.refs_3_, ...), custom_call_target="tpu_custom_call" | custom-call | tf_op jit(solution)/shard_map/modes/pallas_call | solution.py:375
  124.9 12.5 %all_to_all.44.coeff_ref = bf16[32,32,128]{2,1,0:T(8,128)(2,1)S(1)} all-to-all(bf16[32,32,128]{2,1,0:T(8,128)(2,1)S(1)} %get-tuple-element.15), channel_id=1, replica_groups=mesh['blk'=32,'sim'=4] {'blk'}, dimensions={0} | all-to-all | bytes 524288 | tf_op jit(solution)/shard_map/all_to_all | solution.py:391
  137.3 2.6 %rows.5 = bf16[32,32,128]{2,1,0:T(8,128)(2,1)S(1)} custom-call(f32[16,64,128]{2,1,0:T(8,128)S(1)} %bitcast.27, f32[64,128]{1,0:T(8,128)S(1)} %bitcast.31, bf16[2,128,64]{2,1,0:T(8,128)(2,1)S(1)} %copy-done.9, bf16[2,64,128]{2,1,0:T(8,128)(2,1)S(1)} %copy-done.14, f32[2,64,128]{2,1,0:T(8,128)S(1)} %copy-done.11, ...), custom_call_target="tpu_custom_call" | custom-call | tf_op jit(solution)/shard_map/rows/pallas_call | solution.py:325
  139.9 12.5 %all_to_all.45.refs_3_ = bf16[32,32,128]{2,1,0:T(8,128)(2,1)S(1)} all-to-all(bf16[32,32,128]{2,1,0:T(8,128)(2,1)S(1)} %rows.5), channel_id=1, replica_groups=mesh['blk'=32,'sim'=4] {'blk'}, dimensions={0} | all-to-all | bytes 524288 | tf_op jit(solution)/shard_map/all_to_all | solution.py:391
  152.4 11.3 %modes_last.1 = (bf16[34,512,128]{2,1,0:T(8,128)(2,1)}, f32[16,32]{1,0:T(8,128)S(1)}) custom-call(s32[34]{0:T(128)S(1)} %get-tuple-element.20.refs_0_, s32[34]{0:T(128)S(1)} %get-tuple-element.28.refs_1_, s32[34]{0:T(128)S(1)} %get-tuple-element.19.refs_2_, bf16[32,32,128]{2,1,0:T(8,128)(2,1)S(1)} %all_to_all.45.refs_3_, ...), custom_call_target="tpu_custom_call" | custom-call | tf_op jit(solution)/shard_map/modes_last/pallas_call | solution.py:375
  163.7 0.1 reshape.181
  163.9 11.0 %all_to_all.46 = f32[32,1,256]{2,1,0:T(1,128)S(1)} all-to-all(f32[32,1,256]{2,1,0:T(1,128)S(1)} %reshape.181), channel_id=1, replica_groups=mesh['blk'=32,'sim'=4] {'blk'}, dimensions={0} | all-to-all | bytes 65536 | tf_op jit(solution)/shard_map/all_to_all | solution.py:455
  174.8 0.5 broadcast.240
  175.3 0.7 reduce.4
  176.1 0.1 reshape.182
  176.2 12.5 %all_gather.3 = f32[32,32]{1,0:T(8,128)S(1)} all-gather(f32[8,32]{1,0:T(8,128)S(1)} %reduce_sum.68), channel_id=1, replica_groups=mesh['blk'=32,'sim'=4] {'sim'}, dimensions={0}, use_global_device_ids=true | all-gather | bytes 5120 | tf_op jit(solution)/shard_map/all_gather | solution.py:456
  188.7 0.8 convolution_multiply_fusion
  (38 shorter events, 0.2 us)
Async XLA Ops:
  2.8 1.0 copy-start.2
  3.8 0.8 copy-start.8
  4.7 0.8 copy-start.10
  5.5 0.8 copy-start.12
  8.3 17.2 %all-to-all-start = ((bf16[32,32,128]{2,1,0:T(8,128)(2,1)}), bf16[32,32,128]{2,1,0:T(8,128)(2,1)S(1)}, u32[]{:S(2)}, u32[]{:S(2)}) async-start(bf16[32,32,128]{2,1,0:T(8,128)(2,1)} %first_rows.1), calls=%async_computation | async-start | bytes 524288 | tf_op jit(solution)/shard_map/all_to_all | solution.py:391
  25.5 3.5 %copy-start = (bf16[34,16,64,128]{3,2,1,0:T(8,128)(2,1)S(1)}, bf16[34,16,64,128]{3,2,1,0:T(8,128)(2,1)}, u32[]{:S(2)}) copy-start(bf16[34,16,64,128]{3,2,1,0:T(8,128)(2,1)} %refs_4_.7) | copy-start | bytes 26738692
  29.0 0.9 copy-start.6
  29.9 0.7 copy-start.15
  30.6 0.7 copy-start.17
  31.3 25.9 %copy-start.3 = (f32[2,8,2,4096]{3,2,1,0:T(2,128)S(1)}, f32[2,8,2,4096]{3,2,1,0:T(2,128)}, u32[]{:S(2)}) copy-start(f32[2,8,2,4096]{3,2,1,0:T(2,128)} %param.12) | copy-start | bytes 1572868
  31.3 25.9 %copy-start.9 = (bf16[2,128,64]{2,1,0:T(8,128)(2,1)S(1)}, bf16[2,128,64]{2,1,0:T(8,128)(2,1)}, u32[]{:S(2)}) copy-start(bf16[2,128,64]{2,1,0:T(8,128)(2,1)} %constant.84.clone.outer_ref) | copy-start | bytes 98308
  31.3 25.9 %copy-start.11 = (f32[2,64,128]{2,1,0:T(8,128)S(1)}, f32[2,64,128]{2,1,0:T(8,128)}, u32[]{:S(2)}) copy-start(f32[2,64,128]{2,1,0:T(8,128)} %constant.86.clone.twist_ref) | copy-start | bytes 196612
  31.3 25.9 %copy-start.13 = (f32[2,4096]{1,0:T(2,128)S(1)}, f32[2,4096]{1,0:T(2,128)}, u32[]{:S(2)}) copy-start(f32[2,4096]{1,0:T(2,128)} %param.13) | copy-start | bytes 98308
  31.3 25.9 %copy-start.14 = (bf16[2,64,128]{2,1,0:T(8,128)(2,1)S(1)}, bf16[2,64,128]{2,1,0:T(8,128)(2,1)}, u32[]{:S(2)}) copy-start(bf16[2,64,128]{2,1,0:T(8,128)(2,1)} %constant.85.clone.outer_t_ref) | copy-start | bytes 98308
  31.3 40.9 %copy-start.1 = (bf16[34,16,64,128]{3,2,1,0:T(8,128)(2,1)S(1)}, bf16[34,16,64,128]{3,2,1,0:T(8,128)(2,1)}, u32[]{:S(2)}) copy-start(bf16[34,16,64,128]{3,2,1,0:T(8,128)(2,1)} %refs_4_.7) | copy-start | bytes 26738692
  31.4 40.9 %copy-start.7 = (bf16[4,64,256]{2,1,0:T(8,128)(2,1)S(1)}, bf16[4,64,256]{2,1,0:T(8,128)(2,1)}, u32[]{:S(2)}) copy-start(bf16[4,64,256]{2,1,0:T(8,128)(2,1)} %constant.87.clone.refs_6_) | copy-start | bytes 393220
  31.4 40.9 %copy-start.16 = (bf16[64,128]{1,0:T(8,128)(2,1)S(1)}, bf16[64,128]{1,0:T(8,128)(2,1)}, u32[]{:S(2)}) copy-start(bf16[64,128]{1,0:T(8,128)(2,1)} %constant.88.clone.refs_7_) | copy-start | bytes 49156
  31.4 40.9 %copy-start.18 = (f32[2048]{0:T(1024)S(1)}, f32[2048]{0:T(1024)}, u32[]{:S(2)}) copy-start(f32[2048]{0:T(1024)} %param.14) | copy-start | bytes 24580
  42.6 2.1 %copy-start.4 = (bf16[34,512,128]{2,1,0:T(8,128)(2,1)}, bf16[34,512,128]{2,1,0:T(8,128)(2,1)S(1)}, u32[]{:S(2)}) copy-start(bf16[34,512,128]{2,1,0:T(8,128)(2,1)S(1)} %get-tuple-element.12.refs_8_) | copy-start | bytes 13369348
  72.3 2.3 %copy-start.5 = (bf16[34,512,128]{2,1,0:T(8,128)(2,1)S(1)}, bf16[34,512,128]{2,1,0:T(8,128)(2,1)}, u32[]{:S(2)}) copy-start(bf16[34,512,128]{2,1,0:T(8,128)(2,1)} %copy-done.4) | copy-start | bytes 13369348
  113.5 38.9 %copy-start.19 = (s32[2048]{0:T(1024)S(1)}, s32[2048]{0:T(1024)}, u32[]{:S(2)}) copy-start(s32[2048]{0:T(1024)} %param.18) | copy-start | bytes 24580
  176.2 13.3 %copy-start.20 = (f32[8,32]{1,0:T(8,128)}, f32[8,32]{1,0:T(8,128)S(1)}, u32[]{:S(2)}) copy-start(f32[8,32]{1,0:T(8,128)S(1)} %reduce_sum.68) | copy-start | bytes 3076

commit v2 on v1

v2 whole, which is shorter than its diff:
```python
import math

import jax
import jax.numpy as jnp
import numpy as np
from jax import lax
from jax.experimental import pallas as pl
from jax.experimental.pallas import tpu as pltpu
from jax.sharding import PartitionSpec as P

NPHI = 4096
BANDS = 32
ITERS = 4
BLK = 32
CYC = 2
VEC = 16
OUTER = 32
INNER = 128
MG = 16
SLOTS = 4
PAIRS = 18
F32 = jnp.float32
BF16 = jnp.bfloat16
PRECISE = lax.Precision.HIGHEST
NT = (((1,), (1,)), ((), ()))
TN = (((0,), (0,)), ((), ()))
NN = (((1,), (0,)), ((), ()))


def split(value):
    high = value.astype(BF16)
    return high, (value - high.astype(F32)).astype(BF16)


def dot(left, right, dims=NN):
    return lax.dot_general(left, right, dims, preferred_element_type=F32)


def dot3(left, right, dims=NN):
    return (
        dot(left[0], right[0], dims) + dot(left[0], right[1], dims) + dot(left[1], right[0], dims)
    )


def np_split(value):
    high = value.astype(np.float32).astype(jnp.bfloat16)
    low = (value - high.astype(np.float64)).astype(np.float32).astype(jnp.bfloat16)
    return np.stack([high, low])


def constant_tables():
    k = np.arange(OUTER).reshape(2, 1, MG)
    k_rows = np.broadcast_to(k, (2, CYC, MG)).reshape(-1)
    cycle_rows = np.broadcast_to(np.arange(CYC).reshape(1, CYC, 1), (2, CYC, MG)).reshape(-1)
    a_cols = np.repeat(np.arange(OUTER), CYC)
    cycle_cols = np.tile(np.arange(CYC), OUTER)
    angle = 2.0 * np.pi * (k_rows[:, None] * a_cols[None, :] % OUTER) / OUTER
    same = cycle_rows[:, None] == cycle_cols[None, :]
    outer = np.concatenate([np.cos(angle) * same, -np.sin(angle) * same], axis=0)
    twist = 2.0 * np.pi * (k_rows[:, None] * np.arange(INNER)[None, :]) / NPHI
    twist_table = np.stack([np.cos(twist), np.sin(twist)]).astype(np.float32)
    return np_split(outer), np_split(outer.T), twist_table


def column(half, j, p, upper):
    return ((half * 2 + j) * 2 + p) * 2 + upper


def forward_part(field_of, outer_ref, twist_ref, inner_ref, zero_ref, out_ref, turned, staged):
    outer = (outer_ref[0], outer_ref[1])
    cos_twist, sin_twist = twist_ref[0], twist_ref[1]
    for v in range(VEC):
        first = dot3(outer, split(field_of(v)))
        real, imag = first[:64], first[64:]
        turned_real = real * cos_twist + imag * sin_twist
        turned_imag = imag * cos_twist - real * sin_twist
        for half in range(2):
            for cycle in range(CYC):
                at = (half * 2 + cycle) * MG
                rows = pl.ds(cycle * 256 + v, MG, stride=VEC)
                turned[half, 0, rows, :] = turned_real[at : at + MG]
                turned[half, 1, rows, :] = turned_imag[at : at + MG]
    for half in range(2):
        inner = (inner_ref[0, half], inner_ref[1, half])
        both = jnp.concatenate([turned[half, 0], turned[half, 1]], axis=1)
        coeffs = dot3(inner, split(both), NT)
        if half == 0:
            coeffs = coeffs * zero_scale(zero_ref)
        for j in range(2):
            for p in range(2):
                for upper in range(2):
                    for cycle in range(CYC):
                        row = column(half, j, p, upper) * 2 + cycle
                        lanes = cycle * 256 + upper * 128
                        staged[:, row, :] = coeffs[
                            (j * 2 + p) * 32 : (j * 2 + p + 1) * 32, lanes : lanes + 128
                        ]
    out_ref[...] = staged[...].astype(BF16)


def zero_scale(zero_ref):
    lane = lax.broadcasted_iota(jnp.int32, (128, 512), 1)
    own = jnp.broadcast_to(zero_ref[...], (128, 512))
    return jnp.where(jnp.logical_and(lane % 256 < VEC, own > 0.0), math.sqrt(0.5), 1.0)


def first_rows_kernel(
    sky_ref, noise_ref, outer_ref, twist_ref, inner_ref, zero_ref, out_ref, turned, staged
):
    noise = noise_ref[...]
    forward_part(
        lambda v: noise * sky_ref[v],
        outer_ref, twist_ref, inner_ref, zero_ref, out_ref, turned, staged,
    )


def rows_kernel(
    sky_ref, noise_ref, outer_ref, outer_t_ref, twist_ref, inner_ref, zero_ref, coeff_ref,
    out_ref, turned, staged,
):
    staged[...] = coeff_ref[...].astype(F32)
    for half in range(2):
        rows = []
        for j in range(2):
            for p in range(2):
                rows.append(
                    jnp.concatenate(
                        [
                            staged[:, column(half, j, p, upper) * 2 + cycle, :]
                            for cycle in range(CYC)
                            for upper in range(2)
                        ],
                        axis=1,
                    )
                )
        coeffs = jnp.concatenate(rows, axis=0)
        if half == 0:
            coeffs = coeffs * zero_scale(zero_ref)
        coeffs = coeffs.astype(BF16)
        inner = dot(coeffs, inner_ref[0, half], TN) + dot(coeffs, inner_ref[1, half], TN)
        for i in range(MG):
            at = half * CYC * MG + i
            cos_twist = jnp.broadcast_to(twist_ref[0, at : at + 1], (VEC, 128))
            sin_twist = jnp.broadcast_to(twist_ref[1, at : at + 1], (VEC, 128))
            for cycle in range(CYC):
                rows = slice(cycle * 256 + i * VEC, cycle * 256 + (i + 1) * VEC)
                real, imag = inner[rows, :128], inner[rows, 128:]
                turned[half, 0, rows, :] = real * cos_twist - imag * sin_twist
                turned[half, 1, rows, :] = real * sin_twist + imag * cos_twist
    noise = noise_ref[...]
    outer_t = (outer_t_ref[0], outer_t_ref[1])
    fields = []
    for v in range(VEC):
        spectrum = jnp.concatenate(
            [
                turned[half, part, pl.ds(cycle * 256 + v, MG, stride=VEC), :]
                for part in range(2)
                for half in range(2)
                for cycle in range(CYC)
            ],
            axis=0,
        )
        fields.append(noise * (sky_ref[v] - dot3(outer_t, split(spectrum))))
    forward_part(
        lambda v: fields[v],
        outer_ref, twist_ref, inner_ref, zero_ref, out_ref, turned, staged,
    )


def find_pairs(group_ref, block_ref, own_ref, order, pair_slot, pair_live, pair_zero, counter):
    own = own_ref[0]
    groups = [group_ref[own, s] for s in range(SLOTS)]
    base = jnp.int32(0)
    for s in range(SLOTS):
        half = groups[s] % 2
        rank = jnp.int32(0)
        for earlier in range(s):
            rank = rank + jnp.where(groups[earlier] % 2 == half, 1, 0)
        slot = 2 * half + rank
        is_zero = jnp.where(groups[s] == 0, 1, 0)
        count = 16 - groups[s] // 8
        pairs = (count + 1) // 2
        counter[s] = 2 * base

        def mark(pair, carry, slot=slot, is_zero=is_zero):
            pair_slot[pair] = slot
            pair_zero[pair] = is_zero
            pair_live[pair] = 1
            return carry

        lax.fori_loop(base, base + pairs, mark, 0)
        base = base + pairs

    def place(block, carry):
        slot = block_ref[block, 0]
        at = counter[slot]
        order[at] = block
        counter[slot] = at + 1
        return carry

    lax.fori_loop(0, 34, place, 0)
    for s in range(SLOTS):
        at = counter[s]

        @pl.when(at % 2 == 1)
        def _():
            order[at] = order[at - 1]
            pair_live[at // 2] = 0


def block_copy(legendre_ref, table, arrived, order, at):
    block = order[at]
    return pltpu.make_async_copy(legendre_ref.at[block], table.at[block], arrived.at[at])


def start_blocks(legendre_ref, table, arrived, order, pair_live):
    def start(pair, carry):
        block_copy(legendre_ref, table, arrived, order, 2 * pair).start()

        @pl.when(pair_live[pair] == 1)
        def _():
            block_copy(legendre_ref, table, arrived, order, 2 * pair + 1).start()

        return carry

    lax.fori_loop(0, PAIRS, start, 0)


def wait_blocks(legendre_ref, table, arrived, order, pair_live, pair):
    block_copy(legendre_ref, table, arrived, order, 2 * pair).wait()

    @pl.when(pair_live[pair] == 1)
    def _():
        block_copy(legendre_ref, table, arrived, order, 2 * pair + 1).wait()


def products_kernel(
    group_ref, block_ref, own_ref, legendre_ref, signal_ref, out_ref,
    table, sums, order, pair_slot, pair_live, pair_zero, counter, arrived,
):
    find_pairs(group_ref, block_ref, own_ref, order, pair_slot, pair_live, pair_zero, counter)
    start_blocks(legendre_ref, table, arrived, order, pair_live)
    sums[...] = jnp.zeros_like(sums)

    def pair_step(pair, carry):
        wait_blocks(legendre_ref, table, arrived, order, pair_live, pair)
        first, second = order[2 * pair], order[2 * pair + 1]
        live = pair_live[pair].astype(F32)
        precond_first = 1.0 / (2.0 + signal_ref[pl.ds(block_ref[first, 1], 1), :])
        precond_second = 1.0 / (2.0 + signal_ref[pl.ds(block_ref[second, 1], 1), :])
        precond = jnp.concatenate([precond_first, precond_second], axis=1)
        weight = jnp.concatenate([precond_first, precond_second * live], axis=1)
        weights = []
        for _ in range(ITERS - 1):
            weights.append(jnp.broadcast_to(weight, (64, 256)))
            weight = weight * (2.0 * precond)
        for i in range(MG):
            values = jnp.concatenate([table[first, i], table[second, i]], axis=1)
            wide = values.astype(F32)
            scaled = jnp.concatenate([(wide * w).astype(BF16) for w in weights], axis=0)
            sums[pair_slot[pair] * MG + i] += dot(values, scaled, NT)
        return carry

    lax.fori_loop(0, PAIRS, pair_step, 0)
    for at in range(SLOTS * MG):
        out_ref[at // 8, (at % 8) * 64 : (at % 8 + 1) * 64, :] = sums[at].astype(BF16)


def apply_kernel(count, *refs):
    coeff_ref, product_ref = refs[:2]
    earlier = refs[2 : 1 + count]
    kept_ref, out_ref, staged, ordered = refs[1 + count :]
    staged[...] = coeff_ref[...].astype(F32)
    for c in range(16):
        for cycle in range(CYC):
            ordered[c, pl.ds(cycle, BLK, stride=2), :] = staged[:, 2 * c + cycle, :]
    kept_ref[...] = ordered[...].astype(BF16)
    history = [kept_ref] + list(earlier)[::-1]
    lane = lax.broadcasted_iota(jnp.int32, (64, 256), 1) % 128 // VEC
    for slot in range(SLOTS):
        for upper in range(2):
            at = [(slot * 2 + p) * 2 + upper for p in range(2)]
            right = jnp.concatenate(
                [jnp.concatenate([ref[at[0]], ref[at[1]]], axis=1) for ref in history], axis=0
            )
            mixed = dot(product_ref[slot * 2 + upper, :, : 64 * count], right)
            result = mixed[:64]
            for i in range(1, 8):
                result = jnp.where(lane == i, mixed[i * 64 : (i + 1) * 64], result)
            ordered[at[0]] = result[:, :128]
            ordered[at[1]] = result[:, 128:]
    for c in range(16):
        for cycle in range(CYC):
            staged[:, 2 * c + cycle, :] = ordered[c, pl.ds(cycle, BLK, stride=2), :]
    out_ref[...] = staged[...].astype(BF16)


def last_kernel(
    group_ref, block_ref, own_ref, coeff_ref, kept0_ref, kept1_ref, kept2_ref, legendre_ref,
    signal_ref, band_ref, state_ref, band_out,
    table, staged, mixed, packed, products, outgoing,
    order, pair_slot, pair_live, pair_zero, counter, arrived, sent,
):
    find_pairs(group_ref, block_ref, own_ref, order, pair_slot, pair_live, pair_zero, counter)
    start_blocks(legendre_ref, table, arrived, order, pair_live)
    products[...] = jnp.zeros_like(products)
    staged[...] = coeff_ref[...].astype(F32)
    blank = jnp.zeros((64, 128), BF16)
    unit = (
        lax.broadcasted_iota(jnp.int32, (128, 128), 0)
        == lax.broadcasted_iota(jnp.int32, (128, 128), 1)
    ).astype(BF16)
    for slot in range(SLOTS):
        for upper in range(2):
            for sweep in range(ITERS):
                for p in range(2):
                    c = (slot * 2 + p) * 2 + upper
                    if sweep < ITERS - 1:
                        tile = (kept0_ref, kept1_ref, kept2_ref)[sweep][c]
                    else:
                        for cycle in range(CYC):
                            mixed[0, pl.ds(cycle, BLK, stride=2), :] = staged[:, 2 * c + cycle, :]
                        tile = mixed[0, 0:64, :].astype(BF16)
                    turned = dot(unit, jnp.concatenate([tile, blank], axis=0), NT)
                    for i in range(8):
                        rows = pl.ds(sweep * 32 + p, VEC, stride=2)
                        mixed[1 + i, rows, :] = turned[i * VEC : (i + 1) * VEC]
            for i in range(8):
                packed[slot * MG + upper * 8 + i] = mixed[1 + i, :, 0:64].astype(BF16)

    def out_copy(pair, which):
        slot = pair % 2
        return pltpu.make_async_copy(
            outgoing.at[slot, which],
            state_ref.at[order[2 * pair + which]],
            sent.at[slot, which],
        )

    def wait_out(pair):
        out_copy(pair, 0).wait()

        @pl.when(pair_live[pair] == 1)
        def _():
            out_copy(pair, 1).wait()

    def pair_step(pair, carry):
        wait_blocks(legendre_ref, table, arrived, order, pair_live, pair)

        @pl.when(pair >= 2)
        def _():
            wait_out(pair - 2)

        first, second = order[2 * pair], order[2 * pair + 1]
        degrees = (block_ref[first, 1], block_ref[second, 1])
        precond = jnp.concatenate(
            [1.0 / (2.0 + signal_ref[pl.ds(degree, 1), :]) for degree in degrees], axis=1
        )
        damp = 2.0 * precond
        total = jnp.zeros((VEC, 256), F32)
        for i in range(MG):
            values = jnp.concatenate([table[first, i], table[second, i]], axis=1)
            harmonic = dot(packed[pair_slot[pair] * MG + i], values)
            state = harmonic[0:32]
            for sweep in range(1, ITERS):
                state = harmonic[sweep * 32 : (sweep + 1) * 32] + damp * state
            state = precond * state
            rounded = state.astype(BF16)
            outgoing[pair % 2, 0, i * 32 : (i + 1) * 32, :] = rounded[:, :128]
            outgoing[pair % 2, 1, i * 32 : (i + 1) * 32, :] = rounded[:, 128:]
            one = state[:VEC] * state[VEC:]
            if i == 0:
                one = one * jnp.where(pair_zero[pair] > 0, 0.5, 1.0)
            total = total + one
        total = 2.0 * total
        products[degrees[0]] += total[:, :128]
        out_copy(pair, 0).start()

        @pl.when(pair_live[pair] == 1)
        def _():
            products[degrees[1]] += total[:, 128:]
            out_copy(pair, 1).start()

        return carry

    lax.fori_loop(0, PAIRS, pair_step, 0)
    raw = jnp.zeros((VEC, BANDS), F32)
    counts = jnp.zeros((VEC, BANDS), F32)
    bins = lax.broadcasted_iota(jnp.int32, (BANDS, 128), 0)
    lane = lax.broadcasted_iota(jnp.int32, (VEC, 128), 1)
    for e in range(16):
        member = (jnp.broadcast_to(band_ref[e : e + 1, :], (BANDS, 128)) == bins).astype(F32)
        raw = raw + lax.dot_general(
            products[e], member, NT, precision=PRECISE, preferred_element_type=F32
        )
        weight = (2 * (e * 128 + lane) + 1).astype(F32)
        counts = counts + lax.dot_general(
            weight, member, NT, precision=PRECISE, preferred_element_type=F32
        )
    band_out[...] = raw * (1.0 / jnp.sqrt(counts))
    wait_out(PAIRS - 2)
    wait_out(PAIRS - 1)


def params(megabytes, **more):
    return pltpu.CompilerParams(vmem_limit_bytes=megabytes << 20, **more)


SENT = jax.ShapeDtypeStruct((BLK, 32, 128), BF16)
KEPT = jax.ShapeDtypeStruct((16, 64, 128), BF16)
SMEM = pl.BlockSpec(memory_space=pltpu.SMEM)
VMEM = pl.BlockSpec(memory_space=pltpu.VMEM)
ANY = pl.BlockSpec(memory_space=pl.ANY)


def row_transforms(sky, noise, outer, outer_t, twist, inner, zero_rows, coeffs):
    scratch = [pltpu.VMEM((2, 2, 512, 128), F32), pltpu.VMEM((BLK, 32, 128), F32)]
    if coeffs is None:
        return pl.pallas_call(
            first_rows_kernel,
            out_shape=SENT,
            scratch_shapes=scratch,
            compiler_params=params(32),
            name="first_rows",
        )(sky, noise, outer, twist, inner, zero_rows)
    return pl.pallas_call(
        rows_kernel,
        out_shape=SENT,
        scratch_shapes=scratch,
        compiler_params=params(32),
        name="rows",
    )(sky, noise, outer, outer_t, twist, inner, zero_rows, coeffs)


def pair_scratch():
    return [
        pltpu.SMEM((2 * PAIRS,), jnp.int32),
        pltpu.SMEM((PAIRS,), jnp.int32),
        pltpu.SMEM((PAIRS,), jnp.int32),
        pltpu.SMEM((PAIRS,), jnp.int32),
        pltpu.SMEM((SLOTS,), jnp.int32),
        pltpu.SemaphoreType.DMA((2 * PAIRS,)),
    ]


def cycle_products(scalars, legendre, signal):
    return pl.pallas_call(
        products_kernel,
        out_shape=jax.ShapeDtypeStruct((8, 512, 192), BF16),
        in_specs=[SMEM, SMEM, SMEM, ANY, VMEM],
        scratch_shapes=[
            pltpu.VMEM(legendre.shape, BF16),
            pltpu.VMEM((SLOTS * MG, 64, 192), F32),
        ]
        + pair_scratch(),
        compiler_params=params(40),
        name="cycle_products",
    )(*scalars, legendre, signal)


def apply_products(coeffs, products, kept):
    count = len(kept) + 1

    def body(*refs):
        apply_kernel(count, *refs)

    return pl.pallas_call(
        body,
        out_shape=(KEPT, SENT),
        scratch_shapes=[pltpu.VMEM((BLK, 32, 128), F32), pltpu.VMEM((16, 64, 128), F32)],
        compiler_params=params(32),
        name="apply_products_" + str(count),
    )(coeffs, products, *kept)


def last_step(scalars, coeffs, kept, legendre, signal, bands):
    return pl.pallas_call(
        last_kernel,
        out_shape=(
            jax.ShapeDtypeStruct((legendre.shape[0], 512, 128), BF16),
            jax.ShapeDtypeStruct((VEC, BANDS), F32),
        ),
        in_specs=[SMEM] * 3 + [VMEM] * 4 + [ANY, VMEM, VMEM],
        out_specs=(ANY, VMEM),
        scratch_shapes=[
            pltpu.VMEM(legendre.shape, BF16),
            pltpu.VMEM((BLK, 32, 128), F32),
            pltpu.VMEM((9, 128, 128), F32),
            pltpu.VMEM((SLOTS * MG, 128, 64), BF16),
            pltpu.VMEM((16, VEC, 128), F32),
            pltpu.VMEM((2, 2, 512, 128), BF16),
        ]
        + pair_scratch()
        + [pltpu.SemaphoreType.DMA((2, 2))],
        compiler_params=params(40),
        name="last_modes",
    )(*scalars, coeffs, *kept, legendre, signal, bands)


def exchange(rows):
    return lax.all_to_all(rows, "blk", 0, 0, tiled=True)


def shards(sky_maps, noise_weight, signal_inverse, legendre, m_groups, block_list, band_of_ell):
    blk_index = lax.axis_index("blk")
    set_count, sim_local, cycle_local, cycle_pixels = sky_maps.shape
    block_count = legendre.shape[0]
    outer, outer_t, twist = [jnp.asarray(t) for t in constant_tables()]
    sky = sky_maps.reshape(set_count, sim_local, cycle_local, OUTER, INNER)
    sky = sky.transpose(0, 1, 3, 2, 4).reshape(VEC, OUTER * CYC, INNER)
    noise = noise_weight.reshape(CYC, OUTER, INNER).transpose(1, 0, 2).reshape(OUTER * CYC, INNER)
    half_of = m_groups % 2
    upper_of = m_groups // 2
    earlier = jnp.tril(jnp.ones((SLOTS, SLOTS), jnp.int32), -1)
    rank = jnp.sum(
        (half_of[:, :, None] == half_of[:, None, :]).astype(jnp.int32) * earlier[None], axis=2
    )
    new_slot = 2 * half_of + rank
    chosen = new_slot[:, :, None] == jnp.arange(SLOTS, dtype=jnp.int32)[None, None, :]
    upper = jnp.sum(jnp.where(chosen, upper_of[:, :, None], 0), axis=1)
    upper_rows = upper.T.reshape(2, 2, 1, BLK, 1)
    angle = (2.0 * math.pi / 128.0) * (
        upper_rows * jnp.arange(128, dtype=jnp.int32) % 128
    ).astype(F32)
    cos_inner = math.sqrt(2.0 / NPHI) * jnp.cos(angle)
    sin_inner = math.sqrt(2.0 / NPHI) * jnp.sin(angle)
    inner = jnp.concatenate(
        [
            jnp.concatenate([cos_inner, sin_inner], axis=-1),
            jnp.concatenate([-sin_inner, cos_inner], axis=-1),
        ],
        axis=2,
    ).reshape(2, 128, 256)
    inner = jnp.stack(split(inner))
    zero_rows = jnp.broadcast_to(
        (upper[:, :2].T == 0).astype(F32)[:, None, :], (2, 2, BLK)
    ).reshape(128, 1)
    scalars = (m_groups, block_list, blk_index.astype(jnp.int32).reshape(1))
    signal = signal_inverse.reshape(16, 128)
    bands = band_of_ell.reshape(16, 128)

    rows = row_transforms(sky, noise, outer, outer_t, twist, inner, zero_rows, None)
    products = cycle_products(scalars, legendre, signal)
    kept = []
    for sweep in range(ITERS - 1):
        coeffs, rows = apply_products(exchange(rows), products, kept)
        kept.append(coeffs)
        rows = row_transforms(
            sky, noise, outer, outer_t, twist, inner, zero_rows, exchange(rows)
        )
    state, result = last_step(scalars, exchange(rows), kept, legendre, signal, bands)
    partial = result.reshape(sim_local, 2, BANDS).sum(axis=1)
    devices = BLK * lax.axis_size("sim")
    copies = jnp.broadcast_to(partial[None], (devices, sim_local, BANDS))
    terms = lax.all_to_all(copies, ("blk", "sim"), 0, 0, tiled=True)
    all_proj = jnp.sum(terms.reshape(BLK, -1, BANDS), axis=0)
    band_proj = lax.dynamic_slice_in_dim(all_proj, lax.axis_index("sim") * sim_local, sim_local, 0)
    sim_mean = jnp.mean(all_proj, axis=0)
    center = all_proj - sim_mean[None, :]
    fisher = jnp.dot(center.T, center, precision=PRECISE) / all_proj.shape[0]
    filtered = state.reshape(block_count, MG, set_count, sim_local, 2, 128)
    return (filtered, band_proj, fisher)


def solution(mesh):
    return jax.shard_map(
        shards,
        mesh=mesh,
        in_specs=(
            P(None, "sim", "blk", None),
            P("blk", None),
            P(),
            P("blk", None, None, None),
            P(),
            P("blk", None),
            P(),
        ),
        out_specs=(P("blk", None, None, "sim", None, None), P("sim", None), P()),
        check_vma=False,
    )
```

time: 190 us -> 169 us (0.89)
  blocking collectives: 98.1 us -> 78.4 us
  Pallas kernels: 55.1 us -> 44.9 us
  starting transfers between devices: 8.24 us -> 14.9 us
  waiting for transfers between devices: 7.18 us -> 9.39 us
    all_gather x1 -> x0, blocking collectives: 12.5 us -> none  [shards(): all_proj = lax.all_gather(band_proj, 'sim', axis=0, tiled=True)]
    all_to_all x1 -> x0, blocking collectives: 11 us -> none  [shards(): band_proj = jnp.sum(lax.all_to_all(copies, 'blk', 0, 0, tiled=True), axis=0)]
    pallas_call x8 -> x9, Pallas kernels: 55.1 us -> 44.9 us  [the longest x1 15.4 us: cycle_products(): pl.pallas_call(products_kernel, out_shape=jax.ShapeDtypeStruct((8, 512, 1...]
    all_to_all x0 -> x1, waiting for transfers between devices: none -> 9.38 us  [shards(): terms = lax.all_to_all(copies, ('blk', 'sim'), 0, 0, tiled=True)]
    all_to_all x1, waiting for transfers between devices: 7.18 us -> 0.01 us  [exchange(): return lax.all_to_all(rows, 'blk', 0, 0, tiled=True)]
    all_to_all x0 -> x1, starting transfers between devices: none -> 6.61 us  [shards(): terms = lax.all_to_all(copies, ('blk', 'sim'), 0, 0, tiled=True)]
    all_to_all x6, blocking collectives: 74.7 us -> 78.4 us  [exchange(): return lax.all_to_all(rows, 'blk', 0, 0, tiled=True)]
    unnamed x44 -> x32, local copies, waits for them, and re-layouts: 13.9 us -> 13.9 us
  transfers between devices with their start and end apart: 1 -> 2, of which waited for: 1 -> 1; matrix products, arithmetic and copies ran while one was open for 1% -> 1% of each run, Pallas kernels for 0% -> 9%
where the time goes in v2:
time: 169 us; the launch traced here: 168 us
  blocking collectives  78.4 us (46%)
  Pallas kernels  44.9 us (27%)
  local copies, waits for them, and re-layouts  15.1 us (9%)
  starting transfers between devices  14.9 us (9%)
  waiting for transfers between devices  9.39 us (6%)
  other arithmetic  3.16 us (2%)
    all_to_all x6, blocking collectives, exchange(): return lax.all_to_all(rows, 'blk', 0, 0, tiled=True)  78.4 us
    pallas_call x1, Pallas kernels, cycle_products(): pl.pallas_call(products_kernel, out_shape=jax.ShapeDtypeStruct((8, 512, 1...  15.4 us
    pallas_call x1, Pallas kernels, last_step(): pl.pallas_call(last_kernel, out_shape=(jax.ShapeDtypeStruct((legendre.sha...  15.1 us
    unnamed x32, local copies, waits for them, and re-layouts  13.9 us
    all_to_all x1, waiting for transfers between devices, shards(): terms = lax.all_to_all(copies, ('blk', 'sim'), 0, 0, tiled=True)  9.38 us
    pallas_call x3, Pallas kernels, row_transforms(): pl.pallas_call(rows_kernel, out_shape=SENT, scratch_shapes=scratch, compi...  8.32 us
    all_to_all x1, starting transfers between devices, exchange(): return lax.all_to_all(rows, 'blk', 0, 0, tiled=True)  8.25 us
    all_to_all x1, starting transfers between devices, shards(): terms = lax.all_to_all(copies, ('blk', 'sim'), 0, 0, tiled=True)  6.61 us
  transfers between devices with their start and end apart: 2, of which 1 were waited for; matrix products, arithmetic and copies ran while one was open for 1% of the time, Pallas kernels for 9%

profile of v2, /device:TPU:0, one launch (start us, length us, event | category | flops | bytes accessed | tf_op | source)
XLA Modules:
  0.0 167.6 jit_solution(9438344529479431092)
XLA Ops:
  0.6 0.1 fusion.9
  0.7 0.7 add_select_fusion.2
  1.4 0.1 select_reduce_fusion.1
  1.5 0.7 multiply_add_fusion
  2.2 0.3 sine_multiply_fusion
  2.6 0.1 reshape.185.zero_ref
  2.8 0.0 copy-start.2
  2.8 1.0 copy-done.2
  3.8 0.8 copy-done.4
  4.7 0.8 copy-done.6
  5.5 0.8 copy-done.8
  6.3 2.4 %first_rows.1 = bf16[32,32,128]{2,1,0:T(8,128)(2,1)} custom-call(f32[16,64,128]{2,1,0:T(8,128)S(1)} %bitcast.24, f32[64,128]{1,0:T(8,128)S(1)} %bitcast.28, bf16[2,128,64]{2,1,0:T(8,128)(2,1)S(1)} %copy-done.4, f32[2,64,128]{2,1,0:T(8,128)S(1)} %copy-done.6, bf16[2,2,128,256]{3,2,1,0:T(8,128)(2,1)S(1)} %pad_maximum_fusion.inner_ref, ...), custom_call_target="tpu_custom_call" | custom-call | tf_op jit(solution)/shard_map/first_rows/pallas_call | solution.py:418
  8.6 8.2 %all-to-all-start = ((bf16[32,32,128]{2,1,0:T(8,128)(2,1)}), bf16[32,32,128]{2,1,0:T(8,128)(2,1)S(1)}, u32[]{:S(2)}, u32[]{:S(2)}) async-start(bf16[32,32,128]{2,1,0:T(8,128)(2,1)} %first_rows.1), calls=%async_computation | async-start | bytes 524288 | tf_op jit(solution)/shard_map/all_to_all | solution.py:500
  16.9 0.8 copy.45.group_ref
  17.6 0.8 copy.46.block_ref
  18.4 3.5 %copy-done = bf16[34,16,64,128]{3,2,1,0:T(8,128)(2,1)S(1)} copy-done((bf16[34,16,64,128]{3,2,1,0:T(8,128)(2,1)S(1)}, bf16[34,16,64,128]{3,2,1,0:T(8,128)(2,1)}, u32[]{:S(2)}) %copy-start) | copy-done | bytes 8912920
  22.0 0.7 copy-done.11
  22.7 0.0 copy-start.10
  22.7 15.4 %cycle_products.1.refs_1_ = bf16[8,512,192]{2,1,0:T(8,128)(2,1)S(1)} custom-call(s32[32,4]{1,0:T(8,128)S(1)} %copy.45.group_ref, s32[34,2]{1,0:T(8,128)S(1)} %copy.46.block_ref, s32[1]{0:T(128)} %bitcast.own_ref, bf16[34,16,64,128]{3,2,1,0:T(8,128)(2,1)S(1)} %copy-done, f32[16,128]{1,0:T(8,128)S(1)} %bitcast.32), custom_call_target="tpu_custom_call" | custom-call | tf_op jit(solution)/shard_map/cycle_products/pallas_call | solution.py:446
  38.1 0.0 all-to-all-done.refs_0_
  38.1 1.2 apply_products_1.1
  39.3 16.1 %all_to_all.40.coeff_ref = bf16[32,32,128]{2,1,0:T(8,128)(2,1)S(1)} all-to-all(bf16[32,32,128]{2,1,0:T(8,128)(2,1)S(1)} %get-tuple-element.11), channel_id=1, replica_groups=mesh['blk'=32,'sim'=4] {'blk'}, dimensions={0} | all-to-all | bytes 524288 | tf_op jit(solution)/shard_map/all_to_all | solution.py:500
  55.4 0.0 copy-done.3
  55.4 0.0 copy-done.5
  55.4 2.8 %rows.3 = bf16[32,32,128]{2,1,0:T(8,128)(2,1)S(1)} custom-call(f32[16,64,128]{2,1,0:T(8,128)S(1)} %bitcast.25, f32[64,128]{1,0:T(8,128)S(1)} %bitcast.29, bf16[2,128,64]{2,1,0:T(8,128)(2,1)S(1)} %copy-done.5, bf16[2,64,128]{2,1,0:T(8,128)(2,1)S(1)} %copy-done.10, f32[2,64,128]{2,1,0:T(8,128)S(1)} %copy-done.7, ...), custom_call_target="tpu_custom_call" | custom-call | tf_op jit(solution)/shard_map/rows/pallas_call | solution.py:425
  58.2 12.5 %all_to_all.41.refs_0_ = bf16[32,32,128]{2,1,0:T(8,128)(2,1)S(1)} all-to-all(bf16[32,32,128]{2,1,0:T(8,128)(2,1)S(1)} %rows.3), channel_id=1, replica_groups=mesh['blk'=32,'sim'=4] {'blk'}, dimensions={0} | all-to-all | bytes 524288 | tf_op jit(solution)/shard_map/all_to_all | solution.py:500
  70.7 1.3 apply_products_2.1
  71.9 0.0 copy-start.12
  71.9 0.0 copy-start.13
  71.9 12.5 %all_to_all.42.coeff_ref = bf16[32,32,128]{2,1,0:T(8,128)(2,1)S(1)} all-to-all(bf16[32,32,128]{2,1,0:T(8,128)(2,1)S(1)} %get-tuple-element.13), channel_id=1, replica_groups=mesh['blk'=32,'sim'=4] {'blk'}, dimensions={0} | all-to-all | bytes 524288 | tf_op jit(solution)/shard_map/all_to_all | solution.py:500
  84.4 2.8 %rows.4 = bf16[32,32,128]{2,1,0:T(8,128)(2,1)S(1)} custom-call(f32[16,64,128]{2,1,0:T(8,128)S(1)} %bitcast.26, f32[64,128]{1,0:T(8,128)S(1)} %bitcast.30, bf16[2,128,64]{2,1,0:T(8,128)(2,1)S(1)} %copy-done.5, bf16[2,64,128]{2,1,0:T(8,128)(2,1)S(1)} %copy-done.10, f32[2,64,128]{2,1,0:T(8,128)S(1)} %copy-done.7, ...), custom_call_target="tpu_custom_call" | custom-call | tf_op jit(solution)/shard_map/rows/pallas_call | solution.py:425
  87.2 12.5 %all_to_all.43.refs_0_ = bf16[32,32,128]{2,1,0:T(8,128)(2,1)S(1)} all-to-all(bf16[32,32,128]{2,1,0:T(8,128)(2,1)S(1)} %rows.4), channel_id=1, replica_groups=mesh['blk'=32,'sim'=4] {'blk'}, dimensions={0} | all-to-all | bytes 524288 | tf_op jit(solution)/shard_map/all_to_all | solution.py:500
  99.6 1.3 apply_products_3.1
  101.0 12.5 %all_to_all.44.coeff_ref = bf16[32,32,128]{2,1,0:T(8,128)(2,1)S(1)} all-to-all(bf16[32,32,128]{2,1,0:T(8,128)(2,1)S(1)} %get-tuple-element.15), channel_id=1, replica_groups=mesh['blk'=32,'sim'=4] {'blk'}, dimensions={0} | all-to-all | bytes 524288 | tf_op jit(solution)/shard_map/all_to_all | solution.py:500
  113.4 2.8 %rows.5 = bf16[32,32,128]{2,1,0:T(8,128)(2,1)S(1)} custom-call(f32[16,64,128]{2,1,0:T(8,128)S(1)} %bitcast.27, f32[64,128]{1,0:T(8,128)S(1)} %bitcast.31, bf16[2,128,64]{2,1,0:T(8,128)(2,1)S(1)} %copy-done.5, bf16[2,64,128]{2,1,0:T(8,128)(2,1)S(1)} %copy-done.10, f32[2,64,128]{2,1,0:T(8,128)S(1)} %copy-done.7, ...), custom_call_target="tpu_custom_call" | custom-call | tf_op jit(solution)/shard_map/rows/pallas_call | solution.py:425
  116.2 12.5 %all_to_all.45.coeff_ref = bf16[32,32,128]{2,1,0:T(8,128)(2,1)S(1)} all-to-all(bf16[32,32,128]{2,1,0:T(8,128)(2,1)S(1)} %rows.5), channel_id=1, replica_groups=mesh['blk'=32,'sim'=4] {'blk'}, dimensions={0} | all-to-all | bytes 524288 | tf_op jit(solution)/shard_map/all_to_all | solution.py:500
  128.7 3.5 %copy-done.1 = bf16[34,16,64,128]{3,2,1,0:T(8,128)(2,1)S(1)} copy-done((bf16[34,16,64,128]{3,2,1,0:T(8,128)(2,1)S(1)}, bf16[34,16,64,128]{3,2,1,0:T(8,128)(2,1)}, u32[]{:S(2)}) %copy-start.1) | copy-done | bytes 8912920
  132.2 15.1 %last_modes.1 = (bf16[34,512,128]{2,1,0:T(8,128)(2,1)}, f32[16,32]{1,0:T(8,128)S(1)}) custom-call(s32[32,4]{1,0:T(8,128)S(1)} %copy.45.group_ref, s32[34,2]{1,0:T(8,128)S(1)} %copy.46.block_ref, s32[1]{0:T(128)} %bitcast.own_ref, bf16[32,32,128]{2,1,0:T(8,128)(2,1)S(1)} %all_to_all.45.coeff_ref, ...), custom_call_target="tpu_custom_call" | custom-call | tf_op jit(solution)/shard_map/last_modes/pallas_call | solution.py:476
  147.4 0.9 reshape.186
  148.3 6.6 %all-to-all-start.7 = ((f32[128,1,256]{2,1,0:T(1,128)}), f32[128,1,256]{2,1,0:T(1,128)S(1)}, u32[]{:S(2)}, u32[]{:S(2)}) async-start(f32[128,1,256]{2,1,0:T(1,128)} %reshape.186), calls=%async_computation.7 | async-start | bytes 262144 | tf_op jit(solution)/shard_map/all_to_all | solution.py:554
  154.9 9.4 %all-to-all-done.7 = f32[128,1,256]{2,1,0:T(1,128)S(1)} async-done(((f32[128,1,256]{2,1,0:T(1,128)}), f32[128,1,256]{2,1,0:T(1,128)S(1)}, u32[]{:S(2)}, u32[]{:S(2)}) %all-to-all-start.7) | async-done | bytes 131104 | tf_op jit(solution)/shard_map/all_to_all | solution.py:554
  164.3 0.5 broadcast.232
  164.8 1.0 reduce.2
  165.8 0.2 reshape.187
  165.9 0.2 reduce_sum.49
  166.1 0.1 bitcast_reduce_fusion
  166.2 0.8 convolution_multiply_fusion
  167.0 0.6 constant_dynamic-slice_fusion
  (25 shorter events, 0.2 us)
Async XLA Ops:
  2.8 1.0 copy-start.2
  3.8 0.8 copy-start.4
  4.7 0.8 copy-start.6
  5.5 0.8 copy-start.8
  8.6 29.5 %all-to-all-start = ((bf16[32,32,128]{2,1,0:T(8,128)(2,1)}), bf16[32,32,128]{2,1,0:T(8,128)(2,1)S(1)}, u32[]{:S(2)}, u32[]{:S(2)}) async-start(bf16[32,32,128]{2,1,0:T(8,128)(2,1)} %first_rows.1), calls=%async_computation | async-start | bytes 524288 | tf_op jit(solution)/shard_map/all_to_all | solution.py:500
  18.4 3.5 %copy-start = (bf16[34,16,64,128]{3,2,1,0:T(8,128)(2,1)S(1)}, bf16[34,16,64,128]{3,2,1,0:T(8,128)(2,1)}, u32[]{:S(2)}) copy-start(bf16[34,16,64,128]{3,2,1,0:T(8,128)(2,1)} %legendre_ref.3) | copy-start | bytes 26738692
  21.9 0.7 copy-start.11
  22.6 32.7 %copy-start.3 = (f32[2,8,2,4096]{3,2,1,0:T(2,128)S(1)}, f32[2,8,2,4096]{3,2,1,0:T(2,128)}, u32[]{:S(2)}) copy-start(f32[2,8,2,4096]{3,2,1,0:T(2,128)} %param.10) | copy-start | bytes 1572868
  22.6 32.7 %copy-start.5 = (bf16[2,128,64]{2,1,0:T(8,128)(2,1)S(1)}, bf16[2,128,64]{2,1,0:T(8,128)(2,1)}, u32[]{:S(2)}) copy-start(bf16[2,128,64]{2,1,0:T(8,128)(2,1)} %constant.79.clone.outer_ref) | copy-start | bytes 98308
  22.6 32.7 %copy-start.7 = (f32[2,64,128]{2,1,0:T(8,128)S(1)}, f32[2,64,128]{2,1,0:T(8,128)}, u32[]{:S(2)}) copy-start(f32[2,64,128]{2,1,0:T(8,128)} %constant.81.clone.twist_ref) | copy-start | bytes 196612
  22.7 32.7 %copy-start.9 = (f32[2,4096]{1,0:T(2,128)S(1)}, f32[2,4096]{1,0:T(2,128)}, u32[]{:S(2)}) copy-start(f32[2,4096]{1,0:T(2,128)} %param.11) | copy-start | bytes 98308
  22.7 32.7 %copy-start.10 = (bf16[2,64,128]{2,1,0:T(8,128)(2,1)S(1)}, bf16[2,64,128]{2,1,0:T(8,128)(2,1)}, u32[]{:S(2)}) copy-start(bf16[2,64,128]{2,1,0:T(8,128)(2,1)} %constant.80.clone.outer_t_ref) | copy-start | bytes 98308
  71.9 56.8 %copy-start.12 = (f32[2048]{0:T(1024)S(1)}, f32[2048]{0:T(1024)}, u32[]{:S(2)}) copy-start(f32[2048]{0:T(1024)} %param.12) | copy-start | bytes 24580
  71.9 56.7 %copy-start.13 = (s32[2048]{0:T(1024)S(1)}, s32[2048]{0:T(1024)}, u32[]{:S(2)}) copy-start(s32[2048]{0:T(1024)} %param.16) | copy-start | bytes 24580
  128.7 3.5 %copy-start.1 = (bf16[34,16,64,128]{3,2,1,0:T(8,128)(2,1)S(1)}, bf16[34,16,64,128]{3,2,1,0:T(8,128)(2,1)}, u32[]{:S(2)}) copy-start(bf16[34,16,64,128]{3,2,1,0:T(8,128)(2,1)} %legendre_ref.3) | copy-start | bytes 26738692
  148.3 16.0 %all-to-all-start.7 = ((f32[128,1,256]{2,1,0:T(1,128)}), f32[128,1,256]{2,1,0:T(1,128)S(1)}, u32[]{:S(2)}, u32[]{:S(2)}) async-start(f32[128,1,256]{2,1,0:T(1,128)} %reshape.186), calls=%async_computation.7 | async-start | bytes 262144 | tf_op jit(solution)/shard_map/all_to_all | solution.py:554

commit v3 on v2

--- a/solution.py
+++ b/solution.py
@@ -19,6 +19,8 @@
 MG = 16
 SLOTS = 4
 PAIRS = 18
+PAIR_GROUP = 3
+GROUP = 6
 F32 = jnp.float32
 BF16 = jnp.bfloat16
 PRECISE = lax.Precision.HIGHEST
@@ -167,24 +169,49 @@
     )
 
 
-def find_pairs(group_ref, block_ref, own_ref, order, pair_slot, pair_live, pair_zero, counter):
+def own_slots(group_ref, own_ref):
     own = own_ref[0]
-    groups = [group_ref[own, s] for s in range(SLOTS)]
-    base = jnp.int32(0)
+    groups = [group_ref[s, own] for s in range(SLOTS)]
+    slots = []
     for s in range(SLOTS):
         half = groups[s] % 2
         rank = jnp.int32(0)
         for earlier in range(s):
             rank = rank + jnp.where(groups[earlier] % 2 == half, 1, 0)
-        slot = 2 * half + rank
-        is_zero = jnp.where(groups[s] == 0, 1, 0)
-        count = 16 - groups[s] // 8
+        slots.append((2 * half + rank, groups[s]))
+    return slots
+
+
+def table_copy(legendre_ref, table, arrived, group, size):
+    blocks = pl.ds(group * GROUP, size)
+    return pltpu.make_async_copy(legendre_ref.at[blocks], table.at[blocks], arrived.at[group])
+
+
+def by_groups(blocks, step):
+    def body(group, carry):
+        step(group, GROUP)
+        return carry
+
+    lax.fori_loop(0, blocks // GROUP, body, 0)
+    if blocks % GROUP:
+        step(blocks // GROUP, blocks % GROUP)
+
+
+def mark_slots(group_ref, own_ref, new_slot, zero_slot):
+    for s, (slot, group) in enumerate(own_slots(group_ref, own_ref)):
+        new_slot[s] = slot
+        zero_slot[s] = jnp.where(group == 0, 1, 0)
+
+
+def find_pairs(group_ref, block_ref, own_ref, order, pair_slot, pair_live, counter):
+    base = jnp.int32(0)
+    for s, (slot, group) in enumerate(own_slots(group_ref, own_ref)):
+        count = 16 - group // 8
         pairs = (count + 1) // 2
         counter[s] = 2 * base
 
-        def mark(pair, carry, slot=slot, is_zero=is_zero):
+        def mark(pair, carry, slot=slot):
             pair_slot[pair] = slot
-            pair_zero[pair] = is_zero
             pair_live[pair] = 1
             return carry
 
@@ -192,13 +219,13 @@
         base = base + pairs
 
     def place(block, carry):
-        slot = block_ref[block, 0]
+        slot = block_ref[0, block]
         at = counter[slot]
         order[at] = block
         counter[slot] = at + 1
         return carry
 
-    lax.fori_loop(0, 34, place, 0)
+    lax.fori_loop(0, block_ref.shape[1], place, 0)
     for s in range(SLOTS):
         at = counter[s]
 
@@ -208,68 +235,56 @@
             pair_live[at // 2] = 0
 
 
-def block_copy(legendre_ref, table, arrived, order, at):
-    block = order[at]
-    return pltpu.make_async_copy(legendre_ref.at[block], table.at[block], arrived.at[at])
-
-
-def start_blocks(legendre_ref, table, arrived, order, pair_live):
-    def start(pair, carry):
-        block_copy(legendre_ref, table, arrived, order, 2 * pair).start()
-
-        @pl.when(pair_live[pair] == 1)
-        def _():
-            block_copy(legendre_ref, table, arrived, order, 2 * pair + 1).start()
-
+def products_kernel(
+    power, group_ref, block_ref, own_ref, legendre_ref, signal_ref, out_ref,
+    table, sums, order, pair_slot, pair_live, counter, arrived,
+):
+    find_pairs(group_ref, block_ref, own_ref, order, pair_slot, pair_live, counter)
+
+    def place_copy(at):
+        return pltpu.make_async_copy(legendre_ref.at[order[at]], table.at[at], arrived.at[at])
+
+    def fetch(at, carry):
+        place_copy(at).start()
         return carry
 
-    lax.fori_loop(0, PAIRS, start, 0)
-
-
-def wait_blocks(legendre_ref, table, arrived, order, pair_live, pair):
-    block_copy(legendre_ref, table, arrived, order, 2 * pair).wait()
-
-    @pl.when(pair_live[pair] == 1)
-    def _():
-        block_copy(legendre_ref, table, arrived, order, 2 * pair + 1).wait()
-
-
-def products_kernel(
-    group_ref, block_ref, own_ref, legendre_ref, signal_ref, out_ref,
-    table, sums, order, pair_slot, pair_live, pair_zero, counter, arrived,
-):
-    find_pairs(group_ref, block_ref, own_ref, order, pair_slot, pair_live, pair_zero, counter)
-    start_blocks(legendre_ref, table, arrived, order, pair_live)
+    lax.fori_loop(0, 2 * PAIRS, fetch, 0)
     sums[...] = jnp.zeros_like(sums)
 
-    def pair_step(pair, carry):
-        wait_blocks(legendre_ref, table, arrived, order, pair_live, pair)
-        first, second = order[2 * pair], order[2 * pair + 1]
-        live = pair_live[pair].astype(F32)
-        precond_first = 1.0 / (2.0 + signal_ref[pl.ds(block_ref[first, 1], 1), :])
-        precond_second = 1.0 / (2.0 + signal_ref[pl.ds(block_ref[second, 1], 1), :])
-        precond = jnp.concatenate([precond_first, precond_second], axis=1)
-        weight = jnp.concatenate([precond_first, precond_second * live], axis=1)
-        weights = []
-        for _ in range(ITERS - 1):
-            weights.append(jnp.broadcast_to(weight, (64, 256)))
-            weight = weight * (2.0 * precond)
-        for i in range(MG):
-            values = jnp.concatenate([table[first, i], table[second, i]], axis=1)
-            wide = values.astype(F32)
-            scaled = jnp.concatenate([(wide * w).astype(BF16) for w in weights], axis=0)
-            sums[pair_slot[pair] * MG + i] += dot(values, scaled, NT)
+    def pair_step(group, carry):
+        pairs = [group * PAIR_GROUP + n for n in range(PAIR_GROUP)]
+        for pair in pairs:
+            place_copy(2 * pair).wait()
+            place_copy(2 * pair + 1).wait()
+        slots = [pair_slot[pair] for pair in pairs]
+        lives = [pair_live[pair].astype(F32) for pair in pairs]
+        degrees = [
+            (block_ref[1, order[2 * pair]], block_ref[1, order[2 * pair + 1]]) for pair in pairs
+        ]
+        for pair, slot, live, (first, second) in zip(pairs, slots, lives, degrees):
+            precond = [1.0 / (2.0 + signal_ref[pl.ds(degree, 1), :]) for degree in (first, second)]
+            precond = jnp.concatenate(precond, axis=1)
+            lane = lax.broadcasted_iota(jnp.int32, (1, 256), 1)
+            weight = precond * jnp.where(lane < 128, 1.0, live)
+            for _ in range(power):
+                weight = weight * (2.0 * precond)
+            weight = jnp.broadcast_to(weight, (64, 256))
+            for i in range(MG):
+                values = jnp.concatenate([table[2 * pair, i], table[2 * pair + 1, i]], axis=1)
+                scaled = (values.astype(F32) * weight).astype(BF16)
+                sums[slot * MG + i] += dot(values, scaled, NT)
         return carry
 
-    lax.fori_loop(0, PAIRS, pair_step, 0)
+    lax.fori_loop(0, PAIRS // PAIR_GROUP, pair_step, 0)
     for at in range(SLOTS * MG):
         out_ref[at // 8, (at % 8) * 64 : (at % 8 + 1) * 64, :] = sums[at].astype(BF16)
 
 
 def apply_kernel(count, *refs):
-    coeff_ref, product_ref = refs[:2]
-    earlier = refs[2 : 1 + count]
-    kept_ref, out_ref, staged, ordered = refs[1 + count :]
+    coeff_ref = refs[0]
+    product_refs = refs[1 : 1 + count]
+    earlier = refs[1 + count : 2 * count]
+    kept_ref, out_ref, staged, ordered = refs[2 * count :]
     staged[...] = coeff_ref[...].astype(F32)
     for c in range(16):
         for cycle in range(CYC):
@@ -280,10 +295,11 @@
     for slot in range(SLOTS):
         for upper in range(2):
             at = [(slot * 2 + p) * 2 + upper for p in range(2)]
-            right = jnp.concatenate(
-                [jnp.concatenate([ref[at[0]], ref[at[1]]], axis=1) for ref in history], axis=0
-            )
-            mixed = dot(product_ref[slot * 2 + upper, :, : 64 * count], right)
+            mixed = None
+            for product_ref, ref in zip(product_refs, history):
+                right = jnp.concatenate([ref[at[0]], ref[at[1]]], axis=1)
+                term = dot(product_ref[slot * 2 + upper], right)
+                mixed = term if mixed is None else mixed + term
             result = mixed[:64]
             for i in range(1, 8):
                 result = jnp.where(lane == i, mixed[i * 64 : (i + 1) * 64], result)
@@ -298,11 +314,12 @@
 def last_kernel(
     group_ref, block_ref, own_ref, coeff_ref, kept0_ref, kept1_ref, kept2_ref, legendre_ref,
     signal_ref, band_ref, state_ref, band_out,
-    table, staged, mixed, packed, products, outgoing,
-    order, pair_slot, pair_live, pair_zero, counter, arrived, sent,
+    table, staged, mixed, packed, products, outgoing, new_slot, zero_slot, arrived, sent,
 ):
-    find_pairs(group_ref, block_ref, own_ref, order, pair_slot, pair_live, pair_zero, counter)
-    start_blocks(legendre_ref, table, arrived, order, pair_live)
+    blocks = legendre_ref.shape[0]
+
+    by_groups(blocks, lambda g, n: table_copy(legendre_ref, table, arrived, g, n).start())
+    mark_slots(group_ref, own_ref, new_slot, zero_slot)
     products[...] = jnp.zeros_like(products)
     staged[...] = coeff_ref[...].astype(F32)
     blank = jnp.zeros((64, 128), BF16)
@@ -328,61 +345,37 @@
             for i in range(8):
                 packed[slot * MG + upper * 8 + i] = mixed[1 + i, :, 0:64].astype(BF16)
 
-    def out_copy(pair, which):
-        slot = pair % 2
-        return pltpu.make_async_copy(
-            outgoing.at[slot, which],
-            state_ref.at[order[2 * pair + which]],
-            sent.at[slot, which],
-        )
-
-    def wait_out(pair):
-        out_copy(pair, 0).wait()
-
-        @pl.when(pair_live[pair] == 1)
-        def _():
-            out_copy(pair, 1).wait()
-
-    def pair_step(pair, carry):
-        wait_blocks(legendre_ref, table, arrived, order, pair_live, pair)
-
-        @pl.when(pair >= 2)
-        def _():
-            wait_out(pair - 2)
-
-        first, second = order[2 * pair], order[2 * pair + 1]
-        degrees = (block_ref[first, 1], block_ref[second, 1])
-        precond = jnp.concatenate(
-            [1.0 / (2.0 + signal_ref[pl.ds(degree, 1), :]) for degree in degrees], axis=1
-        )
-        damp = 2.0 * precond
-        total = jnp.zeros((VEC, 256), F32)
-        for i in range(MG):
-            values = jnp.concatenate([table[first, i], table[second, i]], axis=1)
-            harmonic = dot(packed[pair_slot[pair] * MG + i], values)
-            state = harmonic[0:32]
-            for sweep in range(1, ITERS):
-                state = harmonic[sweep * 32 : (sweep + 1) * 32] + damp * state
-            state = precond * state
-            rounded = state.astype(BF16)
-            outgoing[pair % 2, 0, i * 32 : (i + 1) * 32, :] = rounded[:, :128]
-            outgoing[pair % 2, 1, i * 32 : (i + 1) * 32, :] = rounded[:, 128:]
-            one = state[:VEC] * state[VEC:]
-            if i == 0:
-                one = one * jnp.where(pair_zero[pair] > 0, 0.5, 1.0)
-            total = total + one
-        total = 2.0 * total
-        products[degrees[0]] += total[:, :128]
-        out_copy(pair, 0).start()
-
-        @pl.when(pair_live[pair] == 1)
-        def _():
-            products[degrees[1]] += total[:, 128:]
-            out_copy(pair, 1).start()
-
-        return carry
-
-    lax.fori_loop(0, PAIRS, pair_step, 0)
+    def out_copy(group, size):
+        some = pl.ds(group * GROUP, size)
+        return pltpu.make_async_copy(outgoing.at[some], state_ref.at[some], sent.at[group])
+
+    def step(group, size):
+        table_copy(legendre_ref, table, arrived, group, size).wait()
+        some = [group * GROUP + n for n in range(size)]
+        slots = [new_slot[block_ref[0, block]] for block in some]
+        halves = [
+            jnp.where(zero_slot[block_ref[0, block]] > 0, 0.5, 1.0) for block in some
+        ]
+        degrees = [block_ref[1, block] for block in some]
+        for block, slot, half, degree in zip(some, slots, halves, degrees):
+            precond = jnp.broadcast_to(1.0 / (2.0 + signal_ref[pl.ds(degree, 1), :]), (32, 128))
+            damp = 2.0 * precond
+            total = jnp.zeros((VEC, 128), F32)
+            for i in range(MG):
+                harmonic = dot(packed[slot * MG + i], table[block, i])
+                state = harmonic[0:32]
+                for sweep in range(1, ITERS):
+                    state = harmonic[sweep * 32 : (sweep + 1) * 32] + damp * state
+                state = precond * state
+                outgoing[block, i * 32 : (i + 1) * 32, :] = state.astype(BF16)
+                one = state[:VEC] * state[VEC:]
+                if i == 0:
+                    one = one * half
+                total = total + one
+            products[degree] += 2.0 * total
+        out_copy(group, size).start()
+
+    by_groups(blocks, step)
     raw = jnp.zeros((VEC, BANDS), F32)
     counts = jnp.zeros((VEC, BANDS), F32)
     bins = lax.broadcasted_iota(jnp.int32, (BANDS, 128), 0)
@@ -397,8 +390,8 @@
             weight, member, NT, precision=PRECISE, preferred_element_type=F32
         )
     band_out[...] = raw * (1.0 / jnp.sqrt(counts))
-    wait_out(PAIRS - 2)
-    wait_out(PAIRS - 1)
+
+    by_groups(blocks, lambda g, n: out_copy(g, n).wait())
 
 
 def params(megabytes, **more):
@@ -431,34 +424,30 @@
     )(sky, noise, outer, outer_t, twist, inner, zero_rows, coeffs)
 
 
-def pair_scratch():
-    return [
-        pltpu.SMEM((2 * PAIRS,), jnp.int32),
-        pltpu.SMEM((PAIRS,), jnp.int32),
-        pltpu.SMEM((PAIRS,), jnp.int32),
-        pltpu.SMEM((PAIRS,), jnp.int32),
-        pltpu.SMEM((SLOTS,), jnp.int32),
-        pltpu.SemaphoreType.DMA((2 * PAIRS,)),
-    ]
-
-
-def cycle_products(scalars, legendre, signal):
+def cycle_products(power, scalars, legendre, signal):
+    def body(*refs):
+        products_kernel(power, *refs)
+
     return pl.pallas_call(
-        products_kernel,
-        out_shape=jax.ShapeDtypeStruct((8, 512, 192), BF16),
+        body,
+        out_shape=jax.ShapeDtypeStruct((8, 512, 64), BF16),
         in_specs=[SMEM, SMEM, SMEM, ANY, VMEM],
         scratch_shapes=[
-            pltpu.VMEM(legendre.shape, BF16),
-            pltpu.VMEM((SLOTS * MG, 64, 192), F32),
-        ]
-        + pair_scratch(),
-        compiler_params=params(40),
-        name="cycle_products",
+            pltpu.VMEM((2 * PAIRS,) + legendre.shape[1:], BF16),
+            pltpu.VMEM((SLOTS * MG, 64, 64), F32),
+            pltpu.SMEM((2 * PAIRS,), jnp.int32),
+            pltpu.SMEM((PAIRS,), jnp.int32),
+            pltpu.SMEM((PAIRS,), jnp.int32),
+            pltpu.SMEM((SLOTS,), jnp.int32),
+            pltpu.SemaphoreType.DMA((2 * PAIRS,)),
+        ],
+        compiler_params=params(52),
+        name="cycle_products_" + str(power),
     )(*scalars, legendre, signal)
 
 
 def apply_products(coeffs, products, kept):
-    count = len(kept) + 1
+    count = len(products)
 
     def body(*refs):
         apply_kernel(count, *refs)
@@ -469,7 +458,7 @@
         scratch_shapes=[pltpu.VMEM((BLK, 32, 128), F32), pltpu.VMEM((16, 64, 128), F32)],
         compiler_params=params(32),
         name="apply_products_" + str(count),
-    )(coeffs, products, *kept)
+    )(coeffs, *products, *kept)
 
 
 def last_step(scalars, coeffs, kept, legendre, signal, bands):
@@ -487,11 +476,15 @@
             pltpu.VMEM((9, 128, 128), F32),
             pltpu.VMEM((SLOTS * MG, 128, 64), BF16),
             pltpu.VMEM((16, VEC, 128), F32),
-            pltpu.VMEM((2, 2, 512, 128), BF16),
+            pltpu.VMEM((legendre.shape[0], 512, 128), BF16),
         ]
-        + pair_scratch()
-        + [pltpu.SemaphoreType.DMA((2, 2))],
-        compiler_params=params(40),
+        + [
+            pltpu.SMEM((SLOTS,), jnp.int32),
+            pltpu.SMEM((SLOTS,), jnp.int32),
+            pltpu.SemaphoreType.DMA((-(-legendre.shape[0] // GROUP),)),
+            pltpu.SemaphoreType.DMA((-(-legendre.shape[0] // GROUP),)),
+        ],
+        compiler_params=params(52),
         name="last_modes",
     )(*scalars, coeffs, *kept, legendre, signal, bands)
 
@@ -534,14 +527,16 @@
     zero_rows = jnp.broadcast_to(
         (upper[:, :2].T == 0).astype(F32)[:, None, :], (2, 2, BLK)
     ).reshape(128, 1)
-    scalars = (m_groups, block_list, blk_index.astype(jnp.int32).reshape(1))
+    scalars = (m_groups.T, block_list.T, blk_index.astype(jnp.int32).reshape(1))
     signal = signal_inverse.reshape(16, 128)
     bands = band_of_ell.reshape(16, 128)
 
     rows = row_transforms(sky, noise, outer, outer_t, twist, inner, zero_rows, None)
-    products = cycle_products(scalars, legendre, signal)
     kept = []
+    products = []
     for sweep in range(ITERS - 1):
+        own, rows = lax.optimization_barrier((scalars[2], rows))
+        products.append(cycle_products(sweep, scalars[:2] + (own,), legendre, signal))
         coeffs, rows = apply_products(exchange(rows), products, kept)
         kept.append(coeffs)
         rows = row_transforms(

time: 169 us -> 164 us (0.970)
  blocking collectives: 78.4 us -> 58.1 us
  starting transfers between devices: 14.9 us -> 24.2 us
  Pallas kernels: 44.9 us -> 48.5 us
  waiting for transfers between devices: 9.39 us -> 12 us
  local copies, waits for them, and re-layouts: 15.1 us -> 13.4 us
    all_to_all x6 -> x4, blocking collectives: 78.4 us -> 58.1 us  [exchange(): return lax.all_to_all(rows, 'blk', 0, 0, tiled=True)]
    all_to_all x1 -> x3, starting transfers between devices: 8.25 us -> 17.6 us  [exchange(): return lax.all_to_all(rows, 'blk', 0, 0, tiled=True)]
    pallas_call x1, Pallas kernels: 15.1 us -> 8.55 us  [last_step(): pl.pallas_call(last_kernel, out_shape=(jax.ShapeDtypeStruct((legendre.sha...]
    pallas_call x1 -> x3, Pallas kernels: 15.4 us -> 21.4 us  [cycle_products(): pl.pallas_call(body, out_shape=jax.ShapeDtypeStruct((8, 512, 64), BF16),...]
    pallas_call x3, Pallas kernels: 3.75 us -> 7.17 us  [apply_products(): pl.pallas_call(body, out_shape=(KEPT, SENT), scratch_shapes=[pltpu.VMEM((...]
    all_to_all x1 -> x3, waiting for transfers between devices: 0.01 us -> 2.57 us  [exchange(): return lax.all_to_all(rows, 'blk', 0, 0, tiled=True)]
    unnamed x32 -> x46, local copies, waits for them, and re-layouts: 13.9 us -> 12.1 us
  transfers between devices with their start and end apart: 2 -> 4, of which waited for: 1 -> 3; matrix products, arithmetic and copies ran while one was open for 1% -> 0% of each run, Pallas kernels for 9% -> 13%
where the time goes in v3:
time: 164 us; the launch traced here: 161 us
  blocking collectives  58.1 us (35%)
  Pallas kernels  48.5 us (30%)
  starting transfers between devices  24.2 us (15%)
  local copies, waits for them, and re-layouts  13.4 us (8%)
  waiting for transfers between devices  12 us (7%)
  other arithmetic  3.25 us (2%)
    all_to_all x4, blocking collectives, exchange(): return lax.all_to_all(rows, 'blk', 0, 0, tiled=True)  58.1 us
    pallas_call x3, Pallas kernels, cycle_products(): pl.pallas_call(body, out_shape=jax.ShapeDtypeStruct((8, 512, 64), BF16),...  21.4 us
    all_to_all x3, starting transfers between devices, exchange(): return lax.all_to_all(rows, 'blk', 0, 0, tiled=True)  17.6 us
    unnamed x46, local copies, waits for them, and re-layouts  12.1 us
    all_to_all x1, waiting for transfers between devices, shards(): terms = lax.all_to_all(copies, ('blk', 'sim'), 0, 0, tiled=True)  9.39 us
    pallas_call x3, Pallas kernels, row_transforms(): pl.pallas_call(rows_kernel, out_shape=SENT, scratch_shapes=scratch, compi...  9.02 us
    pallas_call x1, Pallas kernels, last_step(): pl.pallas_call(last_kernel, out_shape=(jax.ShapeDtypeStruct((legendre.sha...  8.55 us
    pallas_call x3, Pallas kernels, apply_products(): pl.pallas_call(body, out_shape=(KEPT, SENT), scratch_shapes=[pltpu.VMEM((...  7.17 us
  transfers between devices with their start and end apart: 4, of which 3 were waited for; matrix products, arithmetic and copies ran while one was open for 0% of the time, Pallas kernels for 13%

profile of v3, /device:TPU:0, one launch (start us, length us, event | category | flops | bytes accessed | tf_op | source)
XLA Modules:
  0.0 161.2 jit_solution(11268798749904354279)
XLA Ops:
  0.7 0.1 fusion.9
  0.8 0.8 add_select_fusion.2
  1.6 0.1 select_reduce_fusion.1
  1.7 0.7 multiply_add_fusion
  2.4 0.3 sine_multiply_fusion
  2.8 0.1 reshape.185.zero_ref
  3.0 1.0 copy-done
  4.0 0.8 copy-done.4
  4.9 0.8 copy-done.6
  5.7 0.8 copy-done.12
  6.5 2.4 %first_rows.1 = bf16[32,32,128]{2,1,0:T(8,128)(2,1)} custom-call(f32[16,64,128]{2,1,0:T(8,128)S(1)} %bitcast.26, f32[64,128]{1,0:T(8,128)S(1)} %bitcast.30, bf16[2,128,64]{2,1,0:T(8,128)(2,1)S(1)} %copy-done.4, f32[2,64,128]{2,1,0:T(8,128)S(1)} %copy-done.6, bf16[2,2,128,256]{3,2,1,0:T(8,128)(2,1)S(1)} %pad_maximum_fusion.inner_ref, ...), custom_call_target="tpu_custom_call" | custom-call | tf_op jit(solution)/shard_map/first_rows/pallas_call | solution.py:411
  8.8 8.2 %all-to-all-start = ((bf16[32,32,128]{2,1,0:T(8,128)(2,1)}), bf16[32,32,128]{2,1,0:T(8,128)(2,1)S(1)}, u32[]{:S(2)}, u32[]{:S(2)}) async-start(bf16[32,32,128]{2,1,0:T(8,128)(2,1)} %first_rows.1), calls=%async_computation | async-start | bytes 524288 | tf_op jit(solution)/shard_map/all_to_all | solution.py:493
  17.1 0.7 copy-done.15
  17.8 0.7 copy-done.17
  18.4 0.7 copy-done.19
  19.1 7.1 %cycle_products_0.1.refs_1_ = bf16[8,512,64]{2,1,0:T(8,128)(2,1)S(1)} custom-call(s32[4,32]{1,0:T(4,128)S(1)} %bitcast.38, s32[2,34]{1,0:T(2,128)S(1)} %bitcast.42, s32[1]{0:T(128)} %bitcast.2.refs_2_.own_ref, bf16[34,16,64,128]{3,2,1,0:T(8,128)(2,1)} %legendre_ref.1, f32[16,128]{1,0:T(8,128)S(1)} %bitcast.34), custom_call_target="tpu_custom_call" | custom-call | tf_op jit(solution)/shard_map/cycle_products_0/pallas_call | solution.py:431
  26.3 1.2 apply_products_1.1
  27.5 16.1 %all_to_all.40.coeff_ref = bf16[32,32,128]{2,1,0:T(8,128)(2,1)S(1)} all-to-all(bf16[32,32,128]{2,1,0:T(8,128)(2,1)S(1)} %get-tuple-element.19), channel_id=1, replica_groups=mesh['blk'=32,'sim'=4] {'blk'}, dimensions={0} | all-to-all | bytes 524288 | tf_op jit(solution)/shard_map/all_to_all | solution.py:493
  43.6 3.5 %rows.3 = bf16[32,32,128]{2,1,0:T(8,128)(2,1)} custom-call(f32[16,64,128]{2,1,0:T(8,128)S(1)} %bitcast.27, f32[64,128]{1,0:T(8,128)S(1)} %bitcast.31, bf16[2,128,64]{2,1,0:T(8,128)(2,1)S(1)} %copy-done.5, bf16[2,64,128]{2,1,0:T(8,128)(2,1)S(1)} %copy-done.14, f32[2,64,128]{2,1,0:T(8,128)S(1)} %copy-done.7, ...), custom_call_target="tpu_custom_call" | custom-call | tf_op jit(solution)/shard_map/rows/pallas_call | solution.py:418
  47.1 4.6 %all-to-all-start.2 = ((bf16[32,32,128]{2,1,0:T(8,128)(2,1)}), bf16[32,32,128]{2,1,0:T(8,128)(2,1)}, u32[]{:S(2)}, u32[]{:S(2)}) async-start(bf16[32,32,128]{2,1,0:T(8,128)(2,1)} %rows.3), calls=%async_computation.2 | async-start | bytes 524288 | tf_op jit(solution)/shard_map/all_to_all | solution.py:493
  51.7 7.1 %cycle_products_1.1.refs_2_ = bf16[8,512,64]{2,1,0:T(8,128)(2,1)S(1)} custom-call(s32[4,32]{1,0:T(4,128)S(1)} %bitcast.39, s32[2,34]{1,0:T(2,128)S(1)} %bitcast.43, s32[1]{0:T(128)} %bitcast.2.refs_2_.own_ref, bf16[34,16,64,128]{3,2,1,0:T(8,128)(2,1)} %legendre_ref.1, f32[16,128]{1,0:T(8,128)S(1)} %bitcast.35), custom_call_target="tpu_custom_call" | custom-call | tf_op jit(solution)/shard_map/cycle_products_1/pallas_call | solution.py:431
  58.8 1.8 %all-to-all-done.2.refs_0_ = bf16[32,32,128]{2,1,0:T(8,128)(2,1)} async-done(((bf16[32,32,128]{2,1,0:T(8,128)(2,1)}), bf16[32,32,128]{2,1,0:T(8,128)(2,1)}, u32[]{:S(2)}, u32[]{:S(2)}) %all-to-all-start.2) | async-done | bytes 262176 | tf_op jit(solution)/shard_map/all_to_all | solution.py:493
  60.6 2.7 %apply_products_2.1 = (bf16[16,64,128]{2,1,0:T(8,128)(2,1)S(1)}, bf16[32,32,128]{2,1,0:T(8,128)(2,1)S(1)}) custom-call(bf16[32,32,128]{2,1,0:T(8,128)(2,1)} %all-to-all-done.2.refs_0_, bf16[8,512,64]{2,1,0:T(8,128)(2,1)S(1)} %cycle_products_0.1.refs_1_, bf16[8,512,64]{2,1,0:T(8,128)(2,1)S(1)} %cycle_products_1.1.refs_2_, ...), custom_call_target="tpu_custom_call" | custom-call | tf_op jit(solution)/shard_map/apply_products_2/pallas_call | solution.py:455
  63.3 0.7 copy-done.9
  64.0 14.3 %all_to_all.41.coeff_ref = bf16[32,32,128]{2,1,0:T(8,128)(2,1)S(1)} all-to-all(bf16[32,32,128]{2,1,0:T(8,128)(2,1)S(1)} %get-tuple-element.23), channel_id=1, replica_groups=mesh['blk'=32,'sim'=4] {'blk'}, dimensions={0} | all-to-all | bytes 524288 | tf_op jit(solution)/shard_map/all_to_all | solution.py:493
  78.3 2.8 %rows.4 = bf16[32,32,128]{2,1,0:T(8,128)(2,1)S(1)} custom-call(f32[16,64,128]{2,1,0:T(8,128)S(1)} %bitcast.28, f32[64,128]{1,0:T(8,128)S(1)} %bitcast.32, bf16[2,128,64]{2,1,0:T(8,128)(2,1)S(1)} %copy-done.5, bf16[2,64,128]{2,1,0:T(8,128)(2,1)S(1)} %copy-done.14, f32[2,64,128]{2,1,0:T(8,128)S(1)} %copy-done.7, ...), custom_call_target="tpu_custom_call" | custom-call | tf_op jit(solution)/shard_map/rows/pallas_call | solution.py:418
  81.1 0.7 copy-done.8
  81.8 4.7 %all-to-all-start.4 = ((bf16[32,32,128]{2,1,0:T(8,128)(2,1)}), bf16[32,32,128]{2,1,0:T(8,128)(2,1)}, u32[]{:S(2)}, u32[]{:S(2)}) async-start(bf16[32,32,128]{2,1,0:T(8,128)(2,1)} %copy-done.8), calls=%async_computation.4 | async-start | bytes 524288 | tf_op jit(solution)/shard_map/all_to_all | solution.py:493
  86.5 7.1 %cycle_products_2.1.refs_3_ = bf16[8,512,64]{2,1,0:T(8,128)(2,1)S(1)} custom-call(s32[4,32]{1,0:T(4,128)S(1)} %bitcast.40, s32[2,34]{1,0:T(2,128)S(1)} %bitcast.44, s32[1]{0:T(128)} %bitcast.2.refs_2_.own_ref, bf16[34,16,64,128]{3,2,1,0:T(8,128)(2,1)} %legendre_ref.1, f32[16,128]{1,0:T(8,128)S(1)} %bitcast.36), custom_call_target="tpu_custom_call" | custom-call | tf_op jit(solution)/shard_map/cycle_products_2/pallas_call | solution.py:431
  93.7 1.0 copy-done.2
  94.6 0.8 all-to-all-done.4.refs_0_
  95.4 1.2 copy-done.3
  96.7 0.9 copy-done.10
  97.6 3.3 %apply_products_3.1 = (bf16[16,64,128]{2,1,0:T(8,128)(2,1)S(1)}, bf16[32,32,128]{2,1,0:T(8,128)(2,1)S(1)}) custom-call(bf16[32,32,128]{2,1,0:T(8,128)(2,1)} %all-to-all-done.4.refs_0_, bf16[8,512,64]{2,1,0:T(8,128)(2,1)S(1)} %cycle_products_0.1.refs_1_, bf16[8,512,64]{2,1,0:T(8,128)(2,1)S(1)} %cycle_products_1.1.refs_2_, bf16[8,512,64]{2,1,0:T(8,128)(2,1)S(1)} %copy-done.3, ...), custom_call_target="tpu_custom_call" | custom-call | tf_op jit(solution)/shard_map/apply_products_3/pallas_call | solution.py:455
  100.9 15.3 %all_to_all.42.coeff_ref = bf16[32,32,128]{2,1,0:T(8,128)(2,1)S(1)} all-to-all(bf16[32,32,128]{2,1,0:T(8,128)(2,1)S(1)} %get-tuple-element.27), channel_id=1, replica_groups=mesh['blk'=32,'sim'=4] {'blk'}, dimensions={0} | all-to-all | bytes 524288 | tf_op jit(solution)/shard_map/all_to_all | solution.py:493
  116.1 2.8 %rows.5 = bf16[32,32,128]{2,1,0:T(8,128)(2,1)S(1)} custom-call(f32[16,64,128]{2,1,0:T(8,128)S(1)} %bitcast.29, f32[64,128]{1,0:T(8,128)S(1)} %bitcast.33, bf16[2,128,64]{2,1,0:T(8,128)(2,1)S(1)} %copy-done.5, bf16[2,64,128]{2,1,0:T(8,128)(2,1)S(1)} %copy-done.14, f32[2,64,128]{2,1,0:T(8,128)S(1)} %copy-done.7, ...), custom_call_target="tpu_custom_call" | custom-call | tf_op jit(solution)/shard_map/rows/pallas_call | solution.py:418
  118.9 12.5 %all_to_all.43.coeff_ref = bf16[32,32,128]{2,1,0:T(8,128)(2,1)S(1)} all-to-all(bf16[32,32,128]{2,1,0:T(8,128)(2,1)S(1)} %rows.5), channel_id=1, replica_groups=mesh['blk'=32,'sim'=4] {'blk'}, dimensions={0} | all-to-all | bytes 524288 | tf_op jit(solution)/shard_map/all_to_all | solution.py:493
  131.4 0.9 copy-done.11
  132.3 8.5 %last_modes.1 = (bf16[34,512,128]{2,1,0:T(8,128)(2,1)}, f32[16,32]{1,0:T(8,128)S(1)}) custom-call(s32[4,32]{1,0:T(4,128)S(1)} %bitcast.41, s32[2,34]{1,0:T(2,128)S(1)} %bitcast.45, s32[1]{0:T(128)} %bitcast.2.refs_2_.own_ref, bf16[32,32,128]{2,1,0:T(8,128)(2,1)S(1)} %all_to_all.43.coeff_ref, ...), custom_call_target="tpu_custom_call" | custom-call | tf_op jit(solution)/shard_map/last_modes/pallas_call | solution.py:465
  140.9 0.9 reshape.186
  141.9 6.6 %all-to-all-start.7 = ((f32[128,1,256]{2,1,0:T(1,128)}), f32[128,1,256]{2,1,0:T(1,128)S(1)}, u32[]{:S(2)}, u32[]{:S(2)}) async-start(f32[128,1,256]{2,1,0:T(1,128)} %reshape.186), calls=%async_computation.7 | async-start | bytes 262144 | tf_op jit(solution)/shard_map/all_to_all | solution.py:549
  148.5 9.4 %all-to-all-done.7 = f32[128,1,256]{2,1,0:T(1,128)S(1)} async-done(((f32[128,1,256]{2,1,0:T(1,128)}), f32[128,1,256]{2,1,0:T(1,128)S(1)}, u32[]{:S(2)}, u32[]{:S(2)}) %all-to-all-start.7) | async-done | bytes 131104 | tf_op jit(solution)/shard_map/all_to_all | solution.py:549
  157.9 0.5 broadcast.232
  158.4 1.0 reduce.2
  159.3 0.2 reshape.187
  159.5 0.2 reduce_sum.49
  159.7 0.8 convolution_multiply_fusion
  160.6 0.6 constant_dynamic-slice_fusion
  (43 shorter events, 0.3 us)
Async XLA Ops:
  0.6 43.0 %copy-start.5 = (bf16[2,128,64]{2,1,0:T(8,128)(2,1)S(1)}, bf16[2,128,64]{2,1,0:T(8,128)(2,1)}, u32[]{:S(2)}) copy-start(bf16[2,128,64]{2,1,0:T(8,128)(2,1)} %constant.79.clone.outer_ref) | copy-start | bytes 98308
  0.6 43.0 %copy-start.7 = (f32[2,64,128]{2,1,0:T(8,128)S(1)}, f32[2,64,128]{2,1,0:T(8,128)}, u32[]{:S(2)}) copy-start(f32[2,64,128]{2,1,0:T(8,128)} %constant.81.clone.twist_ref) | copy-start | bytes 196612
  0.7 42.9 %copy-start.14 = (bf16[2,64,128]{2,1,0:T(8,128)(2,1)S(1)}, bf16[2,64,128]{2,1,0:T(8,128)(2,1)}, u32[]{:S(2)}) copy-start(bf16[2,64,128]{2,1,0:T(8,128)(2,1)} %constant.80.clone.outer_t_ref) | copy-start | bytes 98308
  0.7 51.0 %copy-start.18 = (s32[32,4]{0,1:T(4,128)S(1)}, s32[32,4]{0,1:T(4,128)}, u32[]{:S(2)}) copy-start(s32[32,4]{0,1:T(4,128)} %param.14) | copy-start | bytes 1540
  0.7 42.9 %copy-start.1 = (f32[2,8,2,4096]{3,2,1,0:T(2,128)S(1)}, f32[2,8,2,4096]{3,2,1,0:T(2,128)}, u32[]{:S(2)}) copy-start(f32[2,8,2,4096]{3,2,1,0:T(2,128)} %param.10) | copy-start | bytes 1572868
  0.7 42.9 %copy-start.13 = (f32[2,4096]{1,0:T(2,128)S(1)}, f32[2,4096]{1,0:T(2,128)}, u32[]{:S(2)}) copy-start(f32[2,4096]{1,0:T(2,128)} %param.11) | copy-start | bytes 98308
  0.7 51.0 %copy-start.20 = (s32[34,2]{0,1:T(2,128)S(1)}, s32[34,2]{0,1:T(2,128)}, u32[]{:S(2)}) copy-start(s32[34,2]{0,1:T(2,128)} %param.15) | copy-start | bytes 820
  0.7 51.0 %copy-start.16 = (f32[2048]{0:T(1024)S(1)}, f32[2048]{0:T(1024)}, u32[]{:S(2)}) copy-start(f32[2048]{0:T(1024)} %param.12) | copy-start | bytes 24580
  3.0 1.0 copy-start
  4.0 0.8 copy-start.4
  4.9 0.8 copy-start.6
  5.7 0.8 copy-start.12
  8.8 17.4 %all-to-all-start = ((bf16[32,32,128]{2,1,0:T(8,128)(2,1)}), bf16[32,32,128]{2,1,0:T(8,128)(2,1)S(1)}, u32[]{:S(2)}, u32[]{:S(2)}) async-start(bf16[32,32,128]{2,1,0:T(8,128)(2,1)} %first_rows.1), calls=%async_computation | async-start | bytes 524288 | tf_op jit(solution)/shard_map/all_to_all | solution.py:493
  17.1 0.7 copy-start.15
  17.8 0.7 copy-start.17
  18.4 0.7 copy-start.19
  47.1 13.5 %all-to-all-start.2 = ((bf16[32,32,128]{2,1,0:T(8,128)(2,1)}), bf16[32,32,128]{2,1,0:T(8,128)(2,1)}, u32[]{:S(2)}, u32[]{:S(2)}) async-start(bf16[32,32,128]{2,1,0:T(8,128)(2,1)} %rows.3), calls=%async_computation.2 | async-start | bytes 524288 | tf_op jit(solution)/shard_map/all_to_all | solution.py:493
  63.3 0.7 copy-start.9
  81.1 0.7 copy-start.8
  81.8 49.6 %copy-start.21 = (s32[2048]{0:T(1024)S(1)}, s32[2048]{0:T(1024)}, u32[]{:S(2)}) copy-start(s32[2048]{0:T(1024)} %param.16) | copy-start | bytes 24580
  81.8 13.7 %all-to-all-start.4 = ((bf16[32,32,128]{2,1,0:T(8,128)(2,1)}), bf16[32,32,128]{2,1,0:T(8,128)(2,1)}, u32[]{:S(2)}, u32[]{:S(2)}) async-start(bf16[32,32,128]{2,1,0:T(8,128)(2,1)} %copy-done.8), calls=%async_computation.4 | async-start | bytes 524288 | tf_op jit(solution)/shard_map/all_to_all | solution.py:493
  93.7 1.0 copy-start.2
  95.4 1.2 copy-start.3
  96.7 0.9 copy-start.10
  131.4 1.0 copy-start.11
  141.9 16.0 %all-to-all-start.7 = ((f32[128,1,256]{2,1,0:T(1,128)}), f32[128,1,256]{2,1,0:T(1,128)S(1)}, u32[]{:S(2)}, u32[]{:S(2)}) async-start(f32[128,1,256]{2,1,0:T(1,128)} %reshape.186), calls=%async_computation.7 | async-start | bytes 262144 | tf_op jit(solution)/shard_map/all_to_all | solution.py:549

commit v4 on v3

--- a/solution.py
+++ b/solution.py
@@ -44,6 +44,10 @@
     )
 
 
+def precise(left, right, dims=NN):
+    return lax.dot_general(left, right, dims, precision=PRECISE, preferred_element_type=F32)
+
+
 def np_split(value):
     high = value.astype(np.float32).astype(jnp.bfloat16)
     low = (value - high.astype(np.float64)).astype(np.float32).astype(jnp.bfloat16)
@@ -61,7 +65,10 @@
     outer = np.concatenate([np.cos(angle) * same, -np.sin(angle) * same], axis=0)
     twist = 2.0 * np.pi * (k_rows[:, None] * np.arange(INNER)[None, :]) / NPHI
     twist_table = np.stack([np.cos(twist), np.sin(twist)]).astype(np.float32)
-    return np_split(outer), np_split(outer.T), twist_table
+    angle = 2.0 * np.pi * (np.arange(64)[:, None] * np.arange(INNER)[None, :] % INNER) / INNER
+    cosine, sine = [math.sqrt(2.0 / NPHI) * f(angle) for f in (np.cos, np.sin)]
+    upper_table = np_split(np.concatenate([cosine, sine, -sine, cosine], axis=1))
+    return np_split(outer), np_split(outer.T), twist_table, upper_table
 
 
 def column(half, j, p, upper):
@@ -102,13 +109,45 @@
 
 def zero_scale(zero_ref):
     lane = lax.broadcasted_iota(jnp.int32, (128, 512), 1)
-    own = jnp.broadcast_to(zero_ref[...], (128, 512))
+    own = jnp.concatenate([zero_ref[...]] * 4, axis=1)
     return jnp.where(jnp.logical_and(lane % 256 < VEC, own > 0.0), math.sqrt(0.5), 1.0)
 
 
+def fill_inner(group_ref, upper_ref, inner_ref, zero_ref):
+    groups = [group_ref[s : s + 1, :] for s in range(SLOTS)]
+    halves = [group % 2 for group in groups]
+    ranks = []
+    for s in range(SLOTS):
+        rank = jnp.zeros_like(groups[s])
+        for earlier in range(s):
+            rank = rank + (halves[earlier] == halves[s]).astype(jnp.int32)
+        ranks.append(rank)
+    index = lax.broadcasted_iota(jnp.int32, (64, BLK), 0)
+    is_first = (lax.broadcasted_iota(jnp.int32, (64, 128), 0) == 0).astype(BF16)
+    for half in range(2):
+        for j in range(2):
+            upper = jnp.zeros_like(groups[0])
+            for s in range(SLOTS):
+                mine = jnp.logical_and(halves[s] == half, ranks[s] == j)
+                upper = upper + jnp.where(mine, groups[s] // 2, 0)
+            hot = (index == jnp.broadcast_to(upper, (64, BLK))).astype(F32).astype(BF16)
+            for part in range(2):
+                rows = dot(hot, upper_ref[part], TN).astype(BF16)
+                for p in range(2):
+                    at = (j * 2 + p) * BLK
+                    inner_ref[part, half, at : at + BLK, :] = rows[:, p * 256 : (p + 1) * 256]
+            if half == 0:
+                zero = dot(hot, is_first, TN)
+                for p in range(2):
+                    at = (j * 2 + p) * BLK
+                    zero_ref[at : at + BLK, :] = zero
+
+
 def first_rows_kernel(
-    sky_ref, noise_ref, outer_ref, twist_ref, inner_ref, zero_ref, out_ref, turned, staged
+    group_ref, sky_ref, noise_ref, outer_ref, twist_ref, upper_ref,
+    out_ref, inner_ref, zero_ref, turned, staged,
 ):
+    fill_inner(group_ref, upper_ref, inner_ref, zero_ref)
     noise = noise_ref[...]
     forward_part(
         lambda v: noise * sky_ref[v],
@@ -236,7 +275,7 @@
 
 
 def products_kernel(
-    power, group_ref, block_ref, own_ref, legendre_ref, signal_ref, out_ref,
+    group_ref, block_ref, own_ref, legendre_ref, signal_ref, out_ref,
     table, sums, order, pair_slot, pair_live, counter, arrived,
 ):
     find_pairs(group_ref, block_ref, own_ref, order, pair_slot, pair_live, counter)
@@ -266,25 +305,28 @@
             precond = jnp.concatenate(precond, axis=1)
             lane = lax.broadcasted_iota(jnp.int32, (1, 256), 1)
             weight = precond * jnp.where(lane < 128, 1.0, live)
-            for _ in range(power):
+            weights = []
+            for _ in range(ITERS - 1):
+                weights.append(jnp.broadcast_to(weight, (64, 256)))
                 weight = weight * (2.0 * precond)
-            weight = jnp.broadcast_to(weight, (64, 256))
             for i in range(MG):
                 values = jnp.concatenate([table[2 * pair, i], table[2 * pair + 1, i]], axis=1)
-                scaled = (values.astype(F32) * weight).astype(BF16)
-                sums[slot * MG + i] += dot(values, scaled, NT)
+                wide = values.astype(F32)
+                scaled = jnp.concatenate([(wide * w).astype(BF16) for w in weights], axis=0)
+                sums[slot * MG + i] += dot(scaled, values, NT)
         return carry
 
     lax.fori_loop(0, PAIRS // PAIR_GROUP, pair_step, 0)
     for at in range(SLOTS * MG):
-        out_ref[at // 8, (at % 8) * 64 : (at % 8 + 1) * 64, :] = sums[at].astype(BF16)
+        out_ref[at // 8, (at % 8) * 64 : (at % 8 + 1) * 64, :] = jnp.concatenate(
+            [sums[at, n * 64 : (n + 1) * 64] for n in range(ITERS - 1)], axis=1
+        ).astype(BF16)
 
 
 def apply_kernel(count, *refs):
-    coeff_ref = refs[0]
-    product_refs = refs[1 : 1 + count]
-    earlier = refs[1 + count : 2 * count]
-    kept_ref, out_ref, staged, ordered = refs[2 * count :]
+    coeff_ref, product_ref = refs[:2]
+    earlier = refs[2 : 1 + count]
+    kept_ref, out_ref, staged, ordered = refs[1 + count :]
     staged[...] = coeff_ref[...].astype(F32)
     for c in range(16):
         for cycle in range(CYC):
@@ -295,11 +337,10 @@
     for slot in range(SLOTS):
         for upper in range(2):
             at = [(slot * 2 + p) * 2 + upper for p in range(2)]
-            mixed = None
-            for product_ref, ref in zip(product_refs, history):
-                right = jnp.concatenate([ref[at[0]], ref[at[1]]], axis=1)
-                term = dot(product_ref[slot * 2 + upper], right)
-                mixed = term if mixed is None else mixed + term
+            right = jnp.concatenate(
+                [jnp.concatenate([ref[at[0]], ref[at[1]]], axis=1) for ref in history], axis=0
+            )
+            mixed = dot(product_ref[slot * 2 + upper, :, : 64 * count], right)
             result = mixed[:64]
             for i in range(1, 8):
                 result = jnp.where(lane == i, mixed[i * 64 : (i + 1) * 64], result)
@@ -376,26 +417,53 @@
         out_copy(group, size).start()
 
     by_groups(blocks, step)
-    raw = jnp.zeros((VEC, BANDS), F32)
-    counts = jnp.zeros((VEC, BANDS), F32)
-    bins = lax.broadcasted_iota(jnp.int32, (BANDS, 128), 0)
+    raw = jnp.zeros((VEC, 128), F32)
+    counts = jnp.zeros((VEC, 128), F32)
+    bins = lax.broadcasted_iota(jnp.int32, (128, 128), 0) % BANDS
     lane = lax.broadcasted_iota(jnp.int32, (VEC, 128), 1)
+    row = lax.broadcasted_iota(jnp.int32, (VEC, 128), 0)
     for e in range(16):
-        member = (jnp.broadcast_to(band_ref[e : e + 1, :], (BANDS, 128)) == bins).astype(F32)
-        raw = raw + lax.dot_general(
-            products[e], member, NT, precision=PRECISE, preferred_element_type=F32
-        )
-        weight = (2 * (e * 128 + lane) + 1).astype(F32)
-        counts = counts + lax.dot_general(
-            weight, member, NT, precision=PRECISE, preferred_element_type=F32
-        )
-    band_out[...] = raw * (1.0 / jnp.sqrt(counts))
-
+        member = (jnp.broadcast_to(band_ref[e : e + 1, :], (128, 128)) == bins).astype(F32)
+        raw = raw + precise(products[e], member, NT)
+        counts = counts + precise((2 * (e * 128 + lane) + 1).astype(F32), member, NT)
+    terms = jnp.where(lane // BANDS == row // 2 % 4, raw * (1.0 / jnp.sqrt(counts)), 0.0)
+    terms = jnp.concatenate(
+        [jnp.sum(terms[h * 8 : (h + 1) * 8], axis=0, keepdims=True) for h in range(2)], axis=0
+    )
+    band_out[...] = jnp.broadcast_to(terms[None], band_out.shape)
     by_groups(blocks, lambda g, n: out_copy(g, n).wait())
+
+
+def fisher_kernel(sim_ref, term_ref, band_out, fisher_out, rows_ref):
+    sims = term_ref.shape[0] // BLK
+    for part in range(sims):
+        total = term_ref[part]
+        for index in range(1, BLK):
+            total = total + term_ref[index * sims + part]
+        rows_ref[2 * part : 2 * part + 2, :] = total
+    values = rows_ref[...]
+    row = lax.broadcasted_iota(jnp.int32, (128, 128), 0)
+    lane = lax.broadcasted_iota(jnp.int32, (128, 128), 1)
+    count = sims * 8
+    fold = jnp.where(row % BANDS == lane % BANDS, 1.0 / count, 0.0).astype(F32)
+    mean = jnp.sum(precise(values, fold), axis=0, keepdims=True)
+    center = values - jnp.broadcast_to(mean, values.shape)
+    square = jnp.where(row // BANDS == lane // BANDS, precise(center, center, TN), 0.0)
+    column = lax.broadcasted_iota(jnp.int32, (128, BANDS), 0) % BANDS
+    pick = (column == lax.broadcasted_iota(jnp.int32, (128, BANDS), 1)).astype(F32)
+    fisher_out[...] = precise(precise(pick, square, TN), pick) / count
+    own = rows_ref[pl.ds(2 * sim_ref[0], 2), :]
+    own = jnp.concatenate([jnp.broadcast_to(own[h : h + 1], (4, 128)) for h in range(2)], axis=0)
+    keep = lane[:8] // BANDS == row[:8] % 4
+    band_out[...] = precise(jnp.where(keep, own, 0.0), pick)
 
 
 def params(megabytes, **more):
     return pltpu.CompilerParams(vmem_limit_bytes=megabytes << 20, **more)
+
+
+def in_hbm(*arrays):
+    return [pltpu.with_memory_space_constraint(array, pltpu.HBM) for array in arrays]
 
 
 SENT = jax.ShapeDtypeStruct((BLK, 32, 128), BF16)
@@ -405,49 +473,55 @@
 ANY = pl.BlockSpec(memory_space=pl.ANY)
 
 
+def row_scratch():
+    return [pltpu.VMEM((2, 2, 512, 128), F32), pltpu.VMEM((BLK, 32, 128), F32)]
+
+
+def first_transforms(groups, sky, noise, outer, twist, upper):
+    return pl.pallas_call(
+        first_rows_kernel,
+        out_shape=(
+            SENT,
+            jax.ShapeDtypeStruct((2, 2, 128, 256), BF16),
+            jax.ShapeDtypeStruct((128, 128), F32),
+        ),
+        scratch_shapes=row_scratch(),
+        compiler_params=params(28),
+        name="first_rows",
+    )(*in_hbm(groups, sky, noise, outer, twist, upper))
+
+
 def row_transforms(sky, noise, outer, outer_t, twist, inner, zero_rows, coeffs):
-    scratch = [pltpu.VMEM((2, 2, 512, 128), F32), pltpu.VMEM((BLK, 32, 128), F32)]
-    if coeffs is None:
-        return pl.pallas_call(
-            first_rows_kernel,
-            out_shape=SENT,
-            scratch_shapes=scratch,
-            compiler_params=params(32),
-            name="first_rows",
-        )(sky, noise, outer, twist, inner, zero_rows)
     return pl.pallas_call(
         rows_kernel,
         out_shape=SENT,
-        scratch_shapes=scratch,
-        compiler_params=params(32),
+        scratch_shapes=row_scratch(),
+        compiler_params=params(28),
         name="rows",
     )(sky, noise, outer, outer_t, twist, inner, zero_rows, coeffs)
 
 
-def cycle_products(power, scalars, legendre, signal):
-    def body(*refs):
-        products_kernel(power, *refs)
-
+def cycle_products(scalars, legendre, signal):
     return pl.pallas_call(
-        body,
-        out_shape=jax.ShapeDtypeStruct((8, 512, 64), BF16),
+        products_kernel,
+        out_shape=jax.ShapeDtypeStruct((8, 512, 192), BF16),
         in_specs=[SMEM, SMEM, SMEM, ANY, VMEM],
         scratch_shapes=[
             pltpu.VMEM((2 * PAIRS,) + legendre.shape[1:], BF16),
-            pltpu.VMEM((SLOTS * MG, 64, 64), F32),
+            pltpu.VMEM((SLOTS * MG, 192, 64), F32),
             pltpu.SMEM((2 * PAIRS,), jnp.int32),
             pltpu.SMEM((PAIRS,), jnp.int32),
             pltpu.SMEM((PAIRS,), jnp.int32),
             pltpu.SMEM((SLOTS,), jnp.int32),
             pltpu.SemaphoreType.DMA((2 * PAIRS,)),
         ],
-        compiler_params=params(52),
-        name="cycle_products_" + str(power),
-    )(*scalars, legendre, signal)
+        compiler_params=params(28),
+        name="cycle_products",
+    )(*in_hbm(*scalars, legendre, signal))
 
 
 def apply_products(coeffs, products, kept):
-    count = len(products)
+    count = len(kept) + 1
 
     def body(*refs):
         apply_kernel(count, *refs)
@@ -456,17 +530,18 @@
         body,
         out_shape=(KEPT, SENT),
         scratch_shapes=[pltpu.VMEM((BLK, 32, 128), F32), pltpu.VMEM((16, 64, 128), F32)],
-        compiler_params=params(32),
+        compiler_params=params(28),
         name="apply_products_" + str(count),
-    )(coeffs, *products, *kept)
-
-
-def last_step(scalars, coeffs, kept, legendre, signal, bands):
+    )(coeffs, products, *kept)
+
+
+def last_step(copies, scalars, coeffs, kept, legendre, signal, bands):
+    (legendre,) = in_hbm(legendre)
     return pl.pallas_call(
         last_kernel,
         out_shape=(
             jax.ShapeDtypeStruct((legendre.shape[0], 512, 128), BF16),
-            jax.ShapeDtypeStruct((VEC, BANDS), F32),
+            jax.ShapeDtypeStruct((copies, 2, 128), F32),
         ),
         in_specs=[SMEM] * 3 + [VMEM] * 4 + [ANY, VMEM, VMEM],
         out_specs=(ANY, VMEM),
@@ -484,9 +559,23 @@
             pltpu.SemaphoreType.DMA((-(-legendre.shape[0] // GROUP),)),
             pltpu.SemaphoreType.DMA((-(-legendre.shape[0] // GROUP),)),
         ],
-        compiler_params=params(52),
+        compiler_params=params(28),
         name="last_modes",
     )(*scalars, coeffs, *kept, legendre, signal, bands)
+
+
+def fisher_step(sim_index, terms):
+    return pl.pallas_call(
+        fisher_kernel,
+        out_shape=(
+            jax.ShapeDtypeStruct((8, BANDS), F32),
+            jax.ShapeDtypeStruct((BANDS, BANDS), F32),
+        ),
+        in_specs=[SMEM, VMEM],
+        scratch_shapes=[pltpu.VMEM((terms.shape[0] // BLK * 2, 128), F32)],
+        compiler_params=params(28),
+        name="fisher",
+    )(sim_index, terms)
 
 
 def exchange(rows):
@@ -497,61 +586,29 @@
     blk_index = lax.axis_index("blk")
     set_count, sim_local, cycle_local, cycle_pixels = sky_maps.shape
     block_count = legendre.shape[0]
-    outer, outer_t, twist = [jnp.asarray(t) for t in constant_tables()]
+    outer, outer_t, twist, upper = [jnp.asarray(t) for t in constant_tables()]
     sky = sky_maps.reshape(set_count, sim_local, cycle_local, OUTER, INNER)
     sky = sky.transpose(0, 1, 3, 2, 4).reshape(VEC, OUTER * CYC, INNER)
     noise = noise_weight.reshape(CYC, OUTER, INNER).transpose(1, 0, 2).reshape(OUTER * CYC, INNER)
-    half_of = m_groups % 2
-    upper_of = m_groups // 2
-    earlier = jnp.tril(jnp.ones((SLOTS, SLOTS), jnp.int32), -1)
-    rank = jnp.sum(
-        (half_of[:, :, None] == half_of[:, None, :]).astype(jnp.int32) * earlier[None], axis=2
-    )
-    new_slot = 2 * half_of + rank
-    chosen = new_slot[:, :, None] == jnp.arange(SLOTS, dtype=jnp.int32)[None, None, :]
-    upper = jnp.sum(jnp.where(chosen, upper_of[:, :, None], 0), axis=1)
-    upper_rows = upper.T.reshape(2, 2, 1, BLK, 1)
-    angle = (2.0 * math.pi / 128.0) * (
-        upper_rows * jnp.arange(128, dtype=jnp.int32) % 128
-    ).astype(F32)
-    cos_inner = math.sqrt(2.0 / NPHI) * jnp.cos(angle)
-    sin_inner = math.sqrt(2.0 / NPHI) * jnp.sin(angle)
-    inner = jnp.concatenate(
-        [
-            jnp.concatenate([cos_inner, sin_inner], axis=-1),
-            jnp.concatenate([-sin_inner, cos_inner], axis=-1),
-        ],
-        axis=2,
-    ).reshape(2, 128, 256)
-    inner = jnp.stack(split(inner))
-    zero_rows = jnp.broadcast_to(
-        (upper[:, :2].T == 0).astype(F32)[:, None, :], (2, 2, BLK)
-    ).reshape(128, 1)
     scalars = (m_groups.T, block_list.T, blk_index.astype(jnp.int32).reshape(1))
     signal = signal_inverse.reshape(16, 128)
     bands = band_of_ell.reshape(16, 128)
 
-    rows = row_transforms(sky, noise, outer, outer_t, twist, inner, zero_rows, None)
+    rows, inner, zero_rows = first_transforms(scalars[0], sky, noise, outer, twist, upper)
+    own, rows = lax.optimization_barrier((scalars[2], rows))
+    products = cycle_products(scalars[:2] + (own,), legendre, signal)
     kept = []
-    products = []
     for sweep in range(ITERS - 1):
-        own, rows = lax.optimization_barrier((scalars[2], rows))
-        products.append(cycle_products(sweep, scalars[:2] + (own,), legendre, signal))
         coeffs, rows = apply_products(exchange(rows), products, kept)
         kept.append(coeffs)
         rows = row_transforms(
             sky, noise, outer, outer_t, twist, inner, zero_rows, exchange(rows)
         )
-    state, result = last_step(scalars, exchange(rows), kept, legendre, signal, bands)
-    partial = result.reshape(sim_local, 2, BANDS).sum(axis=1)
-    devices = BLK * lax.axis_size("sim")
-    copies = jnp.broadcast_to(partial[None], (devices, sim_local, BANDS))
+    sims = lax.axis_size("sim")
+    state, copies = last_step(BLK * sims, scalars, exchange(rows), kept, legendre, signal, bands)
     terms = lax.all_to_all(copies, ("blk", "sim"), 0, 0, tiled=True)
-    all_proj = jnp.sum(terms.reshape(BLK, -1, BANDS), axis=0)
-    band_proj = lax.dynamic_slice_in_dim(all_proj, lax.axis_index("sim") * sim_local, sim_local, 0)
-    sim_mean = jnp.mean(all_proj, axis=0)
-    center = all_proj - sim_mean[None, :]
-    fisher = jnp.dot(center.T, center, precision=PRECISE) / all_proj.shape[0]
+    sim_index = lax.axis_index("sim").astype(jnp.int32).reshape(1)
+    band_proj, fisher = fisher_step(sim_index, terms)
     filtered = state.reshape(block_count, MG, set_count, sim_local, 2, 128)
     return (filtered, band_proj, fisher)
 

time: 164 us -> 146 us (0.89)
  blocking collectives: 58.1 us -> 78.5 us
  local copies, waits for them, and re-layouts: 13.4 us -> 0.06 us
  starting transfers between devices: 24.2 us -> 14.9 us
  Pallas kernels: 48.5 us -> 40.9 us
  other arithmetic: 3.25 us -> 0 us
  waiting for transfers between devices: 12 us -> 9.4 us
    all_to_all x4 -> x6, blocking collectives: 58.1 us -> 78.5 us  [exchange(): return lax.all_to_all(rows, 'blk', 0, 0, tiled=True)]
    unnamed x46 -> x18, local copies, waits for them, and re-layouts: 12.1 us -> 0.06 us
    all_to_all x3 -> x1, starting transfers between devices: 17.6 us -> 8.25 us  [exchange(): return lax.all_to_all(rows, 'blk', 0, 0, tiled=True)]
    pallas_call x7 -> x6, Pallas kernels: 32.7 us -> 25.4 us  [the longest x1 11.9 us: cycle_products(): pl.pallas_call(products_kernel, out_shape=jax.ShapeDtypeStruct((8, 512, 1...]
    pallas_call x3, Pallas kernels: 7.17 us -> 3.75 us  [apply_products(): pl.pallas_call(body, out_shape=(KEPT, SENT), scratch_shapes=[pltpu.VMEM((...]
    pallas_call x1, Pallas kernels: 8.55 us -> 11.7 us  [last_step(): pl.pallas_call(last_kernel, out_shape=(jax.ShapeDtypeStruct((legendre.sha...]
    all_to_all x3 -> x1, waiting for transfers between devices: 2.57 us -> 0.01 us  [exchange(): return lax.all_to_all(rows, 'blk', 0, 0, tiled=True)]
  transfers between devices with their start and end apart: 4 -> 2, of which waited for: 3 -> 1; matrix products, arithmetic and copies ran while one was open for 0% -> 0% of each run, Pallas kernels for 13% -> 8%
where the time goes in v4:
time: 146 us; the launch traced here: 145 us
  blocking collectives  78.5 us (54%)
  Pallas kernels  40.9 us (28%)
  starting transfers between devices  14.9 us (10%)
  waiting for transfers between devices  9.4 us (6%)
    all_to_all x6, blocking collectives, exchange(): return lax.all_to_all(rows, 'blk', 0, 0, tiled=True)  78.5 us
    pallas_call x1, Pallas kernels, cycle_products(): pl.pallas_call(products_kernel, out_shape=jax.ShapeDtypeStruct((8, 512, 1...  11.9 us
    pallas_call x1, Pallas kernels, last_step(): pl.pallas_call(last_kernel, out_shape=(jax.ShapeDtypeStruct((legendre.sha...  11.7 us
    all_to_all x1, waiting for transfers between devices, shards(): terms = lax.all_to_all(copies, ('blk', 'sim'), 0, 0, tiled=True)  9.4 us
    pallas_call x3, Pallas kernels, row_transforms(): pl.pallas_call(rows_kernel, out_shape=SENT, scratch_shapes=row_scratch(),...  8.26 us
    all_to_all x1, starting transfers between devices, exchange(): return lax.all_to_all(rows, 'blk', 0, 0, tiled=True)  8.25 us
    all_to_all x1, starting transfers between devices, shards(): terms = lax.all_to_all(copies, ('blk', 'sim'), 0, 0, tiled=True)  6.64 us
    pallas_call x3, Pallas kernels, apply_products(): pl.pallas_call(body, out_shape=(KEPT, SENT), scratch_shapes=[pltpu.VMEM((...  3.75 us
  transfers between devices with their start and end apart: 2, of which 1 were waited for; matrix products, arithmetic and copies ran while one was open for 0% of the time, Pallas kernels for 8%

profile of v4, /device:TPU:0, one launch (start us, length us, event | category | flops | bytes accessed | tf_op | source)
XLA Modules:
  0.0 144.6 jit_solution(8101293074968760795)
XLA Ops:
  0.6 3.7 %first_rows.1 = (bf16[32,32,128]{2,1,0:T(8,128)(2,1)}, bf16[2,2,128,256]{3,2,1,0:T(8,128)(2,1)S(1)}, f32[128,128]{1,0:T(8,128)S(1)}) custom-call(s32[4,32]{1,0:T(4,128)} %bitcast.27, f32[16,64,128]{2,1,0:T(8,128)} %bitcast.17, f32[64,128]{1,0:T(8,128)} %bitcast.21, bf16[2,128,64]{2,1,0:T(8,128)(2,1)} %constant.17.clone.outer_ref, ...), custom_call_target="tpu_custom_call" | custom-call | tf_op jit(solution)/shard_map/first_rows/pallas_call | solution.py:481
  4.3 8.2 %all-to-all-start = ((bf16[32,32,128]{2,1,0:T(8,128)(2,1)}), bf16[32,32,128]{2,1,0:T(8,128)(2,1)S(1)}, u32[]{:S(2)}, u32[]{:S(2)}) async-start(bf16[32,32,128]{2,1,0:T(8,128)(2,1)} %get-tuple-element.21), calls=%async_computation | async-start | bytes 524288 | tf_op jit(solution)/shard_map/all_to_all | solution.py:582
  12.5 0.0 copy-start
  12.6 0.0 copy-start.1
  12.6 0.0 copy-start.2
  12.6 0.0 copy-start.3
  12.6 0.0 copy-start.4
  12.6 11.9 %cycle_products.1.refs_1_ = bf16[8,512,192]{2,1,0:T(8,128)(2,1)S(1)} custom-call(s32[4,32]{1,0:T(4,128)} %bitcast.28, s32[2,34]{1,0:T(2,128)} %bitcast.31, s32[1]{0:T(128)} %bitcast.2.own_ref, bf16[34,16,64,128]{3,2,1,0:T(8,128)(2,1)} %legendre_ref.3, f32[16,128]{1,0:T(8,128)} %bitcast.25), custom_call_target="tpu_custom_call" | custom-call | tf_op jit(solution)/shard_map/cycle_products/pallas_call | solution.py:505
  24.6 0.0 all-to-all-done.refs_0_
  24.6 1.2 apply_products_1.1
  25.8 16.1 %all_to_all.40.coeff_ref = bf16[32,32,128]{2,1,0:T(8,128)(2,1)S(1)} all-to-all(bf16[32,32,128]{2,1,0:T(8,128)(2,1)S(1)} %get-tuple-element.23), channel_id=1, replica_groups=mesh['blk'=32,'sim'=4] {'blk'}, dimensions={0} | all-to-all | bytes 524288 | tf_op jit(solution)/shard_map/all_to_all | solution.py:582
  41.9 0.0 copy-done
  41.9 0.0 copy-done.1
  41.9 0.0 copy-done.2
  41.9 0.0 copy-done.3
  41.9 0.0 copy-done.4
  41.9 2.8 %rows.3 = bf16[32,32,128]{2,1,0:T(8,128)(2,1)S(1)} custom-call(f32[16,64,128]{2,1,0:T(8,128)S(1)} %bitcast.18, f32[64,128]{1,0:T(8,128)S(1)} %bitcast.22, bf16[2,128,64]{2,1,0:T(8,128)(2,1)S(1)} %copy-done.2, bf16[2,64,128]{2,1,0:T(8,128)(2,1)S(1)} %copy-done.4, f32[2,64,128]{2,1,0:T(8,128)S(1)} %copy-done.1, ...), custom_call_target="tpu_custom_call" | custom-call | tf_op jit(solution)/shard_map/rows/pallas_call | solution.py:495
  44.7 12.5 %all_to_all.41.refs_0_ = bf16[32,32,128]{2,1,0:T(8,128)(2,1)S(1)} all-to-all(bf16[32,32,128]{2,1,0:T(8,128)(2,1)S(1)} %rows.3), channel_id=1, replica_groups=mesh['blk'=32,'sim'=4] {'blk'}, dimensions={0} | all-to-all | bytes 524288 | tf_op jit(solution)/shard_map/all_to_all | solution.py:582
  57.1 1.3 apply_products_2.1
  58.4 0.0 copy-start.5
  58.4 0.0 copy-start.6
  58.4 0.0 copy-start.7
  58.4 0.0 copy-start.8
  58.4 12.6 %all_to_all.42.coeff_ref = bf16[32,32,128]{2,1,0:T(8,128)(2,1)S(1)} all-to-all(bf16[32,32,128]{2,1,0:T(8,128)(2,1)S(1)} %get-tuple-element.25), channel_id=1, replica_groups=mesh['blk'=32,'sim'=4] {'blk'}, dimensions={0} | all-to-all | bytes 524288 | tf_op jit(solution)/shard_map/all_to_all | solution.py:582
  71.0 2.8 %rows.4 = bf16[32,32,128]{2,1,0:T(8,128)(2,1)S(1)} custom-call(f32[16,64,128]{2,1,0:T(8,128)S(1)} %bitcast.19, f32[64,128]{1,0:T(8,128)S(1)} %bitcast.23, bf16[2,128,64]{2,1,0:T(8,128)(2,1)S(1)} %copy-done.2, bf16[2,64,128]{2,1,0:T(8,128)(2,1)S(1)} %copy-done.4, f32[2,64,128]{2,1,0:T(8,128)S(1)} %copy-done.1, ...), custom_call_target="tpu_custom_call" | custom-call | tf_op jit(solution)/shard_map/rows/pallas_call | solution.py:495
  73.8 12.5 %all_to_all.43.refs_0_ = bf16[32,32,128]{2,1,0:T(8,128)(2,1)S(1)} all-to-all(bf16[32,32,128]{2,1,0:T(8,128)(2,1)S(1)} %rows.4), channel_id=1, replica_groups=mesh['blk'=32,'sim'=4] {'blk'}, dimensions={0} | all-to-all | bytes 524288 | tf_op jit(solution)/shard_map/all_to_all | solution.py:582
  86.2 1.3 apply_products_3.1
  87.6 12.5 %all_to_all.44.coeff_ref = bf16[32,32,128]{2,1,0:T(8,128)(2,1)S(1)} all-to-all(bf16[32,32,128]{2,1,0:T(8,128)(2,1)S(1)} %get-tuple-element.27), channel_id=1, replica_groups=mesh['blk'=32,'sim'=4] {'blk'}, dimensions={0} | all-to-all | bytes 524288 | tf_op jit(solution)/shard_map/all_to_all | solution.py:582
  100.0 2.8 %rows.5 = bf16[32,32,128]{2,1,0:T(8,128)(2,1)S(1)} custom-call(f32[16,64,128]{2,1,0:T(8,128)S(1)} %bitcast.20, f32[64,128]{1,0:T(8,128)S(1)} %bitcast.24, bf16[2,128,64]{2,1,0:T(8,128)(2,1)S(1)} %copy-done.2, bf16[2,64,128]{2,1,0:T(8,128)(2,1)S(1)} %copy-done.4, f32[2,64,128]{2,1,0:T(8,128)S(1)} %copy-done.1, ...), custom_call_target="tpu_custom_call" | custom-call | tf_op jit(solution)/shard_map/rows/pallas_call | solution.py:495
  102.8 12.5 %all_to_all.45.coeff_ref = bf16[32,32,128]{2,1,0:T(8,128)(2,1)S(1)} all-to-all(bf16[32,32,128]{2,1,0:T(8,128)(2,1)S(1)} %rows.5), channel_id=1, replica_groups=mesh['blk'=32,'sim'=4] {'blk'}, dimensions={0} | all-to-all | bytes 524288 | tf_op jit(solution)/shard_map/all_to_all | solution.py:582
  115.2 0.0 copy-done.5
  115.3 0.0 copy-done.6
  115.3 0.0 copy-done.7
  115.3 0.0 copy-done.8
  115.3 11.7 %last_modes.1 = (bf16[34,512,128]{2,1,0:T(8,128)(2,1)}, f32[128,2,128]{2,1,0:T(2,128)}) custom-call(s32[4,32]{1,0:T(4,128)S(1)} %bitcast.29, s32[2,34]{1,0:T(2,128)S(1)} %bitcast.32, s32[1]{0:T(128)} %bitcast.2.own_ref, bf16[32,32,128]{2,1,0:T(8,128)(2,1)S(1)} %all_to_all.45.coeff_ref, bf16[16,64,128]{2,1,0:T(8,128)(2,1)S(1)} %get-tuple-element.24.refs_2_.kept0_ref, ...), custom_call_target="tpu_custom_call" | custom-call | tf_op jit(solution)/shard_map/last_modes/pallas_call | solution.py:540
  127.0 6.6 %all-to-all-start.7 = ((f32[128,2,128]{2,1,0:T(2,128)}), f32[128,2,128]{2,1,0:T(2,128)S(1)}, u32[]{:S(2)}, u32[]{:S(2)}) async-start(f32[128,2,128]{2,1,0:T(2,128)} %get-tuple-element.30), calls=%async_computation.7 | async-start | bytes 262144 | tf_op jit(solution)/shard_map/all_to_all | solution.py:609
  133.6 9.4 %all-to-all-done.7.term_ref = f32[128,2,128]{2,1,0:T(2,128)S(1)} async-done(((f32[128,2,128]{2,1,0:T(2,128)}), f32[128,2,128]{2,1,0:T(2,128)S(1)}, u32[]{:S(2)}, u32[]{:S(2)}) %all-to-all-start.7) | async-done | bytes 131104 | tf_op jit(solution)/shard_map/all_to_all | solution.py:609
  143.0 1.6 %fisher.1 = (f32[8,32]{1,0:T(8,128)}, f32[32,32]{1,0:T(8,128)}) custom-call(s32[1]{0:T(128)} %bitcast.16.sim_ref, f32[128,2,128]{2,1,0:T(2,128)S(1)} %all-to-all-done.7.term_ref), custom_call_target="tpu_custom_call" | custom-call | tf_op jit(solution)/shard_map/fisher/pallas_call | solution.py:568
Async XLA Ops:
  4.3 20.3 %all-to-all-start = ((bf16[32,32,128]{2,1,0:T(8,128)(2,1)}), bf16[32,32,128]{2,1,0:T(8,128)(2,1)S(1)}, u32[]{:S(2)}, u32[]{:S(2)}) async-start(bf16[32,32,128]{2,1,0:T(8,128)(2,1)} %get-tuple-element.21), calls=%async_computation | async-start | bytes 524288 | tf_op jit(solution)/shard_map/all_to_all | solution.py:582
  12.5 29.3 %copy-start = (f32[2,8,2,4096]{3,2,1,0:T(2,128)S(1)}, f32[2,8,2,4096]{3,2,1,0:T(2,128)}, u32[]{:S(2)}) copy-start(f32[2,8,2,4096]{3,2,1,0:T(2,128)} %param.11) | copy-start | bytes 1572868
  12.6 29.3 %copy-start.1 = (f32[2,64,128]{2,1,0:T(8,128)S(1)}, f32[2,64,128]{2,1,0:T(8,128)}, u32[]{:S(2)}) copy-start(f32[2,64,128]{2,1,0:T(8,128)} %constant.19.clone.twist_ref) | copy-start | bytes 196612
  12.6 29.3 %copy-start.2 = (bf16[2,128,64]{2,1,0:T(8,128)(2,1)S(1)}, bf16[2,128,64]{2,1,0:T(8,128)(2,1)}, u32[]{:S(2)}) copy-start(bf16[2,128,64]{2,1,0:T(8,128)(2,1)} %constant.17.clone.outer_ref) | copy-start | bytes 98308
  12.6 29.3 %copy-start.3 = (f32[2,4096]{1,0:T(2,128)S(1)}, f32[2,4096]{1,0:T(2,128)}, u32[]{:S(2)}) copy-start(f32[2,4096]{1,0:T(2,128)} %param.12) | copy-start | bytes 98308
  12.6 29.3 %copy-start.4 = (bf16[2,64,128]{2,1,0:T(8,128)(2,1)S(1)}, bf16[2,64,128]{2,1,0:T(8,128)(2,1)}, u32[]{:S(2)}) copy-start(bf16[2,64,128]{2,1,0:T(8,128)(2,1)} %constant.18.clone.outer_t_ref) | copy-start | bytes 98308
  58.4 56.9 %copy-start.5 = (f32[2048]{0:T(1024)S(1)}, f32[2048]{0:T(1024)}, u32[]{:S(2)}) copy-start(f32[2048]{0:T(1024)} %param.13) | copy-start | bytes 24580
  58.4 56.9 %copy-start.6 = (s32[32,4]{0,1:T(4,128)S(1)}, s32[32,4]{0,1:T(4,128)}, u32[]{:S(2)}) copy-start(s32[32,4]{0,1:T(4,128)} %param.15) | copy-start | bytes 1540
  58.4 56.8 %copy-start.7 = (s32[2048]{0:T(1024)S(1)}, s32[2048]{0:T(1024)}, u32[]{:S(2)}) copy-start(s32[2048]{0:T(1024)} %param.17) | copy-start | bytes 24580
  58.4 56.8 %copy-start.8 = (s32[34,2]{0,1:T(2,128)S(1)}, s32[34,2]{0,1:T(2,128)}, u32[]{:S(2)}) copy-start(s32[34,2]{0,1:T(2,128)} %param.16) | copy-start | bytes 820
  127.0 16.0 %all-to-all-start.7 = ((f32[128,2,128]{2,1,0:T(2,128)}), f32[128,2,128]{2,1,0:T(2,128)S(1)}, u32[]{:S(2)}, u32[]{:S(2)}) async-start(f32[128,2,128]{2,1,0:T(2,128)} %get-tuple-element.30), calls=%async_computation.7 | async-start | bytes 262144 | tf_op jit(solution)/shard_map/all_to_all | solution.py:609

commit v5 on v4

--- a/solution.py
+++ b/solution.py
@@ -38,20 +38,12 @@
     return lax.dot_general(left, right, dims, preferred_element_type=F32)
 
 
-def dot3(left, right, dims=NN):
-    return (
-        dot(left[0], right[0], dims) + dot(left[0], right[1], dims) + dot(left[1], right[0], dims)
-    )
-
-
 def precise(left, right, dims=NN):
     return lax.dot_general(left, right, dims, precision=PRECISE, preferred_element_type=F32)
 
 
-def np_split(value):
-    high = value.astype(np.float32).astype(jnp.bfloat16)
-    low = (value - high.astype(np.float64)).astype(np.float32).astype(jnp.bfloat16)
-    return np.stack([high, low])
+def rounded(value):
+    return value.astype(np.float32).astype(jnp.bfloat16)
 
 
 def constant_tables():
@@ -67,8 +59,8 @@
     twist_table = np.stack([np.cos(twist), np.sin(twist)]).astype(np.float32)
     angle = 2.0 * np.pi * (np.arange(64)[:, None] * np.arange(INNER)[None, :] % INNER) / INNER
     cosine, sine = [math.sqrt(2.0 / NPHI) * f(angle) for f in (np.cos, np.sin)]
-    upper_table = np_split(np.concatenate([cosine, sine, -sine, cosine], axis=1))
-    return np_split(outer), np_split(outer.T), twist_table, upper_table
+    upper_table = rounded(np.concatenate([cosine, sine, -sine, cosine], axis=1))
+    return rounded(outer), rounded(outer.T), twist_table, upper_table
 
 
 def column(half, j, p, upper):
@@ -76,10 +68,10 @@
 
 
 def forward_part(field_of, outer_ref, twist_ref, inner_ref, zero_ref, out_ref, turned, staged):
-    outer = (outer_ref[0], outer_ref[1])
+    outer = outer_ref[...]
     cos_twist, sin_twist = twist_ref[0], twist_ref[1]
     for v in range(VEC):
-        first = dot3(outer, split(field_of(v)))
+        first = dot(outer, field_of(v).astype(BF16))
         real, imag = first[:64], first[64:]
         turned_real = real * cos_twist + imag * sin_twist
         turned_imag = imag * cos_twist - real * sin_twist
@@ -90,9 +82,8 @@
                 turned[half, 0, rows, :] = turned_real[at : at + MG]
                 turned[half, 1, rows, :] = turned_imag[at : at + MG]
     for half in range(2):
-        inner = (inner_ref[0, half], inner_ref[1, half])
         both = jnp.concatenate([turned[half, 0], turned[half, 1]], axis=1)
-        coeffs = dot3(inner, split(both), NT)
+        coeffs = dot(inner_ref[half], both.astype(BF16), NT)
         if half == 0:
             coeffs = coeffs * zero_scale(zero_ref)
         for j in range(2):
@@ -131,11 +122,10 @@
                 mine = jnp.logical_and(halves[s] == half, ranks[s] == j)
                 upper = upper + jnp.where(mine, groups[s] // 2, 0)
             hot = (index == jnp.broadcast_to(upper, (64, BLK))).astype(F32).astype(BF16)
-            for part in range(2):
-                rows = dot(hot, upper_ref[part], TN).astype(BF16)
-                for p in range(2):
-                    at = (j * 2 + p) * BLK
-                    inner_ref[part, half, at : at + BLK, :] = rows[:, p * 256 : (p + 1) * 256]
+            rows = dot(hot, upper_ref[...], TN).astype(BF16)
+            for p in range(2):
+                at = (j * 2 + p) * BLK
+                inner_ref[half, at : at + BLK, :] = rows[:, p * 256 : (p + 1) * 256]
             if half == 0:
                 zero = dot(hot, is_first, TN)
                 for p in range(2):
@@ -178,7 +168,7 @@
         if half == 0:
             coeffs = coeffs * zero_scale(zero_ref)
         coeffs = coeffs.astype(BF16)
-        inner = dot(coeffs, inner_ref[0, half], TN) + dot(coeffs, inner_ref[1, half], TN)
+        inner = dot(coeffs, inner_ref[half], TN)
         for i in range(MG):
             at = half * CYC * MG + i
             cos_twist = jnp.broadcast_to(twist_ref[0, at : at + 1], (VEC, 128))
@@ -189,7 +179,7 @@
                 turned[half, 0, rows, :] = real * cos_twist - imag * sin_twist
                 turned[half, 1, rows, :] = real * sin_twist + imag * cos_twist
     noise = noise_ref[...]
-    outer_t = (outer_t_ref[0], outer_t_ref[1])
+    outer_t = outer_t_ref[...]
     fields = []
     for v in range(VEC):
         spectrum = jnp.concatenate(
@@ -201,7 +191,7 @@
             ],
             axis=0,
         )
-        fields.append(noise * (sky_ref[v] - dot3(outer_t, split(spectrum))))
+        fields.append(noise * (sky_ref[v] - dot(outer_t, spectrum.astype(BF16))))
     forward_part(
         lambda v: fields[v],
         outer_ref, twist_ref, inner_ref, zero_ref, out_ref, turned, staged,
@@ -417,15 +407,19 @@
         out_copy(group, size).start()
 
     by_groups(blocks, step)
-    raw = jnp.zeros((VEC, 128), F32)
-    counts = jnp.zeros((VEC, 128), F32)
     bins = lax.broadcasted_iota(jnp.int32, (128, 128), 0) % BANDS
     lane = lax.broadcasted_iota(jnp.int32, (VEC, 128), 1)
     row = lax.broadcasted_iota(jnp.int32, (VEC, 128), 0)
+    sums = jnp.zeros((80, 128), F32)
     for e in range(16):
         member = (jnp.broadcast_to(band_ref[e : e + 1, :], (128, 128)) == bins).astype(F32)
-        raw = raw + precise(products[e], member, NT)
-        counts = counts + precise((2 * (e * 128 + lane) + 1).astype(F32), member, NT)
+        high = products[e].astype(BF16)
+        middle, low = split(products[e] - high.astype(F32))
+        weight = split((2 * (e * 128 + lane) + 1).astype(F32))
+        left = jnp.concatenate([high, middle, low, weight[0], weight[1]], axis=0)
+        sums = sums + dot(left, member.astype(BF16), NT)
+    raw = sums[0:16] + (sums[16:32] + sums[32:48])
+    counts = sums[48:64] + sums[64:80]
     terms = jnp.where(lane // BANDS == row // 2 % 4, raw * (1.0 / jnp.sqrt(counts)), 0.0)
     terms = jnp.concatenate(
         [jnp.sum(terms[h * 8 : (h + 1) * 8], axis=0, keepdims=True) for h in range(2)], axis=0
@@ -482,7 +476,7 @@
         first_rows_kernel,
         out_shape=(
             SENT,
-            jax.ShapeDtypeStruct((2, 2, 128, 256), BF16),
+            jax.ShapeDtypeStruct((2, 128, 256), BF16),
             jax.ShapeDtypeStruct((128, 128), F32),
         ),
         scratch_shapes=row_scratch(),

time: 146 us -> 141 us (0.966)
  Pallas kernels: 40.9 us -> 35.8 us
    pallas_call x1, Pallas kernels: 11.7 us -> 9.1 us  [last_step(): pl.pallas_call(last_kernel, out_shape=(jax.ShapeDtypeStruct((legendre.sha...]
    pallas_call x3, Pallas kernels: 8.26 us -> 6.46 us  [row_transforms(): pl.pallas_call(rows_kernel, out_shape=SENT, scratch_shapes=row_scratch(),...]
  transfers between devices with their start and end apart: 2 -> 2, of which waited for: 1 -> 1; matrix products, arithmetic and copies ran while one was open for 0% -> 0% of each run, Pallas kernels for 8% -> 9%
where the time goes in v5:
time: 141 us; the launch traced here: 140 us
  blocking collectives  78.7 us (56%)
  Pallas kernels  35.8 us (25%)
  starting transfers between devices  14.9 us (11%)
  waiting for transfers between devices  9.4 us (7%)
    all_to_all x6, blocking collectives, exchange(): return lax.all_to_all(rows, 'blk', 0, 0, tiled=True)  78.7 us
    pallas_call x1, Pallas kernels, cycle_products(): pl.pallas_call(products_kernel, out_shape=jax.ShapeDtypeStruct((8, 512, 1...  11.9 us
    all_to_all x1, waiting for transfers between devices, shards(): terms = lax.all_to_all(copies, ('blk', 'sim'), 0, 0, tiled=True)  9.4 us
    pallas_call x1, Pallas kernels, last_step(): pl.pallas_call(last_kernel, out_shape=(jax.ShapeDtypeStruct((legendre.sha...  9.1 us
    all_to_all x1, starting transfers between devices, exchange(): return lax.all_to_all(rows, 'blk', 0, 0, tiled=True)  8.24 us
    all_to_all x1, starting transfers between devices, shards(): terms = lax.all_to_all(copies, ('blk', 'sim'), 0, 0, tiled=True)  6.62 us
    pallas_call x3, Pallas kernels, row_transforms(): pl.pallas_call(rows_kernel, out_shape=SENT, scratch_shapes=row_scratch(),...  6.46 us
    pallas_call x3, Pallas kernels, apply_products(): pl.pallas_call(body, out_shape=(KEPT, SENT), scratch_shapes=[pltpu.VMEM((...  3.77 us
  transfers between devices with their start and end apart: 2, of which 1 were waited for; matrix products, arithmetic and copies ran while one was open for 0% of the time, Pallas kernels for 9%

profile of v5, /device:TPU:0, one launch (start us, length us, event | category | flops | bytes accessed | tf_op | source)
XLA Modules:
  0.0 139.7 jit_solution(1986786225003165828)
XLA Ops:
  0.6 3.0 %first_rows.1 = (bf16[32,32,128]{2,1,0:T(8,128)(2,1)}, bf16[2,128,256]{2,1,0:T(8,128)(2,1)S(1)}, f32[128,128]{1,0:T(8,128)S(1)}) custom-call(s32[4,32]{1,0:T(4,128)} %bitcast.27, f32[16,64,128]{2,1,0:T(8,128)} %bitcast.17, f32[64,128]{1,0:T(8,128)} %bitcast.21, bf16[128,64]{1,0:T(8,128)(2,1)} %constant.17.clone.outer_ref, ...), custom_call_target="tpu_custom_call" | custom-call | tf_op jit(solution)/shard_map/first_rows/pallas_call | solution.py:475
  3.6 8.2 %all-to-all-start = ((bf16[32,32,128]{2,1,0:T(8,128)(2,1)}), bf16[32,32,128]{2,1,0:T(8,128)(2,1)S(1)}, u32[]{:S(2)}, u32[]{:S(2)}) async-start(bf16[32,32,128]{2,1,0:T(8,128)(2,1)} %get-tuple-element.21), calls=%async_computation | async-start | bytes 524288 | tf_op jit(solution)/shard_map/all_to_all | solution.py:576
  11.9 0.0 copy-start
  11.9 0.0 copy-start.1
  11.9 0.0 copy-start.2
  11.9 0.0 copy-start.3
  11.9 0.0 copy-start.4
  11.9 11.9 %cycle_products.1.refs_1_ = bf16[8,512,192]{2,1,0:T(8,128)(2,1)S(1)} custom-call(s32[4,32]{1,0:T(4,128)} %bitcast.28, s32[2,34]{1,0:T(2,128)} %bitcast.31, s32[1]{0:T(128)} %bitcast.2.own_ref, bf16[34,16,64,128]{3,2,1,0:T(8,128)(2,1)} %legendre_ref.3, f32[16,128]{1,0:T(8,128)} %bitcast.25), custom_call_target="tpu_custom_call" | custom-call | tf_op jit(solution)/shard_map/cycle_products/pallas_call | solution.py:499
  23.9 0.0 all-to-all-done.refs_0_
  23.9 1.2 apply_products_1.1
  25.1 16.3 %all_to_all.40.coeff_ref = bf16[32,32,128]{2,1,0:T(8,128)(2,1)S(1)} all-to-all(bf16[32,32,128]{2,1,0:T(8,128)(2,1)S(1)} %get-tuple-element.23), channel_id=1, replica_groups=mesh['blk'=32,'sim'=4] {'blk'}, dimensions={0} | all-to-all | bytes 524288 | tf_op jit(solution)/shard_map/all_to_all | solution.py:576
  41.3 0.0 copy-done
  41.3 0.0 copy-done.1
  41.4 0.0 copy-done.2
  41.4 0.0 copy-done.3
  41.4 0.0 copy-done.4
  41.4 2.2 %rows.3 = bf16[32,32,128]{2,1,0:T(8,128)(2,1)S(1)} custom-call(f32[16,64,128]{2,1,0:T(8,128)S(1)} %bitcast.18, f32[64,128]{1,0:T(8,128)S(1)} %bitcast.22, bf16[128,64]{1,0:T(8,128)(2,1)S(1)} %copy-done.3, bf16[64,128]{1,0:T(8,128)(2,1)S(1)} %copy-done.4, f32[2,64,128]{2,1,0:T(8,128)S(1)} %copy-done.1, bf16[2,128,256]{2,1,0:T(8,128)(2,1)S(1)} %get-tuple-element.18.inner_ref, ...), custom_call_target="tpu_custom_call" | custom-call | tf_op jit(solution)/shard_map/rows/pallas_call | solution.py:489
  43.5 12.5 %all_to_all.41.refs_0_ = bf16[32,32,128]{2,1,0:T(8,128)(2,1)S(1)} all-to-all(bf16[32,32,128]{2,1,0:T(8,128)(2,1)S(1)} %rows.3), channel_id=1, replica_groups=mesh['blk'=32,'sim'=4] {'blk'}, dimensions={0} | all-to-all | bytes 524288 | tf_op jit(solution)/shard_map/all_to_all | solution.py:576
  56.0 1.3 apply_products_2.1
  57.3 0.0 copy-start.5
  57.3 0.0 copy-start.6
  57.3 0.0 copy-start.7
  57.3 0.0 copy-start.8
  57.3 12.6 %all_to_all.42.coeff_ref = bf16[32,32,128]{2,1,0:T(8,128)(2,1)S(1)} all-to-all(bf16[32,32,128]{2,1,0:T(8,128)(2,1)S(1)} %get-tuple-element.25), channel_id=1, replica_groups=mesh['blk'=32,'sim'=4] {'blk'}, dimensions={0} | all-to-all | bytes 524288 | tf_op jit(solution)/shard_map/all_to_all | solution.py:576
  69.9 2.1 %rows.4 = bf16[32,32,128]{2,1,0:T(8,128)(2,1)S(1)} custom-call(f32[16,64,128]{2,1,0:T(8,128)S(1)} %bitcast.19, f32[64,128]{1,0:T(8,128)S(1)} %bitcast.23, bf16[128,64]{1,0:T(8,128)(2,1)S(1)} %copy-done.3, bf16[64,128]{1,0:T(8,128)(2,1)S(1)} %copy-done.4, f32[2,64,128]{2,1,0:T(8,128)S(1)} %copy-done.1, bf16[2,128,256]{2,1,0:T(8,128)(2,1)S(1)} %get-tuple-element.18.inner_ref, ...), custom_call_target="tpu_custom_call" | custom-call | tf_op jit(solution)/shard_map/rows/pallas_call | solution.py:489
  72.1 12.5 %all_to_all.43.refs_0_ = bf16[32,32,128]{2,1,0:T(8,128)(2,1)S(1)} all-to-all(bf16[32,32,128]{2,1,0:T(8,128)(2,1)S(1)} %rows.4), channel_id=1, replica_groups=mesh['blk'=32,'sim'=4] {'blk'}, dimensions={0} | all-to-all | bytes 524288 | tf_op jit(solution)/shard_map/all_to_all | solution.py:576
  84.5 1.3 apply_products_3.1
  85.9 12.5 %all_to_all.44.coeff_ref = bf16[32,32,128]{2,1,0:T(8,128)(2,1)S(1)} all-to-all(bf16[32,32,128]{2,1,0:T(8,128)(2,1)S(1)} %get-tuple-element.27), channel_id=1, replica_groups=mesh['blk'=32,'sim'=4] {'blk'}, dimensions={0} | all-to-all | bytes 524288 | tf_op jit(solution)/shard_map/all_to_all | solution.py:576
  98.3 2.1 %rows.5 = bf16[32,32,128]{2,1,0:T(8,128)(2,1)S(1)} custom-call(f32[16,64,128]{2,1,0:T(8,128)S(1)} %bitcast.20, f32[64,128]{1,0:T(8,128)S(1)} %bitcast.24, bf16[128,64]{1,0:T(8,128)(2,1)S(1)} %copy-done.3, bf16[64,128]{1,0:T(8,128)(2,1)S(1)} %copy-done.4, f32[2,64,128]{2,1,0:T(8,128)S(1)} %copy-done.1, bf16[2,128,256]{2,1,0:T(8,128)(2,1)S(1)} %get-tuple-element.18.inner_ref, ...), custom_call_target="tpu_custom_call" | custom-call | tf_op jit(solution)/shard_map/rows/pallas_call | solution.py:489
  100.5 12.5 %all_to_all.45.coeff_ref = bf16[32,32,128]{2,1,0:T(8,128)(2,1)S(1)} all-to-all(bf16[32,32,128]{2,1,0:T(8,128)(2,1)S(1)} %rows.5), channel_id=1, replica_groups=mesh['blk'=32,'sim'=4] {'blk'}, dimensions={0} | all-to-all | bytes 524288 | tf_op jit(solution)/shard_map/all_to_all | solution.py:576
  112.9 0.0 copy-done.5
  112.9 0.0 copy-done.6
  112.9 0.0 copy-done.7
  112.9 0.0 copy-done.8
  113.0 9.1 %last_modes.1 = (bf16[34,512,128]{2,1,0:T(8,128)(2,1)}, f32[128,2,128]{2,1,0:T(2,128)}) custom-call(s32[4,32]{1,0:T(4,128)S(1)} %bitcast.29, s32[2,34]{1,0:T(2,128)S(1)} %bitcast.32, s32[1]{0:T(128)} %bitcast.2.own_ref, bf16[32,32,128]{2,1,0:T(8,128)(2,1)S(1)} %all_to_all.45.coeff_ref, bf16[16,64,128]{2,1,0:T(8,128)(2,1)S(1)} %get-tuple-element.24.refs_2_.kept0_ref, ...), custom_call_target="tpu_custom_call" | custom-call | tf_op jit(solution)/shard_map/last_modes/pallas_call | solution.py:534
  122.1 6.6 %all-to-all-start.7 = ((f32[128,2,128]{2,1,0:T(2,128)}), f32[128,2,128]{2,1,0:T(2,128)S(1)}, u32[]{:S(2)}, u32[]{:S(2)}) async-start(f32[128,2,128]{2,1,0:T(2,128)} %get-tuple-element.30), calls=%async_computation.7 | async-start | bytes 262144 | tf_op jit(solution)/shard_map/all_to_all | solution.py:603
  128.7 9.4 %all-to-all-done.7.term_ref = f32[128,2,128]{2,1,0:T(2,128)S(1)} async-done(((f32[128,2,128]{2,1,0:T(2,128)}), f32[128,2,128]{2,1,0:T(2,128)S(1)}, u32[]{:S(2)}, u32[]{:S(2)}) %all-to-all-start.7) | async-done | bytes 131104 | tf_op jit(solution)/shard_map/all_to_all | solution.py:603
  138.1 1.6 %fisher.1 = (f32[8,32]{1,0:T(8,128)}, f32[32,32]{1,0:T(8,128)}) custom-call(s32[1]{0:T(128)} %bitcast.16.sim_ref, f32[128,2,128]{2,1,0:T(2,128)S(1)} %all-to-all-done.7.term_ref), custom_call_target="tpu_custom_call" | custom-call | tf_op jit(solution)/shard_map/fisher/pallas_call | solution.py:562
Async XLA Ops:
  3.6 20.3 %all-to-all-start = ((bf16[32,32,128]{2,1,0:T(8,128)(2,1)}), bf16[32,32,128]{2,1,0:T(8,128)(2,1)S(1)}, u32[]{:S(2)}, u32[]{:S(2)}) async-start(bf16[32,32,128]{2,1,0:T(8,128)(2,1)} %get-tuple-element.21), calls=%async_computation | async-start | bytes 524288 | tf_op jit(solution)/shard_map/all_to_all | solution.py:576
  11.9 29.5 %copy-start = (f32[2,8,2,4096]{3,2,1,0:T(2,128)S(1)}, f32[2,8,2,4096]{3,2,1,0:T(2,128)}, u32[]{:S(2)}) copy-start(f32[2,8,2,4096]{3,2,1,0:T(2,128)} %param.11) | copy-start | bytes 1572868
  11.9 29.5 %copy-start.1 = (f32[2,64,128]{2,1,0:T(8,128)S(1)}, f32[2,64,128]{2,1,0:T(8,128)}, u32[]{:S(2)}) copy-start(f32[2,64,128]{2,1,0:T(8,128)} %constant.19.clone.twist_ref) | copy-start | bytes 196612
  11.9 29.5 %copy-start.2 = (f32[2,4096]{1,0:T(2,128)S(1)}, f32[2,4096]{1,0:T(2,128)}, u32[]{:S(2)}) copy-start(f32[2,4096]{1,0:T(2,128)} %param.12) | copy-start | bytes 98308
  11.9 29.5 %copy-start.3 = (bf16[128,64]{1,0:T(8,128)(2,1)S(1)}, bf16[128,64]{1,0:T(8,128)(2,1)}, u32[]{:S(2)}) copy-start(bf16[128,64]{1,0:T(8,128)(2,1)} %constant.17.clone.outer_ref) | copy-start | bytes 49156
  11.9 29.5 %copy-start.4 = (bf16[64,128]{1,0:T(8,128)(2,1)S(1)}, bf16[64,128]{1,0:T(8,128)(2,1)}, u32[]{:S(2)}) copy-start(bf16[64,128]{1,0:T(8,128)(2,1)} %constant.18.clone.outer_t_ref) | copy-start | bytes 49156
  57.3 55.7 %copy-start.5 = (f32[2048]{0:T(1024)S(1)}, f32[2048]{0:T(1024)}, u32[]{:S(2)}) copy-start(f32[2048]{0:T(1024)} %param.13) | copy-start | bytes 24580
  57.3 55.7 %copy-start.6 = (s32[32,4]{0,1:T(4,128)S(1)}, s32[32,4]{0,1:T(4,128)}, u32[]{:S(2)}) copy-start(s32[32,4]{0,1:T(4,128)} %param.15) | copy-start | bytes 1540
  57.3 55.6 %copy-start.7 = (s32[2048]{0:T(1024)S(1)}, s32[2048]{0:T(1024)}, u32[]{:S(2)}) copy-start(s32[2048]{0:T(1024)} %param.17) | copy-start | bytes 24580
  57.3 55.6 %copy-start.8 = (s32[34,2]{0,1:T(2,128)S(1)}, s32[34,2]{0,1:T(2,128)}, u32[]{:S(2)}) copy-start(s32[34,2]{0,1:T(2,128)} %param.16) | copy-start | bytes 820
  122.1 16.0 %all-to-all-start.7 = ((f32[128,2,128]{2,1,0:T(2,128)}), f32[128,2,128]{2,1,0:T(2,128)S(1)}, u32[]{:S(2)}, u32[]{:S(2)}) async-start(f32[128,2,128]{2,1,0:T(2,128)} %get-tuple-element.30), calls=%async_computation.7 | async-start | bytes 262144 | tf_op jit(solution)/shard_map/all_to_all | solution.py:603

commit v6 on v5

--- a/solution.py
+++ b/solution.py
@@ -232,11 +232,16 @@
         zero_slot[s] = jnp.where(group == 0, 1, 0)
 
 
-def find_pairs(group_ref, block_ref, own_ref, order, pair_slot, pair_live, counter):
+def products_kernel(
+    group_ref, block_ref, own_ref, legendre_ref, signal_ref, out_ref,
+    table, sums, order, sequence, pair_slot, pair_live, counter, arrived,
+):
+    def place_copy(at):
+        return pltpu.make_async_copy(legendre_ref.at[order[at]], table.at[at], arrived.at[at])
+
     base = jnp.int32(0)
     for s, (slot, group) in enumerate(own_slots(group_ref, own_ref)):
-        count = 16 - group // 8
-        pairs = (count + 1) // 2
+        pairs = (17 - group // 8) // 2
         counter[s] = 2 * base
 
         def mark(pair, carry, slot=slot):
@@ -247,41 +252,31 @@
         lax.fori_loop(base, base + pairs, mark, 0)
         base = base + pairs
 
-    def place(block, carry):
+    def place(block, complete):
         slot = block_ref[0, block]
         at = counter[slot]
         order[at] = block
         counter[slot] = at + 1
-        return carry
-
-    lax.fori_loop(0, block_ref.shape[1], place, 0)
+        place_copy(at).start()
+        sequence[complete] = at // 2
+        return complete + at % 2
+
+    complete = lax.fori_loop(0, block_ref.shape[1], place, jnp.int32(0))
     for s in range(SLOTS):
         at = counter[s]
+        sequence[complete] = at // 2
 
         @pl.when(at % 2 == 1)
         def _():
             order[at] = order[at - 1]
             pair_live[at // 2] = 0
-
-
-def products_kernel(
-    group_ref, block_ref, own_ref, legendre_ref, signal_ref, out_ref,
-    table, sums, order, pair_slot, pair_live, counter, arrived,
-):
-    find_pairs(group_ref, block_ref, own_ref, order, pair_slot, pair_live, counter)
-
-    def place_copy(at):
-        return pltpu.make_async_copy(legendre_ref.at[order[at]], table.at[at], arrived.at[at])
-
-    def fetch(at, carry):
-        place_copy(at).start()
-        return carry
-
-    lax.fori_loop(0, 2 * PAIRS, fetch, 0)
+            place_copy(at).start()
+
+        complete = complete + at % 2
     sums[...] = jnp.zeros_like(sums)
 
     def pair_step(group, carry):
-        pairs = [group * PAIR_GROUP + n for n in range(PAIR_GROUP)]
+        pairs = [sequence[group * PAIR_GROUP + n] for n in range(PAIR_GROUP)]
         for pair in pairs:
             place_copy(2 * pair).wait()
             place_copy(2 * pair + 1).wait()
@@ -436,20 +431,25 @@
             total = total + term_ref[index * sims + part]
         rows_ref[2 * part : 2 * part + 2, :] = total
     values = rows_ref[...]
-    row = lax.broadcasted_iota(jnp.int32, (128, 128), 0)
-    lane = lax.broadcasted_iota(jnp.int32, (128, 128), 1)
     count = sims * 8
-    fold = jnp.where(row % BANDS == lane % BANDS, 1.0 / count, 0.0).astype(F32)
-    mean = jnp.sum(precise(values, fold), axis=0, keepdims=True)
+    total = jnp.sum(values, axis=0, keepdims=True)
+    total = jnp.broadcast_to(total, (8, 128))
+    total = total + pltpu.roll(total, 64, 1)
+    total = total + pltpu.roll(total, 32, 1)
+    mean = total[:1] * (1.0 / count)
     center = values - jnp.broadcast_to(mean, values.shape)
-    square = jnp.where(row // BANDS == lane // BANDS, precise(center, center, TN), 0.0)
-    column = lax.broadcasted_iota(jnp.int32, (128, BANDS), 0) % BANDS
-    pick = (column == lax.broadcasted_iota(jnp.int32, (128, BANDS), 1)).astype(F32)
-    fisher_out[...] = precise(precise(pick, square, TN), pick) / count
+    square = precise(center, center, TN)
+    fisher = square[:BANDS]
+    for s in range(1, 4):
+        fisher = fisher + pltpu.roll(square[s * BANDS : (s + 1) * BANDS], 128 - s * BANDS, 1)
+    fisher_out[...] = fisher[:, :BANDS] * (1.0 / count)
     own = rows_ref[pl.ds(2 * sim_ref[0], 2), :]
     own = jnp.concatenate([jnp.broadcast_to(own[h : h + 1], (4, 128)) for h in range(2)], axis=0)
-    keep = lane[:8] // BANDS == row[:8] % 4
-    band_out[...] = precise(jnp.where(keep, own, 0.0), pick)
+    row = lax.broadcasted_iota(jnp.int32, (8, 128), 0) % 4
+    band = own
+    for s in range(1, 4):
+        band = jnp.where(row == s, pltpu.roll(own, 128 - s * BANDS, 1), band)
+    band_out[...] = band[:, :BANDS]
 
 
 def params(megabytes, **more):
@@ -504,6 +504,7 @@
             pltpu.VMEM((2 * PAIRS,) + legendre.shape[1:], BF16),
             pltpu.VMEM((SLOTS * MG, 192, 64), F32),
             pltpu.SMEM((2 * PAIRS,), jnp.int32),
+            pltpu.SMEM((PAIRS + 2,), jnp.int32),
             pltpu.SMEM((PAIRS,), jnp.int32),
             pltpu.SMEM((PAIRS,), jnp.int32),
             pltpu.SMEM((SLOTS,), jnp.int32),
@@ -589,7 +590,8 @@
     bands = band_of_ell.reshape(16, 128)
 
     rows, inner, zero_rows = first_transforms(scalars[0], sky, noise, outer, twist, upper)
-    own, rows = lax.optimization_barrier((scalars[2], rows))
+    sim_index = lax.axis_index("sim").astype(jnp.int32).reshape(1)
+    own, sim_index, rows = lax.optimization_barrier((scalars[2], sim_index, rows))
     products = cycle_products(scalars[:2] + (own,), legendre, signal)
     kept = []
     for sweep in range(ITERS - 1):
@@ -601,7 +603,6 @@
     sims = lax.axis_size("sim")
     state, copies = last_step(BLK * sims, scalars, exchange(rows), kept, legendre, signal, bands)
     terms = lax.all_to_all(copies, ("blk", "sim"), 0, 0, tiled=True)
-    sim_index = lax.axis_index("sim").astype(jnp.int32).reshape(1)
     band_proj, fisher = fisher_step(sim_index, terms)
     filtered = state.reshape(block_count, MG, set_count, sim_local, 2, 128)
     return (filtered, band_proj, fisher)

time: 141 us -> 140 us (level)
  blocking collectives: 78.7 us -> 94.4 us
  waiting for transfers between devices: 9.4 us -> 0.01 us
  starting transfers between devices: 14.9 us -> 8.25 us
    all_to_all x0 -> x1, blocking collectives: none -> 15.9 us  [shards(): terms = lax.all_to_all(copies, ('blk', 'sim'), 0, 0, tiled=True)]
    all_to_all x1 -> x0, waiting for transfers between devices: 9.4 us -> none  [shards(): terms = lax.all_to_all(copies, ('blk', 'sim'), 0, 0, tiled=True)]
    all_to_all x1 -> x0, starting transfers between devices: 6.62 us -> none  [shards(): terms = lax.all_to_all(copies, ('blk', 'sim'), 0, 0, tiled=True)]
  transfers between devices with their start and end apart: 2 -> 1, of which waited for: 1 -> 0; matrix products, arithmetic and copies ran while one was open for 0% -> 0% of each run, Pallas kernels for 9% -> 8%
where the time goes in v6:
time: 140 us; the launch traced here: 138 us
  blocking collectives  94.4 us (67%)
  Pallas kernels  34.4 us (25%)
  starting transfers between devices  8.25 us (6%)
    all_to_all x6, blocking collectives, exchange(): return lax.all_to_all(rows, 'blk', 0, 0, tiled=True)  78.5 us
    all_to_all x1, blocking collectives, shards(): terms = lax.all_to_all(copies, ('blk', 'sim'), 0, 0, tiled=True)  15.9 us
    pallas_call x1, Pallas kernels, cycle_products(): pl.pallas_call(products_kernel, out_shape=jax.ShapeDtypeStruct((8, 512, 1...  11.7 us
    pallas_call x1, Pallas kernels, last_step(): pl.pallas_call(last_kernel, out_shape=(jax.ShapeDtypeStruct((legendre.sha...  8.42 us
    all_to_all x1, starting transfers between devices, exchange(): return lax.all_to_all(rows, 'blk', 0, 0, tiled=True)  8.25 us
    pallas_call x3, Pallas kernels, row_transforms(): pl.pallas_call(rows_kernel, out_shape=SENT, scratch_shapes=row_scratch(),...  6.46 us
    pallas_call x3, Pallas kernels, apply_products(): pl.pallas_call(body, out_shape=(KEPT, SENT), scratch_shapes=[pltpu.VMEM((...  3.76 us
    pallas_call x1, Pallas kernels, first_transforms(): pl.pallas_call(first_rows_kernel, out_shape=(SENT, jax.ShapeDtypeStruct((...  2.98 us
  transfers between devices with their start and end apart: 1, of which 0 were waited for; matrix products, arithmetic and copies ran while one was open for 0% of the time, Pallas kernels for 8%

profile of v6, /device:TPU:0, one launch (start us, length us, event | category | flops | bytes accessed | tf_op | source)
XLA Modules:
  0.0 138.0 jit_solution(6373247117624288694)
XLA Ops:
  0.6 3.0 %first_rows.1 = (bf16[32,32,128]{2,1,0:T(8,128)(2,1)}, bf16[2,128,256]{2,1,0:T(8,128)(2,1)S(1)}, f32[128,128]{1,0:T(8,128)S(1)}) custom-call(s32[4,32]{1,0:T(4,128)} %bitcast.27, f32[16,64,128]{2,1,0:T(8,128)} %bitcast.17, f32[64,128]{1,0:T(8,128)} %bitcast.21, bf16[128,64]{1,0:T(8,128)(2,1)} %constant.17.clone.outer_ref, ...), custom_call_target="tpu_custom_call" | custom-call | tf_op jit(solution)/shard_map/first_rows/pallas_call | solution.py:475
  3.6 8.3 %all-to-all-start = ((bf16[32,32,128]{2,1,0:T(8,128)(2,1)}), bf16[32,32,128]{2,1,0:T(8,128)(2,1)S(1)}, u32[]{:S(2)}, u32[]{:S(2)}) async-start(bf16[32,32,128]{2,1,0:T(8,128)(2,1)} %get-tuple-element.22), calls=%async_computation | async-start | bytes 524288 | tf_op jit(solution)/shard_map/all_to_all | solution.py:577
  11.9 0.0 copy-start
  11.9 0.0 copy-start.1
  11.9 0.0 copy-start.2
  11.9 0.0 copy-start.3
  11.9 0.0 copy-start.4
  11.9 11.7 %cycle_products.1.refs_1_ = bf16[8,512,192]{2,1,0:T(8,128)(2,1)S(1)} custom-call(s32[4,32]{1,0:T(4,128)} %bitcast.28, s32[2,34]{1,0:T(2,128)} %bitcast.31, s32[1]{0:T(128)} %bitcast.2.own_ref, bf16[34,16,64,128]{3,2,1,0:T(8,128)(2,1)} %legendre_ref.3, f32[16,128]{1,0:T(8,128)} %bitcast.25), custom_call_target="tpu_custom_call" | custom-call | tf_op jit(solution)/shard_map/cycle_products/pallas_call | solution.py:499
  23.6 0.0 all-to-all-done.refs_0_
  23.6 1.2 apply_products_1.1
  24.8 16.0 %all_to_all.40.coeff_ref = bf16[32,32,128]{2,1,0:T(8,128)(2,1)S(1)} all-to-all(bf16[32,32,128]{2,1,0:T(8,128)(2,1)S(1)} %get-tuple-element.24), channel_id=1, replica_groups=mesh['blk'=32,'sim'=4] {'blk'}, dimensions={0} | all-to-all | bytes 524288 | tf_op jit(solution)/shard_map/all_to_all | solution.py:577
  40.8 0.0 copy-done
  40.8 0.0 copy-done.1
  40.8 0.0 copy-done.2
  40.9 0.0 copy-done.3
  40.9 0.0 copy-done.4
  40.9 2.2 %rows.3 = bf16[32,32,128]{2,1,0:T(8,128)(2,1)S(1)} custom-call(f32[16,64,128]{2,1,0:T(8,128)S(1)} %bitcast.18, f32[64,128]{1,0:T(8,128)S(1)} %bitcast.22, bf16[128,64]{1,0:T(8,128)(2,1)S(1)} %copy-done.3, bf16[64,128]{1,0:T(8,128)(2,1)S(1)} %copy-done.4, f32[2,64,128]{2,1,0:T(8,128)S(1)} %copy-done.1, bf16[2,128,256]{2,1,0:T(8,128)(2,1)S(1)} %get-tuple-element.19.inner_ref, ...), custom_call_target="tpu_custom_call" | custom-call | tf_op jit(solution)/shard_map/rows/pallas_call | solution.py:489
  43.0 12.5 %all_to_all.41.refs_0_ = bf16[32,32,128]{2,1,0:T(8,128)(2,1)S(1)} all-to-all(bf16[32,32,128]{2,1,0:T(8,128)(2,1)S(1)} %rows.3), channel_id=1, replica_groups=mesh['blk'=32,'sim'=4] {'blk'}, dimensions={0} | all-to-all | bytes 524288 | tf_op jit(solution)/shard_map/all_to_all | solution.py:577
  55.5 1.3 apply_products_2.1
  56.7 0.0 copy-start.5
  56.8 0.0 copy-start.6
  56.8 0.0 copy-start.7
  56.8 0.0 copy-start.8
  56.8 12.6 %all_to_all.42.coeff_ref = bf16[32,32,128]{2,1,0:T(8,128)(2,1)S(1)} all-to-all(bf16[32,32,128]{2,1,0:T(8,128)(2,1)S(1)} %get-tuple-element.26), channel_id=1, replica_groups=mesh['blk'=32,'sim'=4] {'blk'}, dimensions={0} | all-to-all | bytes 524288 | tf_op jit(solution)/shard_map/all_to_all | solution.py:577
  69.4 2.2 %rows.4 = bf16[32,32,128]{2,1,0:T(8,128)(2,1)S(1)} custom-call(f32[16,64,128]{2,1,0:T(8,128)S(1)} %bitcast.19, f32[64,128]{1,0:T(8,128)S(1)} %bitcast.23, bf16[128,64]{1,0:T(8,128)(2,1)S(1)} %copy-done.3, bf16[64,128]{1,0:T(8,128)(2,1)S(1)} %copy-done.4, f32[2,64,128]{2,1,0:T(8,128)S(1)} %copy-done.1, bf16[2,128,256]{2,1,0:T(8,128)(2,1)S(1)} %get-tuple-element.19.inner_ref, ...), custom_call_target="tpu_custom_call" | custom-call | tf_op jit(solution)/shard_map/rows/pallas_call | solution.py:489
  71.6 12.5 %all_to_all.43.refs_0_ = bf16[32,32,128]{2,1,0:T(8,128)(2,1)S(1)} all-to-all(bf16[32,32,128]{2,1,0:T(8,128)(2,1)S(1)} %rows.4), channel_id=1, replica_groups=mesh['blk'=32,'sim'=4] {'blk'}, dimensions={0} | all-to-all | bytes 524288 | tf_op jit(solution)/shard_map/all_to_all | solution.py:577
  84.0 1.3 apply_products_3.1
  85.4 12.5 %all_to_all.44.coeff_ref = bf16[32,32,128]{2,1,0:T(8,128)(2,1)S(1)} all-to-all(bf16[32,32,128]{2,1,0:T(8,128)(2,1)S(1)} %get-tuple-element.28), channel_id=1, replica_groups=mesh['blk'=32,'sim'=4] {'blk'}, dimensions={0} | all-to-all | bytes 524288 | tf_op jit(solution)/shard_map/all_to_all | solution.py:577
  97.8 2.1 %rows.5 = bf16[32,32,128]{2,1,0:T(8,128)(2,1)S(1)} custom-call(f32[16,64,128]{2,1,0:T(8,128)S(1)} %bitcast.20, f32[64,128]{1,0:T(8,128)S(1)} %bitcast.24, bf16[128,64]{1,0:T(8,128)(2,1)S(1)} %copy-done.3, bf16[64,128]{1,0:T(8,128)(2,1)S(1)} %copy-done.4, f32[2,64,128]{2,1,0:T(8,128)S(1)} %copy-done.1, bf16[2,128,256]{2,1,0:T(8,128)(2,1)S(1)} %get-tuple-element.19.inner_ref, ...), custom_call_target="tpu_custom_call" | custom-call | tf_op jit(solution)/shard_map/rows/pallas_call | solution.py:489
  100.0 12.5 %all_to_all.45.coeff_ref = bf16[32,32,128]{2,1,0:T(8,128)(2,1)S(1)} all-to-all(bf16[32,32,128]{2,1,0:T(8,128)(2,1)S(1)} %rows.5), channel_id=1, replica_groups=mesh['blk'=32,'sim'=4] {'blk'}, dimensions={0} | all-to-all | bytes 524288 | tf_op jit(solution)/shard_map/all_to_all | solution.py:577
  112.4 0.0 copy-done.5
  112.4 0.0 copy-done.6
  112.4 0.0 copy-done.7
  112.4 0.0 copy-done.8
  112.4 8.4 %last_modes.1 = (bf16[34,512,128]{2,1,0:T(8,128)(2,1)}, f32[128,2,128]{2,1,0:T(2,128)S(1)}) custom-call(s32[4,32]{1,0:T(4,128)S(1)} %bitcast.29, s32[2,34]{1,0:T(2,128)S(1)} %bitcast.32, s32[1]{0:T(128)} %bitcast.2.own_ref, bf16[32,32,128]{2,1,0:T(8,128)(2,1)S(1)} %all_to_all.45.coeff_ref, bf16[16,64,128]{2,1,0:T(8,128)(2,1)S(1)} %get-tuple-element.25.refs_2_.kept0_ref, ...), custom_call_target="tpu_custom_call" | custom-call | tf_op jit(solution)/shard_map/last_modes/pallas_call | solution.py:535
  120.9 15.9 %all_to_all.46.term_ref = f32[128,2,128]{2,1,0:T(2,128)S(1)} all-to-all(f32[128,2,128]{2,1,0:T(2,128)S(1)} %get-tuple-element.32), channel_id=1, replica_groups=mesh['blk'=32,'sim'=4] {'blk','sim'}, dimensions={0} | all-to-all | bytes 262144 | tf_op jit(solution)/shard_map/all_to_all | solution.py:605
  136.8 1.2 fisher.1
Async XLA Ops:
  3.6 20.0 %all-to-all-start = ((bf16[32,32,128]{2,1,0:T(8,128)(2,1)}), bf16[32,32,128]{2,1,0:T(8,128)(2,1)S(1)}, u32[]{:S(2)}, u32[]{:S(2)}) async-start(bf16[32,32,128]{2,1,0:T(8,128)(2,1)} %get-tuple-element.22), calls=%async_computation | async-start | bytes 524288 | tf_op jit(solution)/shard_map/all_to_all | solution.py:577
  11.9 29.0 %copy-start = (f32[2,8,2,4096]{3,2,1,0:T(2,128)S(1)}, f32[2,8,2,4096]{3,2,1,0:T(2,128)}, u32[]{:S(2)}) copy-start(f32[2,8,2,4096]{3,2,1,0:T(2,128)} %param.11) | copy-start | bytes 1572868
  11.9 29.0 %copy-start.1 = (f32[2,64,128]{2,1,0:T(8,128)S(1)}, f32[2,64,128]{2,1,0:T(8,128)}, u32[]{:S(2)}) copy-start(f32[2,64,128]{2,1,0:T(8,128)} %constant.19.clone.twist_ref) | copy-start | bytes 196612
  11.9 29.0 %copy-start.2 = (f32[2,4096]{1,0:T(2,128)S(1)}, f32[2,4096]{1,0:T(2,128)}, u32[]{:S(2)}) copy-start(f32[2,4096]{1,0:T(2,128)} %param.12) | copy-start | bytes 98308
  11.9 28.9 %copy-start.3 = (bf16[128,64]{1,0:T(8,128)(2,1)S(1)}, bf16[128,64]{1,0:T(8,128)(2,1)}, u32[]{:S(2)}) copy-start(bf16[128,64]{1,0:T(8,128)(2,1)} %constant.17.clone.outer_ref) | copy-start | bytes 49156
  11.9 28.9 %copy-start.4 = (bf16[64,128]{1,0:T(8,128)(2,1)S(1)}, bf16[64,128]{1,0:T(8,128)(2,1)}, u32[]{:S(2)}) copy-start(bf16[64,128]{1,0:T(8,128)(2,1)} %constant.18.clone.outer_t_ref) | copy-start | bytes 49156
  56.7 55.7 %copy-start.5 = (f32[2048]{0:T(1024)S(1)}, f32[2048]{0:T(1024)}, u32[]{:S(2)}) copy-start(f32[2048]{0:T(1024)} %param.13) | copy-start | bytes 24580
  56.8 55.7 %copy-start.6 = (s32[32,4]{0,1:T(4,128)S(1)}, s32[32,4]{0,1:T(4,128)}, u32[]{:S(2)}) copy-start(s32[32,4]{0,1:T(4,128)} %param.15) | copy-start | bytes 1540
  56.8 55.7 %copy-start.7 = (s32[2048]{0:T(1024)S(1)}, s32[2048]{0:T(1024)}, u32[]{:S(2)}) copy-start(s32[2048]{0:T(1024)} %param.17) | copy-start | bytes 24580
  56.8 55.7 %copy-start.8 = (s32[34,2]{0,1:T(2,128)S(1)}, s32[34,2]{0,1:T(2,128)}, u32[]{:S(2)}) copy-start(s32[34,2]{0,1:T(2,128)} %param.16) | copy-start | bytes 820

commit v7 on v6

--- a/solution.py
+++ b/solution.py
@@ -19,7 +19,7 @@
 MG = 16
 SLOTS = 4
 PAIRS = 18
-PAIR_GROUP = 3
+PAIR_GROUP = 6
 GROUP = 6
 F32 = jnp.float32
 BF16 = jnp.bfloat16
@@ -290,22 +290,24 @@
             precond = jnp.concatenate(precond, axis=1)
             lane = lax.broadcasted_iota(jnp.int32, (1, 256), 1)
             weight = precond * jnp.where(lane < 128, 1.0, live)
-            weights = []
-            for _ in range(ITERS - 1):
-                weights.append(jnp.broadcast_to(weight, (64, 256)))
-                weight = weight * (2.0 * precond)
+            weights = [weight, weight * (2.0 * precond)]
+            weights = [jnp.broadcast_to(w, (64, 256)) for w in weights]
             for i in range(MG):
                 values = jnp.concatenate([table[2 * pair, i], table[2 * pair + 1, i]], axis=1)
                 wide = values.astype(F32)
-                scaled = jnp.concatenate([(wide * w).astype(BF16) for w in weights], axis=0)
-                sums[slot * MG + i] += dot(scaled, values, NT)
+                once, twice = [(wide * w).astype(BF16) for w in weights]
+                left = jnp.concatenate([once, twice], axis=0)
+                right = jnp.concatenate([values, once], axis=0)
+                sums[slot * MG + i] += dot(left, right, NT)
         return carry
 
     lax.fori_loop(0, PAIRS // PAIR_GROUP, pair_step, 0)
+    lane = lax.broadcasted_iota(jnp.int32, (64, 128), 1)
+    double = jnp.where(lane < 64, 1.0, 2.0)
     for at in range(SLOTS * MG):
-        out_ref[at // 8, (at % 8) * 64 : (at % 8 + 1) * 64, :] = jnp.concatenate(
-            [sums[at, n * 64 : (n + 1) * 64] for n in range(ITERS - 1)], axis=1
-        ).astype(BF16)
+        rows = slice((at % 8) * 64, (at % 8 + 1) * 64)
+        out_ref[at // 8, rows, 0:128] = (sums[at, 0:64] * double).astype(BF16)
+        out_ref[at // 8, rows, 128:192] = pltpu.roll(2.0 * sums[at, 64:128], 64, 1)[:, :64].astype(BF16)
 
 
 def apply_kernel(count, *refs):
@@ -502,7 +504,7 @@
         in_specs=[SMEM, SMEM, SMEM, ANY, VMEM],
         scratch_shapes=[
             pltpu.VMEM((2 * PAIRS,) + legendre.shape[1:], BF16),
-            pltpu.VMEM((SLOTS * MG, 192, 64), F32),
+            pltpu.VMEM((SLOTS * MG, 128, 128), F32),
             pltpu.SMEM((2 * PAIRS,), jnp.int32),
             pltpu.SMEM((PAIRS + 2,), jnp.int32),
             pltpu.SMEM((PAIRS,), jnp.int32),

time: 140 us -> 137 us (0.979)
  Pallas kernels: 34.4 us -> 32.2 us
    pallas_call x1, Pallas kernels: 11.7 us -> 9.43 us  [cycle_products(): pl.pallas_call(products_kernel, out_shape=jax.ShapeDtypeStruct((8, 512, 1...]
  transfers between devices with their start and end apart: 1 -> 1, of which waited for: 0 -> 0; matrix products, arithmetic and copies ran while one was open for 0% -> 0% of each run, Pallas kernels for 8% -> 7%
where the time goes in v7:
time: 137 us; the launch traced here: 136 us
  blocking collectives  94.5 us (69%)
  Pallas kernels  32.2 us (24%)
  starting transfers between devices  8.25 us (6%)
    all_to_all x6, blocking collectives, exchange(): return lax.all_to_all(rows, 'blk', 0, 0, tiled=True)  78.5 us
    all_to_all x1, blocking collectives, shards(): terms = lax.all_to_all(copies, ('blk', 'sim'), 0, 0, tiled=True)  15.9 us
    pallas_call x1, Pallas kernels, cycle_products(): pl.pallas_call(products_kernel, out_shape=jax.ShapeDtypeStruct((8, 512, 1...  9.43 us
    pallas_call x1, Pallas kernels, last_step(): pl.pallas_call(last_kernel, out_shape=(jax.ShapeDtypeStruct((legendre.sha...  8.42 us
    all_to_all x1, starting transfers between devices, exchange(): return lax.all_to_all(rows, 'blk', 0, 0, tiled=True)  8.25 us
    pallas_call x3, Pallas kernels, row_transforms(): pl.pallas_call(rows_kernel, out_shape=SENT, scratch_shapes=row_scratch(),...  6.45 us
    pallas_call x3, Pallas kernels, apply_products(): pl.pallas_call(body, out_shape=(KEPT, SENT), scratch_shapes=[pltpu.VMEM((...  3.76 us
    pallas_call x1, Pallas kernels, first_transforms(): pl.pallas_call(first_rows_kernel, out_shape=(SENT, jax.ShapeDtypeStruct((...  2.98 us
  transfers between devices with their start and end apart: 1, of which 0 were waited for; matrix products, arithmetic and copies ran while one was open for 0% of the time, Pallas kernels for 7%

profile of v7, /device:TPU:0, one launch (start us, length us, event | category | flops | bytes accessed | tf_op | source)
XLA Modules:
  0.0 135.8 jit_solution(18355106257866957167)
XLA Ops:
  0.6 3.0 %first_rows.1 = (bf16[32,32,128]{2,1,0:T(8,128)(2,1)}, bf16[2,128,256]{2,1,0:T(8,128)(2,1)S(1)}, f32[128,128]{1,0:T(8,128)S(1)}) custom-call(s32[4,32]{1,0:T(4,128)} %bitcast.27, f32[16,64,128]{2,1,0:T(8,128)} %bitcast.17, f32[64,128]{1,0:T(8,128)} %bitcast.21, bf16[128,64]{1,0:T(8,128)(2,1)} %constant.17.clone.outer_ref, ...), custom_call_target="tpu_custom_call" | custom-call | tf_op jit(solution)/shard_map/first_rows/pallas_call | solution.py:477
  3.6 8.3 %all-to-all-start = ((bf16[32,32,128]{2,1,0:T(8,128)(2,1)}), bf16[32,32,128]{2,1,0:T(8,128)(2,1)S(1)}, u32[]{:S(2)}, u32[]{:S(2)}) async-start(bf16[32,32,128]{2,1,0:T(8,128)(2,1)} %get-tuple-element.22), calls=%async_computation | async-start | bytes 524288 | tf_op jit(solution)/shard_map/all_to_all | solution.py:579
  11.9 0.0 copy-start
  11.9 0.0 copy-start.1
  11.9 0.0 copy-start.2
  11.9 0.0 copy-start.3
  11.9 0.0 copy-start.4
  11.9 9.4 %cycle_products.1.refs_1_ = bf16[8,512,192]{2,1,0:T(8,128)(2,1)S(1)} custom-call(s32[4,32]{1,0:T(4,128)} %bitcast.28, s32[2,34]{1,0:T(2,128)} %bitcast.31, s32[1]{0:T(128)} %bitcast.2.own_ref, bf16[34,16,64,128]{3,2,1,0:T(8,128)(2,1)} %legendre_ref.3, f32[16,128]{1,0:T(8,128)} %bitcast.25), custom_call_target="tpu_custom_call" | custom-call | tf_op jit(solution)/shard_map/cycle_products/pallas_call | solution.py:501
  21.4 0.0 all-to-all-done.refs_0_
  21.4 1.2 apply_products_1.1
  22.6 16.1 %all_to_all.40.coeff_ref = bf16[32,32,128]{2,1,0:T(8,128)(2,1)S(1)} all-to-all(bf16[32,32,128]{2,1,0:T(8,128)(2,1)S(1)} %get-tuple-element.24), channel_id=1, replica_groups=mesh['blk'=32,'sim'=4] {'blk'}, dimensions={0} | all-to-all | bytes 524288 | tf_op jit(solution)/shard_map/all_to_all | solution.py:579
  38.7 0.0 copy-done
  38.7 0.0 copy-done.1
  38.7 0.0 copy-done.2
  38.7 0.0 copy-done.3
  38.7 0.0 copy-done.4
  38.7 2.1 %rows.3 = bf16[32,32,128]{2,1,0:T(8,128)(2,1)S(1)} custom-call(f32[16,64,128]{2,1,0:T(8,128)S(1)} %bitcast.18, f32[64,128]{1,0:T(8,128)S(1)} %bitcast.22, bf16[128,64]{1,0:T(8,128)(2,1)S(1)} %copy-done.3, bf16[64,128]{1,0:T(8,128)(2,1)S(1)} %copy-done.4, f32[2,64,128]{2,1,0:T(8,128)S(1)} %copy-done.1, bf16[2,128,256]{2,1,0:T(8,128)(2,1)S(1)} %get-tuple-element.19.inner_ref, ...), custom_call_target="tpu_custom_call" | custom-call | tf_op jit(solution)/shard_map/rows/pallas_call | solution.py:491
  40.9 12.5 %all_to_all.41.refs_0_ = bf16[32,32,128]{2,1,0:T(8,128)(2,1)S(1)} all-to-all(bf16[32,32,128]{2,1,0:T(8,128)(2,1)S(1)} %rows.3), channel_id=1, replica_groups=mesh['blk'=32,'sim'=4] {'blk'}, dimensions={0} | all-to-all | bytes 524288 | tf_op jit(solution)/shard_map/all_to_all | solution.py:579
  53.3 1.3 apply_products_2.1
  54.6 0.0 copy-start.5
  54.6 0.0 copy-start.6
  54.6 0.0 copy-start.7
  54.6 0.0 copy-start.8
  54.6 12.6 %all_to_all.42.coeff_ref = bf16[32,32,128]{2,1,0:T(8,128)(2,1)S(1)} all-to-all(bf16[32,32,128]{2,1,0:T(8,128)(2,1)S(1)} %get-tuple-element.26), channel_id=1, replica_groups=mesh['blk'=32,'sim'=4] {'blk'}, dimensions={0} | all-to-all | bytes 524288 | tf_op jit(solution)/shard_map/all_to_all | solution.py:579
  67.2 2.2 %rows.4 = bf16[32,32,128]{2,1,0:T(8,128)(2,1)S(1)} custom-call(f32[16,64,128]{2,1,0:T(8,128)S(1)} %bitcast.19, f32[64,128]{1,0:T(8,128)S(1)} %bitcast.23, bf16[128,64]{1,0:T(8,128)(2,1)S(1)} %copy-done.3, bf16[64,128]{1,0:T(8,128)(2,1)S(1)} %copy-done.4, f32[2,64,128]{2,1,0:T(8,128)S(1)} %copy-done.1, bf16[2,128,256]{2,1,0:T(8,128)(2,1)S(1)} %get-tuple-element.19.inner_ref, ...), custom_call_target="tpu_custom_call" | custom-call | tf_op jit(solution)/shard_map/rows/pallas_call | solution.py:491
  69.4 12.5 %all_to_all.43.refs_0_ = bf16[32,32,128]{2,1,0:T(8,128)(2,1)S(1)} all-to-all(bf16[32,32,128]{2,1,0:T(8,128)(2,1)S(1)} %rows.4), channel_id=1, replica_groups=mesh['blk'=32,'sim'=4] {'blk'}, dimensions={0} | all-to-all | bytes 524288 | tf_op jit(solution)/shard_map/all_to_all | solution.py:579
  81.8 1.3 apply_products_3.1
  83.2 12.5 %all_to_all.44.coeff_ref = bf16[32,32,128]{2,1,0:T(8,128)(2,1)S(1)} all-to-all(bf16[32,32,128]{2,1,0:T(8,128)(2,1)S(1)} %get-tuple-element.28), channel_id=1, replica_groups=mesh['blk'=32,'sim'=4] {'blk'}, dimensions={0} | all-to-all | bytes 524288 | tf_op jit(solution)/shard_map/all_to_all | solution.py:579
  95.6 2.1 %rows.5 = bf16[32,32,128]{2,1,0:T(8,128)(2,1)S(1)} custom-call(f32[16,64,128]{2,1,0:T(8,128)S(1)} %bitcast.20, f32[64,128]{1,0:T(8,128)S(1)} %bitcast.24, bf16[128,64]{1,0:T(8,128)(2,1)S(1)} %copy-done.3, bf16[64,128]{1,0:T(8,128)(2,1)S(1)} %copy-done.4, f32[2,64,128]{2,1,0:T(8,128)S(1)} %copy-done.1, bf16[2,128,256]{2,1,0:T(8,128)(2,1)S(1)} %get-tuple-element.19.inner_ref, ...), custom_call_target="tpu_custom_call" | custom-call | tf_op jit(solution)/shard_map/rows/pallas_call | solution.py:491
  97.8 12.5 %all_to_all.45.coeff_ref = bf16[32,32,128]{2,1,0:T(8,128)(2,1)S(1)} all-to-all(bf16[32,32,128]{2,1,0:T(8,128)(2,1)S(1)} %rows.5), channel_id=1, replica_groups=mesh['blk'=32,'sim'=4] {'blk'}, dimensions={0} | all-to-all | bytes 524288 | tf_op jit(solution)/shard_map/all_to_all | solution.py:579
  110.3 0.0 copy-done.5
  110.3 0.0 copy-done.6
  110.3 0.0 copy-done.7
  110.3 0.0 copy-done.8
  110.3 8.4 %last_modes.1 = (bf16[34,512,128]{2,1,0:T(8,128)(2,1)}, f32[128,2,128]{2,1,0:T(2,128)S(1)}) custom-call(s32[4,32]{1,0:T(4,128)S(1)} %bitcast.29, s32[2,34]{1,0:T(2,128)S(1)} %bitcast.32, s32[1]{0:T(128)} %bitcast.2.own_ref, bf16[32,32,128]{2,1,0:T(8,128)(2,1)S(1)} %all_to_all.45.coeff_ref, bf16[16,64,128]{2,1,0:T(8,128)(2,1)S(1)} %get-tuple-element.25.refs_2_.kept0_ref, ...), custom_call_target="tpu_custom_call" | custom-call | tf_op jit(solution)/shard_map/last_modes/pallas_call | solution.py:537
  118.7 15.9 %all_to_all.46.term_ref = f32[128,2,128]{2,1,0:T(2,128)S(1)} all-to-all(f32[128,2,128]{2,1,0:T(2,128)S(1)} %get-tuple-element.32), channel_id=1, replica_groups=mesh['blk'=32,'sim'=4] {'blk','sim'}, dimensions={0} | all-to-all | bytes 262144 | tf_op jit(solution)/shard_map/all_to_all | solution.py:607
  134.7 1.1 fisher.1
Async XLA Ops:
  3.6 17.8 %all-to-all-start = ((bf16[32,32,128]{2,1,0:T(8,128)(2,1)}), bf16[32,32,128]{2,1,0:T(8,128)(2,1)S(1)}, u32[]{:S(2)}, u32[]{:S(2)}) async-start(bf16[32,32,128]{2,1,0:T(8,128)(2,1)} %get-tuple-element.22), calls=%async_computation | async-start | bytes 524288 | tf_op jit(solution)/shard_map/all_to_all | solution.py:579
  11.9 26.8 %copy-start = (f32[2,8,2,4096]{3,2,1,0:T(2,128)S(1)}, f32[2,8,2,4096]{3,2,1,0:T(2,128)}, u32[]{:S(2)}) copy-start(f32[2,8,2,4096]{3,2,1,0:T(2,128)} %param.11) | copy-start | bytes 1572868
  11.9 26.8 %copy-start.1 = (f32[2,64,128]{2,1,0:T(8,128)S(1)}, f32[2,64,128]{2,1,0:T(8,128)}, u32[]{:S(2)}) copy-start(f32[2,64,128]{2,1,0:T(8,128)} %constant.19.clone.twist_ref) | copy-start | bytes 196612
  11.9 26.8 %copy-start.2 = (f32[2,4096]{1,0:T(2,128)S(1)}, f32[2,4096]{1,0:T(2,128)}, u32[]{:S(2)}) copy-start(f32[2,4096]{1,0:T(2,128)} %param.12) | copy-start | bytes 98308
  11.9 26.8 %copy-start.3 = (bf16[128,64]{1,0:T(8,128)(2,1)S(1)}, bf16[128,64]{1,0:T(8,128)(2,1)}, u32[]{:S(2)}) copy-start(bf16[128,64]{1,0:T(8,128)(2,1)} %constant.17.clone.outer_ref) | copy-start | bytes 49156
  11.9 26.8 %copy-start.4 = (bf16[64,128]{1,0:T(8,128)(2,1)S(1)}, bf16[64,128]{1,0:T(8,128)(2,1)}, u32[]{:S(2)}) copy-start(bf16[64,128]{1,0:T(8,128)(2,1)} %constant.18.clone.outer_t_ref) | copy-start | bytes 49156
  54.6 55.7 %copy-start.5 = (f32[2048]{0:T(1024)S(1)}, f32[2048]{0:T(1024)}, u32[]{:S(2)}) copy-start(f32[2048]{0:T(1024)} %param.13) | copy-start | bytes 24580
  54.6 55.7 %copy-start.6 = (s32[32,4]{0,1:T(4,128)S(1)}, s32[32,4]{0,1:T(4,128)}, u32[]{:S(2)}) copy-start(s32[32,4]{0,1:T(4,128)} %param.15) | copy-start | bytes 1540
  54.6 55.7 %copy-start.7 = (s32[2048]{0:T(1024)S(1)}, s32[2048]{0:T(1024)}, u32[]{:S(2)}) copy-start(s32[2048]{0:T(1024)} %param.17) | copy-start | bytes 24580
  54.6 55.7 %copy-start.8 = (s32[34,2]{0,1:T(2,128)S(1)}, s32[34,2]{0,1:T(2,128)}, u32[]{:S(2)}) copy-start(s32[34,2]{0,1:T(2,128)} %param.16) | copy-start | bytes 820

commit v8 on v7

--- a/solution.py
+++ b/solution.py
@@ -426,14 +426,12 @@
 
 
 def fisher_kernel(sim_ref, term_ref, band_out, fisher_out, rows_ref):
-    sims = term_ref.shape[0] // BLK
-    for part in range(sims):
-        total = term_ref[part]
-        for index in range(1, BLK):
-            total = total + term_ref[index * sims + part]
-        rows_ref[2 * part : 2 * part + 2, :] = total
-    values = rows_ref[...]
-    count = sims * 8
+    total = term_ref[0]
+    for index in range(1, BLK):
+        total = total + term_ref[index]
+    rows_ref[...] = total
+    values = total
+    count = values.shape[0] * 4
     total = jnp.sum(values, axis=0, keepdims=True)
     total = jnp.broadcast_to(total, (8, 128))
     total = total + pltpu.roll(total, 64, 1)
@@ -569,7 +567,7 @@
             jax.ShapeDtypeStruct((BANDS, BANDS), F32),
         ),
         in_specs=[SMEM, VMEM],
-        scratch_shapes=[pltpu.VMEM((terms.shape[0] // BLK * 2, 128), F32)],
+        scratch_shapes=[pltpu.VMEM(terms.shape[1:], F32)],
         compiler_params=params(28),
         name="fisher",
     )(sim_index, terms)
@@ -605,7 +603,7 @@
     sims = lax.axis_size("sim")
     state, copies = last_step(BLK * sims, scalars, exchange(rows), kept, legendre, signal, bands)
     terms = lax.all_to_all(copies, ("blk", "sim"), 0, 0, tiled=True)
-    band_proj, fisher = fisher_step(sim_index, terms)
+    band_proj, fisher = fisher_step(sim_index, terms.reshape(BLK, 2 * sims, 128))
     filtered = state.reshape(block_count, MG, set_count, sim_local, 2, 128)
     return (filtered, band_proj, fisher)
 

time: 137 us -> 138 us (level)
  no operation moved by 1% of the time
where the time goes in v8:
time: 138 us; the launch traced here: 136 us
  blocking collectives  94.6 us (69%)
  Pallas kernels  32.2 us (23%)
  starting transfers between devices  8.25 us (6%)
    all_to_all x6, blocking collectives, exchange(): return lax.all_to_all(rows, 'blk', 0, 0, tiled=True)  78.6 us
    all_to_all x1, blocking collectives, shards(): terms = lax.all_to_all(copies, ('blk', 'sim'), 0, 0, tiled=True)  15.9 us
    pallas_call x1, Pallas kernels, cycle_products(): pl.pallas_call(products_kernel, out_shape=jax.ShapeDtypeStruct((8, 512, 1...  9.43 us
    pallas_call x1, Pallas kernels, last_step(): pl.pallas_call(last_kernel, out_shape=(jax.ShapeDtypeStruct((legendre.sha...  8.43 us
    all_to_all x1, starting transfers between devices, exchange(): return lax.all_to_all(rows, 'blk', 0, 0, tiled=True)  8.25 us
    pallas_call x3, Pallas kernels, row_transforms(): pl.pallas_call(rows_kernel, out_shape=SENT, scratch_shapes=row_scratch(),...  6.46 us
    pallas_call x3, Pallas kernels, apply_products(): pl.pallas_call(body, out_shape=(KEPT, SENT), scratch_shapes=[pltpu.VMEM((...  3.76 us
    pallas_call x1, Pallas kernels, first_transforms(): pl.pallas_call(first_rows_kernel, out_shape=(SENT, jax.ShapeDtypeStruct((...  2.98 us
  transfers between devices with their start and end apart: 1, of which 0 were waited for; matrix products, arithmetic and copies ran while one was open for 0% of the time, Pallas kernels for 7%

profile of v8, /device:TPU:0, one launch (start us, length us, event | category | flops | bytes accessed | tf_op | source)
XLA Modules:
  0.0 135.9 jit_solution(6782595768485940589)
XLA Ops:
  0.6 3.0 %first_rows.1 = (bf16[32,32,128]{2,1,0:T(8,128)(2,1)}, bf16[2,128,256]{2,1,0:T(8,128)(2,1)S(1)}, f32[128,128]{1,0:T(8,128)S(1)}) custom-call(s32[4,32]{1,0:T(4,128)} %bitcast.29, f32[16,64,128]{2,1,0:T(8,128)} %bitcast.18, f32[64,128]{1,0:T(8,128)} %bitcast.22, bf16[128,64]{1,0:T(8,128)(2,1)} %constant.17.clone.outer_ref, ...), custom_call_target="tpu_custom_call" | custom-call | tf_op jit(solution)/shard_map/first_rows/pallas_call | solution.py:475
  3.6 8.3 %all-to-all-start = ((bf16[32,32,128]{2,1,0:T(8,128)(2,1)}), bf16[32,32,128]{2,1,0:T(8,128)(2,1)S(1)}, u32[]{:S(2)}, u32[]{:S(2)}) async-start(bf16[32,32,128]{2,1,0:T(8,128)(2,1)} %get-tuple-element.22), calls=%async_computation | async-start | bytes 524288 | tf_op jit(solution)/shard_map/all_to_all | solution.py:577
  11.9 0.0 copy-start
  11.9 0.0 copy-start.1
  11.9 0.0 copy-start.2
  11.9 0.0 copy-start.3
  11.9 0.0 copy-start.4
  11.9 9.4 %cycle_products.1.refs_1_ = bf16[8,512,192]{2,1,0:T(8,128)(2,1)S(1)} custom-call(s32[4,32]{1,0:T(4,128)} %bitcast.30, s32[2,34]{1,0:T(2,128)} %bitcast.33, s32[1]{0:T(128)} %bitcast.2.own_ref, bf16[34,16,64,128]{3,2,1,0:T(8,128)(2,1)} %legendre_ref.3, f32[16,128]{1,0:T(8,128)} %bitcast.27), custom_call_target="tpu_custom_call" | custom-call | tf_op jit(solution)/shard_map/cycle_products/pallas_call | solution.py:499
  21.4 0.0 all-to-all-done.refs_0_
  21.4 1.2 apply_products_1.1
  22.6 16.2 %all_to_all.40.coeff_ref = bf16[32,32,128]{2,1,0:T(8,128)(2,1)S(1)} all-to-all(bf16[32,32,128]{2,1,0:T(8,128)(2,1)S(1)} %get-tuple-element.24), channel_id=1, replica_groups=mesh['blk'=32,'sim'=4] {'blk'}, dimensions={0} | all-to-all | bytes 524288 | tf_op jit(solution)/shard_map/all_to_all | solution.py:577
  38.8 0.0 copy-done
  38.8 0.0 copy-done.1
  38.8 0.0 copy-done.2
  38.8 0.0 copy-done.3
  38.8 0.0 copy-done.4
  38.8 2.1 %rows.3 = bf16[32,32,128]{2,1,0:T(8,128)(2,1)S(1)} custom-call(f32[16,64,128]{2,1,0:T(8,128)S(1)} %bitcast.19, f32[64,128]{1,0:T(8,128)S(1)} %bitcast.23, bf16[128,64]{1,0:T(8,128)(2,1)S(1)} %copy-done.3, bf16[64,128]{1,0:T(8,128)(2,1)S(1)} %copy-done.4, f32[2,64,128]{2,1,0:T(8,128)S(1)} %copy-done.1, bf16[2,128,256]{2,1,0:T(8,128)(2,1)S(1)} %get-tuple-element.19.inner_ref, ...), custom_call_target="tpu_custom_call" | custom-call | tf_op jit(solution)/shard_map/rows/pallas_call | solution.py:489
  40.9 12.5 %all_to_all.41.refs_0_ = bf16[32,32,128]{2,1,0:T(8,128)(2,1)S(1)} all-to-all(bf16[32,32,128]{2,1,0:T(8,128)(2,1)S(1)} %rows.3), channel_id=1, replica_groups=mesh['blk'=32,'sim'=4] {'blk'}, dimensions={0} | all-to-all | bytes 524288 | tf_op jit(solution)/shard_map/all_to_all | solution.py:577
  53.4 1.3 apply_products_2.1
  54.7 0.0 copy-start.5
  54.7 0.0 copy-start.6
  54.7 0.0 copy-start.7
  54.7 0.0 copy-start.8
  54.7 12.6 %all_to_all.42.coeff_ref = bf16[32,32,128]{2,1,0:T(8,128)(2,1)S(1)} all-to-all(bf16[32,32,128]{2,1,0:T(8,128)(2,1)S(1)} %get-tuple-element.26), channel_id=1, replica_groups=mesh['blk'=32,'sim'=4] {'blk'}, dimensions={0} | all-to-all | bytes 524288 | tf_op jit(solution)/shard_map/all_to_all | solution.py:577
  67.3 2.2 %rows.4 = bf16[32,32,128]{2,1,0:T(8,128)(2,1)S(1)} custom-call(f32[16,64,128]{2,1,0:T(8,128)S(1)} %bitcast.20, f32[64,128]{1,0:T(8,128)S(1)} %bitcast.24, bf16[128,64]{1,0:T(8,128)(2,1)S(1)} %copy-done.3, bf16[64,128]{1,0:T(8,128)(2,1)S(1)} %copy-done.4, f32[2,64,128]{2,1,0:T(8,128)S(1)} %copy-done.1, bf16[2,128,256]{2,1,0:T(8,128)(2,1)S(1)} %get-tuple-element.19.inner_ref, ...), custom_call_target="tpu_custom_call" | custom-call | tf_op jit(solution)/shard_map/rows/pallas_call | solution.py:489
  69.5 12.5 %all_to_all.43.refs_0_ = bf16[32,32,128]{2,1,0:T(8,128)(2,1)S(1)} all-to-all(bf16[32,32,128]{2,1,0:T(8,128)(2,1)S(1)} %rows.4), channel_id=1, replica_groups=mesh['blk'=32,'sim'=4] {'blk'}, dimensions={0} | all-to-all | bytes 524288 | tf_op jit(solution)/shard_map/all_to_all | solution.py:577
  81.9 1.3 apply_products_3.1
  83.3 12.5 %all_to_all.44.coeff_ref = bf16[32,32,128]{2,1,0:T(8,128)(2,1)S(1)} all-to-all(bf16[32,32,128]{2,1,0:T(8,128)(2,1)S(1)} %get-tuple-element.28), channel_id=1, replica_groups=mesh['blk'=32,'sim'=4] {'blk'}, dimensions={0} | all-to-all | bytes 524288 | tf_op jit(solution)/shard_map/all_to_all | solution.py:577
  95.7 2.1 %rows.5 = bf16[32,32,128]{2,1,0:T(8,128)(2,1)S(1)} custom-call(f32[16,64,128]{2,1,0:T(8,128)S(1)} %bitcast.21, f32[64,128]{1,0:T(8,128)S(1)} %bitcast.25, bf16[128,64]{1,0:T(8,128)(2,1)S(1)} %copy-done.3, bf16[64,128]{1,0:T(8,128)(2,1)S(1)} %copy-done.4, f32[2,64,128]{2,1,0:T(8,128)S(1)} %copy-done.1, bf16[2,128,256]{2,1,0:T(8,128)(2,1)S(1)} %get-tuple-element.19.inner_ref, ...), custom_call_target="tpu_custom_call" | custom-call | tf_op jit(solution)/shard_map/rows/pallas_call | solution.py:489
  97.9 12.5 %all_to_all.45.coeff_ref = bf16[32,32,128]{2,1,0:T(8,128)(2,1)S(1)} all-to-all(bf16[32,32,128]{2,1,0:T(8,128)(2,1)S(1)} %rows.5), channel_id=1, replica_groups=mesh['blk'=32,'sim'=4] {'blk'}, dimensions={0} | all-to-all | bytes 524288 | tf_op jit(solution)/shard_map/all_to_all | solution.py:577
  110.3 0.0 copy-done.5
  110.3 0.0 copy-done.6
  110.3 0.0 copy-done.7
  110.3 0.0 copy-done.8
  110.4 8.4 %last_modes.1 = (bf16[34,512,128]{2,1,0:T(8,128)(2,1)}, f32[128,2,128]{2,1,0:T(2,128)S(1)}) custom-call(s32[4,32]{1,0:T(4,128)S(1)} %bitcast.31, s32[2,34]{1,0:T(2,128)S(1)} %bitcast.34, s32[1]{0:T(128)} %bitcast.2.own_ref, bf16[32,32,128]{2,1,0:T(8,128)(2,1)S(1)} %all_to_all.45.coeff_ref, bf16[16,64,128]{2,1,0:T(8,128)(2,1)S(1)} %get-tuple-element.25.refs_2_.kept0_ref, ...), custom_call_target="tpu_custom_call" | custom-call | tf_op jit(solution)/shard_map/last_modes/pallas_call | solution.py:535
  118.8 15.9 %all_to_all.46 = f32[128,2,128]{2,1,0:T(2,128)S(1)} all-to-all(f32[128,2,128]{2,1,0:T(2,128)S(1)} %get-tuple-element.32), channel_id=1, replica_groups=mesh['blk'=32,'sim'=4] {'blk','sim'}, dimensions={0} | all-to-all | bytes 262144 | tf_op jit(solution)/shard_map/all_to_all | solution.py:605
  134.7 1.1 fisher.1
Async XLA Ops:
  3.6 17.8 %all-to-all-start = ((bf16[32,32,128]{2,1,0:T(8,128)(2,1)}), bf16[32,32,128]{2,1,0:T(8,128)(2,1)S(1)}, u32[]{:S(2)}, u32[]{:S(2)}) async-start(bf16[32,32,128]{2,1,0:T(8,128)(2,1)} %get-tuple-element.22), calls=%async_computation | async-start | bytes 524288 | tf_op jit(solution)/shard_map/all_to_all | solution.py:577
  11.9 26.9 %copy-start = (f32[2,8,2,4096]{3,2,1,0:T(2,128)S(1)}, f32[2,8,2,4096]{3,2,1,0:T(2,128)}, u32[]{:S(2)}) copy-start(f32[2,8,2,4096]{3,2,1,0:T(2,128)} %param.11) | copy-start | bytes 1572868
  11.9 26.9 %copy-start.1 = (f32[2,64,128]{2,1,0:T(8,128)S(1)}, f32[2,64,128]{2,1,0:T(8,128)}, u32[]{:S(2)}) copy-start(f32[2,64,128]{2,1,0:T(8,128)} %constant.19.clone.twist_ref) | copy-start | bytes 196612
  11.9 26.9 %copy-start.2 = (f32[2,4096]{1,0:T(2,128)S(1)}, f32[2,4096]{1,0:T(2,128)}, u32[]{:S(2)}) copy-start(f32[2,4096]{1,0:T(2,128)} %param.12) | copy-start | bytes 98308
  11.9 26.9 %copy-start.3 = (bf16[128,64]{1,0:T(8,128)(2,1)S(1)}, bf16[128,64]{1,0:T(8,128)(2,1)}, u32[]{:S(2)}) copy-start(bf16[128,64]{1,0:T(8,128)(2,1)} %constant.17.clone.outer_ref) | copy-start | bytes 49156
  11.9 26.9 %copy-start.4 = (bf16[64,128]{1,0:T(8,128)(2,1)S(1)}, bf16[64,128]{1,0:T(8,128)(2,1)}, u32[]{:S(2)}) copy-start(bf16[64,128]{1,0:T(8,128)(2,1)} %constant.18.clone.outer_t_ref) | copy-start | bytes 49156
  54.7 55.7 %copy-start.5 = (f32[2048]{0:T(1024)S(1)}, f32[2048]{0:T(1024)}, u32[]{:S(2)}) copy-start(f32[2048]{0:T(1024)} %param.13) | copy-start | bytes 24580
  54.7 55.7 %copy-start.6 = (s32[32,4]{0,1:T(4,128)S(1)}, s32[32,4]{0,1:T(4,128)}, u32[]{:S(2)}) copy-start(s32[32,4]{0,1:T(4,128)} %param.15) | copy-start | bytes 1540
  54.7 55.7 %copy-start.7 = (s32[2048]{0:T(1024)S(1)}, s32[2048]{0:T(1024)}, u32[]{:S(2)}) copy-start(s32[2048]{0:T(1024)} %param.17) | copy-start | bytes 24580
  54.7 55.7 %copy-start.8 = (s32[34,2]{0,1:T(2,128)S(1)}, s32[34,2]{0,1:T(2,128)}, u32[]{:S(2)}) copy-start(s32[34,2]{0,1:T(2,128)} %param.16) | copy-start | bytes 820
